TPU v7x, 256 devices: a whole 4x4x8 slice. The times are simulated.
256 devices in a mesh: row: 32 (over z_hi, x, core), col: 8 (over z_lo, y).
Axes of the slice: x: 4, y: 4, z: 8 (z_hi: 4, z_lo: 2; z = z_hi * 2 + z_lo), core: 2. Of those that a mesh axis runs over, the one named last changes fastest.
Arguments:
- density_factor: bfloat16 [6144, 512], P('row', 'col'), may hold values from -0.25 to 0.25
- hole_factor: bfloat16 [6144, 512], P('row', 'col'), may hold values from -0.25 to 0.25
- ph_factor: bfloat16 [6144, 512], P('row', 'col'), may hold values from -0.25 to 0.25
- hamiltonian: bfloat16 [6144, 6144], P('row', 'col'), as said below
- multiplier_q: bfloat16 [6144, 6144], P('row', 'col'), as said below
- multiplier_g: bfloat16 [6144, 6144], P('row', 'col'), as said below
- ph_perm: int32 [6144], replicated, may hold values from 0 to 6143, as said below
- block_lengths: int32 [48], replicated, may hold values from 1 to 256, 6144 in all
Outputs:
- grad_density: float32 [6144, 512], P('row', 'col')
- grad_hole: float32 [6144, 512], P('row', 'col')
- grad_ph: float32 [6144, 512], P('row', 'col')
Inputs may be any that keep to these rules, and one draw needn't show every extreme that they name: `ph_perm`: a permutation of the rows; each aligned block of 192 entries holds exactly 6 values from each aligned range of 192 rows. `block_lengths`: the lengths sum to 6144. `hamiltonian`: symmetric. `multiplier_q`: symmetric. `multiplier_g`: symmetric.
All inputs are finite; a program needn't handle non-finite values.
Results may differ from a plain program's by a relative error of at most 0.00035.
The roundings to bfloat16 on the way count: a program that leaves them out, or rounds other values in their place, can miss the bound.
Values may be sent and summed in bfloat16 or wider, within the bound.
No kernel may reach another device: no remote copies, remote signals or barrier semaphores. Data moves between devices by JAX's collectives and lax.ppermute only.
A program may use at most 64 MiB of HBM per device.

v0:
```python
import jax
import jax.numpy as jnp
from jax import lax
from jax.sharding import PartitionSpec as P

shift_value = 2.0
penalty = 2.5


def block_means(values, lengths):
    offsets = jnp.cumsum(lengths)
    positions = jnp.arange(values.shape[0], dtype=jnp.int32)
    segment = jnp.sum((positions[:, None] >= offsets[None, :]).astype(jnp.int32), axis=1)
    member = (segment[:, None] == jnp.arange(lengths.shape[0], dtype=jnp.int32)[None, :]).astype(
        jnp.float32
    )
    means = jnp.sum(member * values[:, None], axis=0) / lengths.astype(jnp.float32)
    return jnp.sum(member * means[None, :], axis=1)


def contract_rows(left, right):
    return lax.dot_general(
        left, right, (((1,), (1,)), ((), ())), preferred_element_type=jnp.float32
    )


def local(
    density_factor,
    hole_factor,
    ph_factor,
    hamiltonian,
    multiplier_q,
    multiplier_g,
    ph_perm,
    block_lengths,
):
    groups = lax.axis_size("row")
    row_index = lax.axis_index("row")
    col_index = lax.axis_index("col")
    block = density_factor.shape[0]
    rank_part = density_factor.shape[1]
    width = multiplier_q.shape[1]
    sends = block // groups
    row_ids = row_index * block + jnp.arange(block, dtype=jnp.int32)
    col_ids = col_index * width + jnp.arange(width, dtype=jnp.int32)
    on_diag = row_ids[:, None] == col_ids[None, :]
    density_sq = jnp.sum(jnp.square(density_factor.astype(jnp.float32)), axis=1)
    ph_sq = jnp.sum(jnp.square(ph_factor.astype(jnp.float32)), axis=1)
    mult_diag = jnp.sum(jnp.where(on_diag, multiplier_g.astype(jnp.float32), 0.0), axis=1)
    density_sq, ph_sq, mult_diag = lax.psum((density_sq, ph_sq, mult_diag), "col")
    density_all, ph_all, mult_all = (
        lax.all_gather(density_sq, "row", axis=0, tiled=True),
        lax.all_gather(ph_sq, "row", axis=0, tiled=True),
        lax.all_gather(mult_diag, "row", axis=0, tiled=True),
    )
    shifted = 2.0 * block_means(density_all, block_lengths)
    shifted_ph = jnp.take(shifted, ph_perm)
    weight_diag = mult_all + penalty * (shifted_ph - jnp.take(density_all, ph_perm) - ph_all)
    weight_pair = jnp.zeros_like(weight_diag).at[ph_perm].set(weight_diag)
    scaling = 2.0 * block_means(weight_pair, block_lengths)
    scale_rows = lax.dynamic_slice_in_dim(scaling, row_index * block, block)
    shift_rows = lax.dynamic_slice_in_dim(shifted_ph, row_index * block, block)
    table = ph_perm.reshape(groups, block)
    source = table // block
    mine = lax.dynamic_index_in_dim(source, row_index, 0, keepdims=False)
    member = (mine[:, None] == jnp.arange(groups, dtype=jnp.int32)[None, :]).astype(jnp.int32)
    earlier = jnp.cumsum(member, axis=0) - member
    slot = mine * sends + jnp.sum(earlier * member, axis=1)
    slot_back = jnp.argsort(slot)
    position = jnp.arange(block, dtype=jnp.int32)[None, :]
    ranked = jnp.where(source == row_index, position, block + position)
    chosen = jnp.argsort(ranked, axis=1)[:, :sends]
    anchor = (jnp.take_along_axis(table, chosen, axis=1) - row_index * block).reshape(block)
    anchor_back = jnp.argsort(anchor)
    pair_local = jnp.concatenate([density_factor, hole_factor], axis=1)
    outgoing = jnp.take(density_factor, anchor, axis=0)
    incoming = lax.all_to_all(outgoing, "row", split_axis=0, concat_axis=0, tiled=True)
    density_ph = jnp.take(incoming, slot, axis=0)
    ph_local = jnp.concatenate([density_ph, ph_factor], axis=1)
    pair_whole, ph_whole = (
        lax.all_gather(pair_local, "row", axis=0, tiled=True),
        lax.all_gather(ph_local, "row", axis=0, tiled=True),
    )
    pair_rows = pair_whole
    ph_rows = ph_whole
    gram_cols = lax.psum_scatter(
        jnp.concatenate(
            [contract_rows(pair_rows, pair_local), contract_rows(ph_rows, ph_local)], axis=1
        ),
        "col",
        scatter_dimension=0,
        tiled=True,
    )
    resid_q = jnp.where(on_diag, shift_value, 0.0) - gram_cols[:, :block].T
    resid_g = jnp.where(on_diag, shift_rows[:, None], 0.0) - gram_cols[:, block:].T
    weight_q = (multiplier_q.astype(jnp.float32) + penalty * resid_q).astype(jnp.bfloat16)
    weight_g = (multiplier_g.astype(jnp.float32) + penalty * resid_g).astype(jnp.bfloat16)
    weight_q, weight_g = (weight_q, weight_g)
    pair_rows = pair_whole
    ph_rows = ph_whole
    energy = jnp.dot(
        lax.all_gather(hamiltonian, "col", axis=1, tiled=True),
        pair_rows[:, :rank_part],
        preferred_element_type=jnp.float32,
    )
    pair_acc = jnp.dot(
        lax.all_gather(weight_q, "col", axis=1, tiled=True),
        pair_rows,
        preferred_element_type=jnp.float32,
    )
    ph_acc = jnp.dot(
        lax.all_gather(weight_g, "col", axis=1, tiled=True),
        ph_rows,
        preferred_element_type=jnp.float32,
    )
    pair_grad = jnp.concatenate(
        [2.0 * energy - 2.0 * pair_acc[:, :rank_part], -2.0 * pair_acc[:, rank_part:]], axis=1
    )
    outgoing_back = jnp.take(ph_acc[:, :rank_part], slot_back, axis=0)
    returned = lax.all_to_all(outgoing_back, "row", split_axis=0, concat_axis=0, tiled=True)
    returned = jnp.take(returned, anchor_back, axis=0)
    grad_density = (
        pair_grad[:, :rank_part]
        + 2.0 * scale_rows[:, None] * density_factor.astype(jnp.float32)
        - 2.0 * returned
    )
    grad_hole = pair_grad[:, rank_part:]
    grad_ph = -2.0 * ph_acc[:, rank_part:]
    return (grad_density, grad_hole, grad_ph)


def solution(mesh):
    return jax.shard_map(
        local,
        mesh=mesh,
        in_specs=(
            P("row", "col"),
            P("row", "col"),
            P("row", "col"),
            P("row", "col"),
            P("row", "col"),
            P("row", "col"),
            P(),
            P(),
        ),
        out_specs=(P("row", "col"), P("row", "col"), P("row", "col")),
        check_vma=False,
    )
```

profile of v0, /device:TPU:64, one launch (start us, length us, event | category | flops | bytes accessed | tf_op | source)
XLA Modules:
  0.0 626.5 jit_solution(385054818816971866)
XLA Ops:
  10.6 3.7 sort.48
  18.3 10.7 %all-to-all-start = ((bf16[32,2,192]{2,1,0:T(2,128)(2,1)}), bf16[32,2,192]{2,1,0:T(2,128)(2,1)S(1)}, u32[]{:S(2)}, u32[]{:S(2)}) async-start(bf16[32,2,192]{2,1,0:T(2,128)(2,1)} %reshape.214), calls=%async_computation | async-start | bytes 65536 | tf_op jit(solution)/shard_map/all_to_all | solution.py:77
  30.2 6.8 %all-to-all-done = bf16[32,2,192]{2,1,0:T(2,128)(2,1)S(1)} async-done(((bf16[32,2,192]{2,1,0:T(2,128)(2,1)}), bf16[32,2,192]{2,1,0:T(2,128)(2,1)S(1)}, u32[]{:S(2)}, u32[]{:S(2)}) %all-to-all-start) | async-done | bytes 24608 | tf_op jit(solution)/shard_map/all_to_all | solution.py:77
  40.4 19.3 %all-reduce.5 = (f32[192]{0:T(256)S(1)}, f32[192]{0:T(256)S(1)}, f32[192]{0:T(256)S(1)}) all-reduce(f32[192]{0:T(256)S(1)} %fusion.25, f32[192]{0:T(256)S(1)} %fusion.22, f32[192]{0:T(256)S(1)} %multiply_reduce_fusion), channel_id=1, replica_groups=mesh['row'=32,'col'=8] {'col'}, use_global_device_ids=true, to_apply=%region_10.12 | all-reduce | flops 576 | bytes 4608 | tf_op jit(solution)/shard_map/psum | solution.py:50
  61.2 3.9 all-gather.6.cloned.1.call-done
  65.1 4.3 fusion.35
  69.4 49.3 %all-gather.10.cloned.1.call-done = bf16[6144,128]{1,0:T(8,128)(2,1)} async-done(((bf16[192,128]{1,0:T(8,128)(2,1)}), bf16[6144,128]{1,0:T(8,128)(2,1)}) %all-gather.10.cloned.1.call-update) | async-done | bytes 1572880 | tf_op jit(solution)/shard_map/all_gather | solution.py:82
  118.8 2.3 fusion.36
  121.6 4.7 pad_maximum_fusion
  127.5 238.9 %all-reduce.8.cloned.1.call-done = (f32[6144]{0:T(1024)}, f32[6144]{0:T(1024)}, f32[6144]{0:T(1024)}) async-done(((f32[6144]{0:T(1024)}, f32[6144]{0:T(1024)}, f32[6144]{0:T(1024)}), (f32[6144]{0:T(1024)}, f32[6144]{0:T(1024)}, f32[6144]{0:T(1024)})) %all-reduce.8.cloned.1.call-update) | async-done | bytes 73744
  366.3 28.4 %gather_fusion.4 = f32[6144]{0:T(1024)S(1)} fusion(f32[6144]{0:T(1024)} %get-tuple-element.24, s32[6144]{0:T(1024)S(1)} %get-tuple-element.43), kind=kCustom, calls=%fused_computation.4.clone | custom fusion | bytes 73728 | tf_op jit(solution)/shard_map/jit(_take)/gather | solution.py:58
  395.3 34.3 %gather_fusion.3 = f32[6144]{0:T(1024)S(1)} fusion(f32[6144]{0:T(1024)S(1)} %broadcast_multiply_fusion, s32[6144]{0:T(1024)S(1)} %get-tuple-element.43), kind=kCustom, calls=%fused_computation.1.clone | custom fusion | bytes 73728 | tf_op jit(solution)/shard_map/jit(_take)/gather | solution.py:57
  429.8 49.3 %reduce-scatter.2.cloned.1.call-done = f32[768,384]{0,1:T(8,128)} async-done(((f32[6144,384]{0,1:T(8,128)}), f32[768,384]{0,1:T(8,128)}) %reduce-scatter.2.cloned.1.call-update) | async-done | bytes 1179664 | tf_op jit(solution)/shard_map/reduce_scatter | solution.py:86
  479.1 2.4 fusion.21
  482.8 3.2 sort.49
  486.0 3.2 sort.50
  489.2 23.2 %scatter_custom_fusion = f32[6144]{0:T(1024)S(1)} fusion(s32[6144]{0:T(1024)S(1)} %get-tuple-element.42, f32[6144]{0:T(1024)S(1)} %get-tuple-element.30, f32[]{:T(128)} %constant.68.clone.1), kind=kCustom, calls=%fused_computation.76 | custom fusion | bytes 24580 | tf_op jit(solution)/shard_map/scatter | solution.py:59
  513.0 11.6 %all-gather.14.cloned.1.call-done = bf16[192,6144]{1,0:T(8,128)(2,1)} async-done(((bf16[192,768]{1,0:T(8,128)(2,1)}), bf16[192,6144]{1,0:T(8,128)(2,1)}) %all-gather.14.cloned.1.call-update) | async-done | bytes 2359312 | tf_op jit(solution)/shard_map/all_gather | solution.py:112
  524.7 2.4 fusion.38
  528.8 9.1 %all-to-all-start.1 = ((f32[32,1,384]{2,1,0:T(1,128)}), f32[32,1,384]{2,1,0:T(1,128)S(1)}, u32[]{:S(2)}, u32[]{:S(2)}) async-start(f32[32,1,384]{2,1,0:T(1,128)} %reshape.216), calls=%async_computation.2 | async-start | bytes 98304 | tf_op jit(solution)/shard_map/all_to_all | solution.py:120
  537.9 32.9 %all-gather.12.cloned.1.call-done = bf16[192,6144]{1,0:T(8,128)(2,1)} async-done(((bf16[192,768]{1,0:T(8,128)(2,1)}), bf16[192,6144]{1,0:T(8,128)(2,1)}) %all-gather.12.cloned.1.call-update) | async-done | bytes 2359312 | tf_op jit(solution)/shard_map/all_gather | solution.py:107
  570.8 2.4 fusion.37
  577.0 39.5 %all-gather.8.cloned.1.call-done = bf16[192,6144]{1,0:T(8,128)(2,1)} async-done(((bf16[192,768]{1,0:T(8,128)(2,1)}), bf16[192,6144]{1,0:T(8,128)(2,1)}) %all-gather.8.cloned.1.call-update) | async-done | bytes 2359312 | tf_op jit(solution)/shard_map/all_gather | solution.py:102
  616.5 3.1 fusion.14
  (144 shorter events, 22.2 us)
Async XLA Ops:
  7.2 57.9 %all-gather.6.cloned.1.call-start = ((), (), s32[]{:S(2)}) async-start(), calls=%async_computation.3 | async-start | bytes 1622016 | tf_op jit(solution)/shard_map/all_gather | solution.py:81
  14.4 15.7 %copy-start.10 = (bf16[192,64]{0,1:T(8,128)(2,1)S(1)}, bf16[192,64]{0,1:T(8,128)(2,1)}, u32[]{:S(2)}) copy-start(bf16[192,64]{0,1:T(8,128)(2,1)} %param.16) | copy-start | bytes 73732
  16.3 22.5 %copy-start.19 = (u32[256]{0:T(256)S(1)}, u32[256]{0:T(256)}, u32[]{:S(2)}) copy-start(u32[256]{0:T(256)} %constant.123) | copy-start | bytes 3076
  16.3 23.7 %copy-start.7 = (bf16[192,64]{0,1:T(8,128)(2,1)S(1)}, bf16[192,64]{0,1:T(8,128)(2,1)}, u32[]{:S(2)}) copy-start(bf16[192,64]{0,1:T(8,128)(2,1)} %param.14) | copy-start | bytes 73732
  16.3 23.8 %copy-start.4 = (bf16[192,768]{1,0:T(8,128)(2,1)S(1)}, bf16[192,768]{1,0:T(8,128)(2,1)}, u32[]{:S(2)}) copy-start(bf16[192,768]{1,0:T(8,128)(2,1)} %param.19) | copy-start | bytes 884740
  16.4 48.8 %copy-start.5 = (bf16[192,128]{1,0:T(8,128)(2,1)S(1)}, bf16[192,128]{1,0:T(8,128)(2,1)}, u32[]{:S(2)}) copy-start(bf16[192,128]{1,0:T(8,128)(2,1)} %pad_maximum_fusion.1) | copy-start | bytes 147460
  18.3 18.7 %all-to-all-start = ((bf16[32,2,192]{2,1,0:T(2,128)(2,1)}), bf16[32,2,192]{2,1,0:T(2,128)(2,1)S(1)}, u32[]{:S(2)}, u32[]{:S(2)}) async-start(bf16[32,2,192]{2,1,0:T(2,128)(2,1)} %reshape.214), calls=%async_computation | async-start | bytes 65536 | tf_op jit(solution)/shard_map/all_to_all | solution.py:77
  29.0 89.7 %all-gather.10.cloned.1.call-start = ((), (), s32[]{:S(2)}) async-start(), calls=%async_computation.5 | async-start | bytes 1622016 | tf_op jit(solution)/shard_map/all_gather | solution.py:82
  38.7 327.6 %all-reduce.8.cloned.1.call-start = ((), (), s32[]{:S(2)}) async-start(), calls=%async_computation.9 | async-start | bytes 147456
  40.0 20.4 %copy-start.16 = (s32[192]{0:T(256)}, s32[192]{0:T(256)S(1)}, u32[]{:S(2)}) copy-start(s32[192]{0:T(256)S(1)} %iota_add_fusion.2) | copy-start | bytes 2308
  61.1 57.7 %copy-start.6 = (bf16[192,128]{1,0:T(8,128)(2,1)S(1)}, bf16[192,128]{1,0:T(8,128)(2,1)}, u32[]{:S(2)}) copy-start(bf16[192,128]{1,0:T(8,128)(2,1)} %pad_maximum_fusion.2) | copy-start | bytes 147460
  61.1 418.0 %reduce-scatter.2.cloned.1.call-start = ((), (), s32[]{:S(2)}) async-start(), calls=%async_computation.6 | async-start | bytes 10616832 | tf_op jit(solution)/shard_map/reduce_scatter | solution.py:86
  118.8 2.8 copy-start.1
  126.3 398.4 %all-gather.14.cloned.1.call-start = ((), (), s32[]{:S(2)}) async-start(), calls=%async_computation.8 | async-start | bytes 2654208 | tf_op jit(solution)/shard_map/all_gather | solution.py:112
  366.3 28.4 %copy-start = (f32[6144]{0:T(1024)S(1)}, f32[6144]{0:T(1024)}, u32[]{:S(2)}) copy-start(f32[6144]{0:T(1024)} %get-tuple-element.24) | copy-start | bytes 73732
  395.3 34.3 %copy-start.14 = (f32[6144]{0:T(1024)S(1)}, f32[6144]{0:T(1024)}, u32[]{:S(2)}) copy-start(f32[6144]{0:T(1024)} %get-tuple-element.25) | copy-start | bytes 73732
  395.3 34.3 %copy-start.15 = (f32[6144]{0:T(1024)S(1)}, f32[6144]{0:T(1024)}, u32[]{:S(2)}) copy-start(f32[6144]{0:T(1024)} %get-tuple-element.26) | copy-start | bytes 73732
  395.3 83.8 %copy-start.8 = (bf16[192,768]{1,0:T(8,128)(2,1)S(1)}, bf16[192,768]{1,0:T(8,128)(2,1)}, u32[]{:S(2)}) copy-start(bf16[192,768]{1,0:T(8,128)(2,1)} %param.18) | copy-start | bytes 884740
  395.3 83.7 %copy-start.17 = (s32[192]{0:T(256)S(1)}, s32[192]{0:T(256)}, u32[]{:S(2)}) copy-start(s32[192]{0:T(256)} %copy-done.16) | copy-start | bytes 2308
  429.8 94.9 %copy-start.3 = (bf16[6144,128]{1,0:T(8,128)(2,1)S(1)}, bf16[6144,128]{1,0:T(8,128)(2,1)}, u32[]{:S(2)}) copy-start(bf16[6144,128]{1,0:T(8,128)(2,1)} %all-gather.10.cloned.1.call-done) | copy-start | bytes 4718596
  481.5 89.3 %all-gather.12.cloned.1.call-start = ((), (), s32[]{:S(2)}) async-start(), calls=%async_computation.7 | async-start | bytes 2654208 | tf_op jit(solution)/shard_map/all_gather | solution.py:107
  482.0 134.5 %all-gather.8.cloned.1.call-start = ((), (), s32[]{:S(2)}) async-start(), calls=%async_computation.4 | async-start | bytes 2654208 | tf_op jit(solution)/shard_map/all_gather | solution.py:102
  527.1 43.7 %copy-start.2 = (bf16[6144,128]{1,0:T(8,128)(2,1)S(1)}, bf16[6144,128]{1,0:T(8,128)(2,1)}, u32[]{:S(2)}) copy-start(bf16[6144,128]{1,0:T(8,128)(2,1)} %all-gather.6.cloned.1.call-done) | copy-start | bytes 4718596
  528.8 46.1 %all-to-all-start.1 = ((f32[32,1,384]{2,1,0:T(1,128)}), f32[32,1,384]{2,1,0:T(1,128)S(1)}, u32[]{:S(2)}, u32[]{:S(2)}) async-start(f32[32,1,384]{2,1,0:T(1,128)} %reshape.216), calls=%async_computation.2 | async-start | bytes 98304 | tf_op jit(solution)/shard_map/all_to_all | solution.py:120
  (5 other events, 3.6 us)
Sparse Core Ops, SparseCore 0:
  11.1 53.9 all-gather.5
  68.2 50.4 all-gather.9
  122.2 244.1 all-reduce.7
  368.9 110.1 reduce-scatter.1
  481.6 43.0 all-gather.13
  526.4 44.2 all-gather.11
  572.7 43.7 all-gather.7
where the time goes:
time: 628 us; the launch traced here: 626 us
  waiting for transfers between devices  434 us (69%)
  local copies, waits for them, and re-layouts  101 us (16%)
  other arithmetic  22.5 us (4%)
  starting transfers between devices  20.1 us (3%)
  blocking collectives  19.3 us (3%)
  between operations  15.3 us (2%)
  matrix products  14.6 us (2%)
    unnamed x8, waiting for transfers between devices  240 us
    all_gather x1, waiting for transfers between devices, local(): lax.all_gather(ph_local, 'row', axis=0, tiled=True)  49.3 us
    reduce_scatter x1, waiting for transfers between devices, local(): lax.psum_scatter(jnp.concatenate([contract_rows(pair_rows, pair_local), c...  49.3 us
    all_gather x1, waiting for transfers between devices, local(): lax.all_gather(hamiltonian, 'col', axis=1, tiled=True)  39.5 us
    gather x1, local copies, waits for them, and re-layouts, local(): shifted_ph = jnp.take(shifted, ph_perm)  34.3 us
    all_gather x1, waiting for transfers between devices, local(): lax.all_gather(weight_q, 'col', axis=1, tiled=True)  32.9 us
    gather x1, local copies, waits for them, and re-layouts, local(): jnp.take(density_all, ph_perm)  28.4 us
    scatter x1, local copies, waits for them, and re-layouts, local(): weight_pair = jnp.zeros_like(weight_diag).at[ph_perm].set(weight_diag)  23.2 us
  transfers between devices with their start and end apart: 9, of which 8 were waited for; matrix products, arithmetic and copies ran while one was open for 20% of the time, Pallas kernels for 0%

commit v1 on v0

v1 whole, which is shorter than its diff:
```python
import jax
import jax.numpy as jnp
from jax import lax
from jax.sharding import PartitionSpec as P

shift_value = 2.0
penalty = 2.5
both = ("row", "col")
f32 = jnp.float32
bf16 = jnp.bfloat16


def contract_rows(left, right):
    return lax.dot_general(left, right, (((1,), (1,)), ((), ())), preferred_element_type=f32)


def pick(one_hot, values):
    return jnp.dot(
        one_hot.astype(values.dtype),
        values,
        precision=lax.Precision.HIGHEST if values.dtype == f32 else None,
        preferred_element_type=f32,
    ).astype(values.dtype)


def digit(axis):
    name, stride, length = axis
    return lax.axis_index(name) // stride % length


def turn(x, axis, step):
    name, stride, length = axis
    pairs = []
    for i in range(lax.axis_size(name)):
        d = i // stride % length
        pairs.append((i, i + ((d + step) % length - d) * stride))
    return lax.ppermute(x, name, pairs)


def steps_of(axis):
    return {2: (1,), 4: (1, -1, 2)}[axis[2]]


def gather_digit(x, axis):
    here = digit(axis)
    moved = [(0, x)] + [(-s, turn(x, axis, s)) for s in steps_of(axis)]
    out = jnp.zeros((axis[2],) + x.shape, x.dtype)
    for offset, value in moved:
        out = lax.dynamic_update_slice_in_dim(out, value[None], (here + offset) % axis[2], 0)
    return out


def sum_digit(x, axis):
    total = x
    for s in steps_of(axis):
        total = total + turn(x, axis, s)
    return total


z_hi, x_axis, core = ("row", 8, 4), ("row", 2, 4), ("row", 1, 2)
z_lo, y_axis = ("col", 4, 2), ("col", 1, 4)


def gather_rows(x):
    out = gather_digit(x, z_hi)
    out = gather_digit(out, x_axis)
    out = gather_digit(out, core)
    return jnp.transpose(out, (2, 1, 0) + tuple(range(3, out.ndim))).reshape((-1,) + x.shape)


def gather_cols(x):
    out = gather_digit(gather_digit(x, z_lo), y_axis)
    return jnp.swapaxes(out, 0, 1).reshape((-1,) + x.shape)


def sum_all(x):
    for axis in (core, z_lo, x_axis, y_axis, z_hi):
        x = sum_digit(x, axis)
    return x


def local(
    density_factor,
    hole_factor,
    ph_factor,
    hamiltonian,
    multiplier_q,
    multiplier_g,
    ph_perm,
    block_lengths,
):
    rows, cols = lax.axis_size("row"), lax.axis_size("col")
    row_index = lax.axis_index("row")
    col_index = lax.axis_index("col")
    block, part = density_factor.shape
    width = multiplier_q.shape[1]
    per = width // block
    each = width // rows
    row_ids = row_index * block + jnp.arange(block, dtype=jnp.int32)
    col_ids = col_index * width + jnp.arange(width, dtype=jnp.int32)
    on_diag = row_ids[:, None] == col_ids[None, :]
    mine = lax.dynamic_slice_in_dim(ph_perm, row_index * block, block)
    wide = lax.dynamic_slice_in_dim(ph_perm, col_index * width, width)

    ends = jnp.sum(
        jnp.where(
            jnp.arange(block_lengths.shape[0])[:, None] >= jnp.arange(block_lengths.shape[0])[None, :],
            block_lengths[None, :],
            0,
        ),
        axis=1,
    )
    starts = ends - block_lengths
    in_segment = ((row_ids[:, None] >= starts) & (row_ids[:, None] < ends)).astype(f32)
    ph_segment = ((mine[:, None] >= starts) & (mine[:, None] < ends)).astype(f32)
    density_sq = jnp.sum(jnp.square(density_factor.astype(f32)), axis=1)
    ph_sq = jnp.sum(jnp.square(ph_factor.astype(f32)), axis=1)
    mult_diag = jnp.sum(jnp.where(on_diag, multiplier_g.astype(f32), 0.0), axis=1)
    stats = jnp.stack(
        [
            jnp.sum(in_segment * density_sq[:, None], axis=0),
            jnp.sum(ph_segment * (mult_diag - penalty * ph_sq)[:, None], axis=0),
        ]
    )
    stats = sum_all(stats) / block_lengths.astype(f32)
    shift_rows = jnp.sum(ph_segment * (2.0 * stats[0]), axis=1)
    scale_rows = jnp.sum(in_segment * (2.0 * (stats[1] + penalty * stats[0])), axis=1)

    places = jnp.arange(rows * block, dtype=jnp.int32)
    target = jnp.sum(jnp.where(ph_perm[None, :] == row_ids[:, None], places[None, :], 0), axis=1)
    order = jnp.sum((target[None, :] < target[:, None]).astype(jnp.int32), axis=1)
    send = jnp.arange(block, dtype=jnp.int32)[:, None] == order[None, :]

    def arrival(ids, share):
        source = ids // block
        n = ids.shape[0]
        place = jnp.arange(n, dtype=jnp.int32)
        earlier = (source[None, :] == source[:, None]) & (place[None, :] < place[:, None])
        slot = source * share + jnp.sum(earlier.astype(jnp.int32), axis=1)
        return slot[:, None] == place[None, :]

    receive = arrival(mine, block // rows)
    receive_wide = arrival(wide, each)
    leaving = pick(send, density_factor)

    pair_local = jnp.concatenate([density_factor, hole_factor], axis=1)
    moved = lax.ppermute(
        jnp.concatenate([pair_local, ph_factor], axis=1),
        both,
        [
            (r * cols + c, ((r % per) * cols + c) * cols + r // per)
            for r in range(rows)
            for c in range(cols)
        ],
    )
    by_col = lax.all_to_all(leaving.reshape(cols, each, part), "col", 0, 0)
    density_piece = jnp.swapaxes(by_col, 0, 1).reshape(each * cols * part // part, part)
    column = gather_rows(jnp.concatenate([moved, density_piece], axis=1))
    column = column.reshape(per, cols, block, 4 * part)
    pair_col = jnp.swapaxes(column[..., : 2 * part], 1, 2).reshape(width, cols * 2 * part)
    hole_col = jnp.swapaxes(column[..., 2 * part : 3 * part], 1, 2).reshape(width, cols * part)
    density_col = pick(receive_wide, column[..., 3 * part :].reshape(width, cols * part))

    incoming = lax.all_to_all(leaving, "row", 0, 0, tiled=True)
    density_ph = pick(receive, incoming)
    row_whole = gather_cols(jnp.concatenate([pair_local, ph_factor, density_ph], axis=1))
    row_whole = jnp.swapaxes(row_whole, 0, 1)
    pair_row = row_whole[..., : 2 * part].reshape(block, -1)
    hole_row = row_whole[..., 2 * part : 3 * part].reshape(block, -1)
    density_row = row_whole[..., 3 * part :].reshape(block, -1)

    gram_q = contract_rows(pair_row, pair_col)
    gram_g = contract_rows(density_row, density_col) + contract_rows(hole_row, hole_col)
    resid_q = jnp.where(on_diag, shift_value, 0.0) - gram_q
    resid_g = jnp.where(on_diag, shift_rows[:, None], 0.0) - gram_g
    weight_q = (multiplier_q.astype(f32) + penalty * resid_q).astype(bf16)
    weight_g = (multiplier_g.astype(f32) + penalty * resid_g).astype(bf16)

    energy = jnp.dot(hamiltonian, pair_col, preferred_element_type=f32).reshape(block, cols, -1)
    pair_term = jnp.dot(weight_q, pair_col, preferred_element_type=f32).reshape(block, cols, -1)
    first = jnp.arange(2 * part) < part
    pair_part = jnp.where(first, 2.0 * energy, 0.0) - 2.0 * pair_term
    density_term = jnp.dot(weight_g, density_col, preferred_element_type=f32).reshape(block, cols, -1)
    hole_term = jnp.dot(weight_g, hole_col, preferred_element_type=f32).reshape(block, cols, -1)
    parts = jnp.swapaxes(
        jnp.concatenate([pair_part, -2.0 * density_term, -2.0 * hole_term], axis=2), 0, 1
    )
    done = jnp.sum(lax.all_to_all(parts, "col", 0, 0), axis=0)

    back = pick(receive.T, done[:, 2 * part : 3 * part])
    returned = pick(send.T, lax.all_to_all(back, "row", 0, 0, tiled=True))
    grad_density = (
        done[:, :part] + 2.0 * scale_rows[:, None] * density_factor.astype(f32) + returned
    )
    return (grad_density, done[:, part : 2 * part], done[:, 3 * part :])


def solution(mesh):
    return jax.shard_map(
        local,
        mesh=mesh,
        in_specs=(
            P("row", "col"),
            P("row", "col"),
            P("row", "col"),
            P("row", "col"),
            P("row", "col"),
            P("row", "col"),
            P(),
            P(),
        ),
        out_specs=(P("row", "col"), P("row", "col"), P("row", "col")),
        check_vma=False,
    )
```

time: 628 us -> 224 us (0.36)
  the two profiles are of different devices: /device:TPU:64 before, /device:TPU:1 now
where the time goes in v1:
time: 224 us; the launch traced here: 223 us
  waiting for transfers between devices  73.1 us (33%)
  starting transfers between devices  71.2 us (32%)
  local copies, waits for them, and re-layouts  51.1 us (23%)
  other arithmetic  13.2 us (6%)
  matrix products  12.6 us (6%)
    ppermute x22, waiting for transfers between devices, turn(): return lax.ppermute(x, name, pairs)  37.3 us
    ppermute x22, starting transfers between devices, turn(): return lax.ppermute(x, name, pairs)  35.4 us
    all_to_all x1, waiting for transfers between devices, local(): done = jnp.sum(lax.all_to_all(parts, 'col', 0, 0), axis=0)  20.5 us
    all_to_all x1, starting transfers between devices, local(): incoming = lax.all_to_all(leaving, 'row', 0, 0, tiled=True)  10 us
    all_to_all x1, starting transfers between devices, local(): returned = pick(send.T, lax.all_to_all(back, 'row', 0, 0, tiled=True))  8.86 us
    unnamed x34, local copies, waits for them, and re-layouts  8.34 us
    all_to_all x1, waiting for transfers between devices, local(): returned = pick(send.T, lax.all_to_all(back, 'row', 0, 0, tiled=True))  8.12 us
    dynamic_update_slice x15, local copies, waits for them, and re-layouts, gather_digit(): lax.dynamic_update_slice_in_dim(out, value[None], (here + offset) % axis[...  7.32 us
  transfers between devices with their start and end apart: 27, of which 17 were waited for; matrix products, arithmetic and copies ran while one was open for 12% of the time, Pallas kernels for 0%

profile of v1, /device:TPU:1, one launch (start us, length us, event | category | flops | bytes accessed | tf_op | source)
XLA Modules:
  0.0 222.6 jit_solution(8650943743117299150)
XLA Ops:
  5.0 6.4 %all-to-all-start = ((bf16[8,2,768]{2,1,0:T(2,128)(2,1)}), bf16[8,2,768]{2,1,0:T(2,128)(2,1)S(1)}, u32[]{:S(2)}, u32[]{:S(2)}) async-start(bf16[8,2,768]{2,1,0:T(2,128)(2,1)} %reshape.94), calls=%async_computation | async-start | bytes 49152 | tf_op jit(solution)/shard_map/all_to_all | solution.py:156
  14.1 5.7 %collective-permute-start = (bf16[192,192]{1,0:T(8,128)(2,1)S(1)}, bf16[192,192]{1,0:T(8,128)(2,1)S(1)}, u32[]{:S(2)}, u32[]{:S(2)}) collective-permute-start(bf16[192,192]{1,0:T(8,128)(2,1)S(1)} %pad_maximum_fusion.1), channel_id=1, source_target_pairs={{0,0},{1,8},{2,16},{3,24},{4,32},{5,40},{6,48},{7,56},{8,64},{9,72... | collective-permute-start | bytes 221192 | tf_op jit(solution)/shard_map/ppermute | solution.py:147
  30.9 2.9 %collective-permute-start.16 = (f32[2,48]{1,0:T(2,128)S(1)}, f32[2,48]{1,0:T(2,128)S(1)}, u32[]{:S(2)}, u32[]{:S(2)}) collective-permute-start(f32[2,48]{1,0:T(2,128)S(1)} %fusion.61), channel_id=1, source_target_pairs={{0,32},{8,40},{16,48},{24,56},{32,0},{40,8},{48,16},{56,24},{64,96... | collective-permute-start | bytes 1160 | tf_op jit(solution)/shard_map/ppermute | solution.py:37
  33.8 2.9 %collective-permute-start.15 = (f32[2,48]{1,0:T(2,128)S(1)}, f32[2,48]{1,0:T(2,128)S(1)}, u32[]{:S(2)}, u32[]{:S(2)}) collective-permute-start(f32[2,48]{1,0:T(2,128)S(1)} %fusion.61), channel_id=1, source_target_pairs={{0,48},{8,56},{16,0},{24,8},{32,16},{40,24},{48,32},{56,40},{64,11... | collective-permute-start | bytes 1160 | tf_op jit(solution)/shard_map/ppermute | solution.py:37
  53.1 3.4 %collective-permute-done.20 = f32[2,48]{1,0:T(2,128)S(1)} collective-permute-done((f32[2,48]{1,0:T(2,128)S(1)}, f32[2,48]{1,0:T(2,128)S(1)}, u32[]{:S(2)}, u32[]{:S(2)}) %collective-permute-start.20) | collective-permute-done | bytes 416 | tf_op jit(solution)/shard_map/ppermute | solution.py:37
  56.5 10.0 %all-to-all-start.1 = ((bf16[32,2,192]{2,1,0:T(2,128)(2,1)}), bf16[32,2,192]{2,1,0:T(2,128)(2,1)S(1)}, u32[]{:S(2)}, u32[]{:S(2)}) async-start(bf16[32,2,192]{2,1,0:T(2,128)(2,1)} %reshape.96), calls=%async_computation.1 | async-start | bytes 65536 | tf_op jit(solution)/shard_map/all_to_all | solution.py:164
  69.3 7.2 %all-to-all-done.1 = bf16[32,2,192]{2,1,0:T(2,128)(2,1)S(1)} async-done(((bf16[32,2,192]{2,1,0:T(2,128)(2,1)}), bf16[32,2,192]{2,1,0:T(2,128)(2,1)S(1)}, u32[]{:S(2)}, u32[]{:S(2)}) %all-to-all-start.1) | async-done | bytes 24608 | tf_op jit(solution)/shard_map/all_to_all | solution.py:164
  77.1 3.4 %collective-permute-start.3 = (bf16[192,256]{1,0:T(8,128)(2,1)S(1)}, bf16[192,256]{1,0:T(8,128)(2,1)S(1)}, u32[]{:S(2)}, u32[]{:S(2)}) collective-permute-start(bf16[192,256]{1,0:T(8,128)(2,1)S(1)} %get-tuple-element.19), channel_id=1, source_target_pairs={{0,128},{8,136},{16,144},{24,152},{32,160},{40,168},{48,176},{56,1... | collective-permute-start | bytes 294920 | tf_op jit(solution)/shard_map/ppermute | solution.py:37
  82.0 5.8 %collective-permute-done.3 = bf16[192,256]{1,0:T(8,128)(2,1)S(1)} collective-permute-done((bf16[192,256]{1,0:T(8,128)(2,1)S(1)}, bf16[192,256]{1,0:T(8,128)(2,1)S(1)}, u32[]{:S(2)}, u32[]{:S(2)}) %collective-permute-start.3) | collective-permute-done | bytes 98336 | tf_op jit(solution)/shard_map/ppermute | solution.py:37
  94.2 5.6 %collective-permute-done.4 = bf16[4,192,256]{2,1,0:T(8,128)(2,1)S(1)} collective-permute-done((bf16[4,192,256]{2,1,0:T(8,128)(2,1)S(1)}, bf16[4,192,256]{2,1,0:T(8,128)(2,1)S(1)}, u32[]{:S(2)}, u32[]{:S(2)}) %collective-permute-start.4) | collective-permute-done | bytes 393248 | tf_op jit(solution)/shard_map/ppermute | solution.py:37
  101.4 5.5 %collective-permute-done.6 = bf16[4,192,256]{2,1,0:T(8,128)(2,1)S(1)} collective-permute-done((bf16[4,192,256]{2,1,0:T(8,128)(2,1)S(1)}, bf16[4,192,256]{2,1,0:T(8,128)(2,1)S(1)}, u32[]{:S(2)}, u32[]{:S(2)}) %collective-permute-start.6) | collective-permute-done | bytes 393248 | tf_op jit(solution)/shard_map/ppermute | solution.py:37
  107.7 3.8 %collective-permute-start.7 = (bf16[4,4,192,256]{3,2,1,0:T(8,128)(2,1)}, bf16[4,4,192,256]{3,2,1,0:T(8,128)(2,1)}, u32[]{:S(2)}, u32[]{:S(2)}) collective-permute-start(bf16[4,4,192,256]{3,2,1,0:T(8,128)(2,1)} %bitcast_dynamic-update-slice_fusion), channel_id=1, source_target_pairs={{0,8},{8,0},{16,24},{24,16},{32,40},{40,32},{48,56},{56,48},{64,72... | collective-permute-start | bytes 4718600 | tf_op jit(solution)/shard_map/ppermute | solution.py:37
  114.5 5.4 %collective-permute-done.9 = bf16[2,192,256]{2,1,0:T(8,128)(2,1)S(1)} collective-permute-done((bf16[2,192,256]{2,1,0:T(8,128)(2,1)S(1)}, bf16[2,192,256]{2,1,0:T(8,128)(2,1)S(1)}, u32[]{:S(2)}, u32[]{:S(2)}) %collective-permute-start.9) | collective-permute-done | bytes 196640 | tf_op jit(solution)/shard_map/ppermute | solution.py:37
  126.3 2.9 %copy.120 = bf16[1,4,4,192,256]{3,2,4,0,1:T(4,128)(2,1)S(1)} copy(bf16[1,4,4,192,256]{4,3,2,1,0:T(8,128)(2,1)} %bitcast.11) | data formatting | bytes 3145728 | tf_op jit(solution)/shard_map/broadcast_in_dim | solution.py:49
  129.3 3.0 %broadcast_in_dim.155 = bf16[2,4,4,192,256]{3,2,4,0,1:T(4,128)(2,1)} broadcast(bf16[]{:T(256)} %constant.182.clone.1), dimensions={} | broadcast | bytes 3145730 | tf_op jit(solution)/shard_map/broadcast_in_dim | solution.py:47
  134.3 2.9 %copy.121 = bf16[1,4,4,192,256]{3,2,4,0,1:T(4,128)(2,1)S(1)} copy(bf16[1,4,4,192,256]{4,3,2,1,0:T(8,128)(2,1)} %bitcast.12) | data formatting | bytes 3145728 | tf_op jit(solution)/shard_map/broadcast_in_dim | solution.py:49
  139.3 3.3 %fusion.41 = (bf16[4,8,192,64]{2,0,3,1:T(4,128)(2,1)}, bf16[4,192,8,64]{1,0,3,2:T(4,128)(2,1)S(1)}) fusion(bf16[4,8,192,256]{2,0,3,1:T(4,128)(2,1)} %bitcast.14), kind=kLoop, calls=%fused_computation.113 | loop fusion | bytes 3145728 | tf_op jit(solution)/shard_map/slice | solution.py:162
  146.8 3.4 %copy.133 = bf16[4,8,192,64]{3,2,1,0:T(8,128)(2,1)} copy(bf16[4,8,192,64]{2,0,3,1:T(4,128)(2,1)} %get-tuple-element.20) | data formatting | bytes 1572864 | tf_op jit(solution)/shard_map/slice | solution.py:162
  166.1 3.1 %fusion.4 = f32[24,8,8,128]{3,2,1,0:T(8,128)} fusion(bf16[192,768]{1,0:T(8,128)(2,1)S(1)} %copy-done, bf16[768,1024]{0,1:T(8,128)(2,1)} %reshape.93), kind=kOutput, calls=%fused_computation.12 | convolution fusion | flops 302186496 | bytes 2654208 | tf_op jit(solution)/shard_map/dot_general | solution.py:179
  169.2 3.2 %fusion.3 = f32[192,8,128]{2,0,1:T(8,128)} fusion(bf16[8,128,768]{2,1,0:T(8,128)(2,1)S(1)} %bitcast.114, bf16[768,1024]{0,1:T(8,128)(2,1)S(1)} %copy-done.1, f32[24,8,8,128]{3,2,1,0:T(8,128)} %fusion.4, bf16[192,768]{1,0:T(8,128)(2,1)} %param.12, pred[128]{0:T(512)(128)(4,1)S(1)} %iota_compare_fusion.13, s32[768]{0:T(1024)S(1)} %iota_add_fusion, ...), kind=kOutput, calls=%fused_computation.11 | convolution fusion | flops 605601792 | bytes 5412352 | tf_op jit(solution)/shard_map/dot_general | solution.py:180
  175.2 4.8 %all-to-all-start.2 = ((f32[8,192,256]{2,1,0:T(8,128)}), f32[8,192,256]{2,1,0:T(8,128)S(1)}, u32[]{:S(2)}, u32[]{:S(2)}) async-start(f32[8,192,256]{2,1,0:T(8,128)} %maximum_bitcast_fusion), calls=%async_computation.2 | async-start | bytes 3145728 | tf_op jit(solution)/shard_map/all_to_all | solution.py:188
  179.9 20.5 %all-to-all-done.2 = f32[8,192,256]{2,1,0:T(8,128)S(1)} async-done(((f32[8,192,256]{2,1,0:T(8,128)}), f32[8,192,256]{2,1,0:T(8,128)S(1)}, u32[]{:S(2)}, u32[]{:S(2)}) %all-to-all-start.2) | async-done | bytes 1572896 | tf_op jit(solution)/shard_map/all_to_all | solution.py:188
  201.7 8.9 %all-to-all-start.3 = ((f32[32,1,384]{2,1,0:T(1,128)}), f32[32,1,384]{2,1,0:T(1,128)S(1)}, u32[]{:S(2)}, u32[]{:S(2)}) async-start(f32[32,1,384]{2,1,0:T(1,128)} %reshape.98), calls=%async_computation.3 | async-start | bytes 98304 | tf_op jit(solution)/shard_map/all_to_all | solution.py:191
  212.2 8.1 %all-to-all-done.3 = f32[32,1,384]{2,1,0:T(1,128)S(1)} async-done(((f32[32,1,384]{2,1,0:T(1,128)}), f32[32,1,384]{2,1,0:T(1,128)S(1)}, u32[]{:S(2)}, u32[]{:S(2)}) %all-to-all-start.3) | async-done | bytes 49184 | tf_op jit(solution)/shard_map/all_to_all | solution.py:191
  (151 shorter events, 89.0 us)
Async XLA Ops:
  5.0 51.5 %all-to-all-start = ((bf16[8,2,768]{2,1,0:T(2,128)(2,1)}), bf16[8,2,768]{2,1,0:T(2,128)(2,1)S(1)}, u32[]{:S(2)}, u32[]{:S(2)}) async-start(bf16[8,2,768]{2,1,0:T(2,128)(2,1)} %reshape.94), calls=%async_computation | async-start | bytes 49152 | tf_op jit(solution)/shard_map/all_to_all | solution.py:156
  14.1 52.6 %collective-permute-start = (bf16[192,192]{1,0:T(8,128)(2,1)S(1)}, bf16[192,192]{1,0:T(8,128)(2,1)S(1)}, u32[]{:S(2)}, u32[]{:S(2)}) collective-permute-start(bf16[192,192]{1,0:T(8,128)(2,1)S(1)} %pad_maximum_fusion.1), channel_id=1, source_target_pairs={{0,0},{1,8},{2,16},{3,24},{4,32},{5,40},{6,48},{7,56},{8,64},{9,72... | collective-permute-start | bytes 221192 | tf_op jit(solution)/shard_map/ppermute | solution.py:147
  27.1 3.8 %collective-permute-start.13 = (f32[2,48]{1,0:T(2,128)S(1)}, f32[2,48]{1,0:T(2,128)S(1)}, u32[]{:S(2)}, u32[]{:S(2)}) collective-permute-start(f32[2,48]{1,0:T(2,128)S(1)} %fusion.39), channel_id=1, source_target_pairs={{0,4},{1,5},{2,6},{3,7},{4,0},{5,1},{6,2},{7,3},{8,12},{9,13},{10,... | collective-permute-start | bytes 1160 | tf_op jit(solution)/shard_map/ppermute | solution.py:37
  30.9 6.4 %collective-permute-start.16 = (f32[2,48]{1,0:T(2,128)S(1)}, f32[2,48]{1,0:T(2,128)S(1)}, u32[]{:S(2)}, u32[]{:S(2)}) collective-permute-start(f32[2,48]{1,0:T(2,128)S(1)} %fusion.61), channel_id=1, source_target_pairs={{0,32},{8,40},{16,48},{24,56},{32,0},{40,8},{48,16},{56,24},{64,96... | collective-permute-start | bytes 1160 | tf_op jit(solution)/shard_map/ppermute | solution.py:37
  33.8 4.4 %collective-permute-start.15 = (f32[2,48]{1,0:T(2,128)S(1)}, f32[2,48]{1,0:T(2,128)S(1)}, u32[]{:S(2)}, u32[]{:S(2)}) collective-permute-start(f32[2,48]{1,0:T(2,128)S(1)} %fusion.61), channel_id=1, source_target_pairs={{0,48},{8,56},{16,0},{24,8},{32,16},{40,24},{48,32},{56,40},{64,11... | collective-permute-start | bytes 1160 | tf_op jit(solution)/shard_map/ppermute | solution.py:37
  36.7 3.6 %collective-permute-start.14 = (f32[2,48]{1,0:T(2,128)S(1)}, f32[2,48]{1,0:T(2,128)S(1)}, u32[]{:S(2)}, u32[]{:S(2)}) collective-permute-start(f32[2,48]{1,0:T(2,128)S(1)} %fusion.61), channel_id=1, source_target_pairs={{0,16},{8,24},{16,32},{24,40},{32,48},{40,56},{48,0},{56,8},{64,80... | collective-permute-start | bytes 1160 | tf_op jit(solution)/shard_map/ppermute | solution.py:37
  40.4 4.2 %collective-permute-start.19 = (f32[2,48]{1,0:T(2,128)S(1)}, f32[2,48]{1,0:T(2,128)S(1)}, u32[]{:S(2)}, u32[]{:S(2)}) collective-permute-start(f32[2,48]{1,0:T(2,128)S(1)} %add_add_fusion.1), channel_id=1, source_target_pairs={{0,2},{1,3},{2,0},{3,1},{4,6},{5,7},{6,4},{7,5},{8,10},{9,11},{10,... | collective-permute-start | bytes 1160 | tf_op jit(solution)/shard_map/ppermute | solution.py:37
  46.7 6.3 %collective-permute-start.22 = (f32[2,48]{1,0:T(2,128)S(1)}, f32[2,48]{1,0:T(2,128)S(1)}, u32[]{:S(2)}, u32[]{:S(2)}) collective-permute-start(f32[2,48]{1,0:T(2,128)S(1)} %add_add_fusion), channel_id=1, source_target_pairs={{0,128},{8,136},{16,144},{24,152},{32,160},{40,168},{48,176},{56,1... | collective-permute-start | bytes 1160 | tf_op jit(solution)/shard_map/ppermute | solution.py:37
  49.3 3.8 %collective-permute-start.21 = (f32[2,48]{1,0:T(2,128)S(1)}, f32[2,48]{1,0:T(2,128)S(1)}, u32[]{:S(2)}, u32[]{:S(2)}) collective-permute-start(f32[2,48]{1,0:T(2,128)S(1)} %add_add_fusion), channel_id=1, source_target_pairs={{0,192},{8,200},{16,208},{24,216},{32,224},{40,232},{48,240},{56,2... | collective-permute-start | bytes 1160 | tf_op jit(solution)/shard_map/ppermute | solution.py:37
  51.9 4.5 %collective-permute-start.20 = (f32[2,48]{1,0:T(2,128)S(1)}, f32[2,48]{1,0:T(2,128)S(1)}, u32[]{:S(2)}, u32[]{:S(2)}) collective-permute-start(f32[2,48]{1,0:T(2,128)S(1)} %add_add_fusion), channel_id=1, source_target_pairs={{0,64},{8,72},{16,80},{24,88},{32,96},{40,104},{48,112},{56,120},{... | collective-permute-start | bytes 1160 | tf_op jit(solution)/shard_map/ppermute | solution.py:37
  56.5 20.0 %all-to-all-start.1 = ((bf16[32,2,192]{2,1,0:T(2,128)(2,1)}), bf16[32,2,192]{2,1,0:T(2,128)(2,1)S(1)}, u32[]{:S(2)}, u32[]{:S(2)}) async-start(bf16[32,2,192]{2,1,0:T(2,128)(2,1)} %reshape.96), calls=%async_computation.1 | async-start | bytes 65536 | tf_op jit(solution)/shard_map/all_to_all | solution.py:164
  66.8 13.6 %collective-permute-start.1 = (bf16[192,256]{1,0:T(8,128)(2,1)S(1)}, bf16[192,256]{1,0:T(8,128)(2,1)S(1)}, u32[]{:S(2)}, u32[]{:S(2)}) collective-permute-start(bf16[192,256]{1,0:T(8,128)(2,1)S(1)} %get-tuple-element.19), channel_id=1, source_target_pairs={{0,64},{8,72},{16,80},{24,88},{32,96},{40,104},{48,112},{56,120},{... | collective-permute-start | bytes 294920 | tf_op jit(solution)/shard_map/ppermute | solution.py:37
  76.6 5.4 %collective-permute-start.2 = (bf16[192,256]{1,0:T(8,128)(2,1)S(1)}, bf16[192,256]{1,0:T(8,128)(2,1)S(1)}, u32[]{:S(2)}, u32[]{:S(2)}) collective-permute-start(bf16[192,256]{1,0:T(8,128)(2,1)S(1)} %get-tuple-element.19), channel_id=1, source_target_pairs={{0,192},{8,200},{16,208},{24,216},{32,224},{40,232},{48,240},{56,2... | collective-permute-start | bytes 294920 | tf_op jit(solution)/shard_map/ppermute | solution.py:37
  77.1 10.7 %collective-permute-start.3 = (bf16[192,256]{1,0:T(8,128)(2,1)S(1)}, bf16[192,256]{1,0:T(8,128)(2,1)S(1)}, u32[]{:S(2)}, u32[]{:S(2)}) collective-permute-start(bf16[192,256]{1,0:T(8,128)(2,1)S(1)} %get-tuple-element.19), channel_id=1, source_target_pairs={{0,128},{8,136},{16,144},{24,152},{32,160},{40,168},{48,176},{56,1... | collective-permute-start | bytes 294920 | tf_op jit(solution)/shard_map/ppermute | solution.py:37
  87.8 12.1 %collective-permute-start.4 = (bf16[4,192,256]{2,1,0:T(8,128)(2,1)S(1)}, bf16[4,192,256]{2,1,0:T(8,128)(2,1)S(1)}, u32[]{:S(2)}, u32[]{:S(2)}) collective-permute-start(bf16[4,192,256]{2,1,0:T(8,128)(2,1)S(1)} %bitcast_dynamic-update-slice_fusion.8), channel_id=1, source_target_pairs={{0,16},{8,24},{16,32},{24,40},{32,48},{40,56},{48,0},{56,8},{64,80... | collective-permute-start | bytes 1179656 | tf_op jit(solution)/shard_map/ppermute | solution.py:37
  88.5 23.0 %collective-permute-start.8 = (bf16[192,256]{0,1:T(8,128)(2,1)S(1)}, bf16[192,256]{0,1:T(8,128)(2,1)S(1)}, u32[]{:S(2)}, u32[]{:S(2)}) collective-permute-start(bf16[192,256]{0,1:T(8,128)(2,1)S(1)} %get-tuple-element.27), channel_id=1, source_target_pairs={{0,4},{1,5},{2,6},{3,7},{4,0},{5,1},{6,2},{7,3},{8,12},{9,13},{10,... | collective-permute-start | bytes 294920 | tf_op jit(solution)/shard_map/ppermute | solution.py:37
  89.9 10.7 %collective-permute-start.5 = (bf16[4,192,256]{2,1,0:T(8,128)(2,1)S(1)}, bf16[4,192,256]{2,1,0:T(8,128)(2,1)S(1)}, u32[]{:S(2)}, u32[]{:S(2)}) collective-permute-start(bf16[4,192,256]{2,1,0:T(8,128)(2,1)S(1)} %bitcast_dynamic-update-slice_fusion.8), channel_id=1, source_target_pairs={{0,48},{8,56},{16,0},{24,8},{32,16},{40,24},{48,32},{56,40},{64,11... | collective-permute-start | bytes 1179656 | tf_op jit(solution)/shard_map/ppermute | solution.py:37
  92.1 14.8 %collective-permute-start.6 = (bf16[4,192,256]{2,1,0:T(8,128)(2,1)S(1)}, bf16[4,192,256]{2,1,0:T(8,128)(2,1)S(1)}, u32[]{:S(2)}, u32[]{:S(2)}) collective-permute-start(bf16[4,192,256]{2,1,0:T(8,128)(2,1)S(1)} %bitcast_dynamic-update-slice_fusion.8), channel_id=1, source_target_pairs={{0,32},{8,40},{16,48},{24,56},{32,0},{40,8},{48,16},{56,24},{64,96... | collective-permute-start | bytes 1179656 | tf_op jit(solution)/shard_map/ppermute | solution.py:37
  107.7 26.7 %collective-permute-start.7 = (bf16[4,4,192,256]{3,2,1,0:T(8,128)(2,1)}, bf16[4,4,192,256]{3,2,1,0:T(8,128)(2,1)}, u32[]{:S(2)}, u32[]{:S(2)}) collective-permute-start(bf16[4,4,192,256]{3,2,1,0:T(8,128)(2,1)} %bitcast_dynamic-update-slice_fusion), channel_id=1, source_target_pairs={{0,8},{8,0},{16,24},{24,16},{32,40},{40,32},{48,56},{56,48},{64,72... | collective-permute-start | bytes 4718600 | tf_op jit(solution)/shard_map/ppermute | solution.py:37
  111.6 8.2 %collective-permute-start.9 = (bf16[2,192,256]{2,1,0:T(8,128)(2,1)S(1)}, bf16[2,192,256]{2,1,0:T(8,128)(2,1)S(1)}, u32[]{:S(2)}, u32[]{:S(2)}) collective-permute-start(bf16[2,192,256]{2,1,0:T(8,128)(2,1)S(1)} %constant_dynamic-update-slice_fusion), channel_id=1, source_target_pairs={{0,1},{1,2},{2,3},{3,0},{4,5},{5,6},{6,7},{7,4},{8,9},{9,10},{10,1... | collective-permute-start | bytes 589832 | tf_op jit(solution)/shard_map/ppermute | solution.py:37
  111.9 10.6 %collective-permute-start.10 = (bf16[2,192,256]{2,1,0:T(8,128)(2,1)S(1)}, bf16[2,192,256]{2,1,0:T(8,128)(2,1)S(1)}, u32[]{:S(2)}, u32[]{:S(2)}) collective-permute-start(bf16[2,192,256]{2,1,0:T(8,128)(2,1)S(1)} %constant_dynamic-update-slice_fusion), channel_id=1, source_target_pairs={{0,3},{1,0},{2,1},{3,2},{4,7},{5,4},{6,5},{7,6},{8,11},{9,8},{10,9... | collective-permute-start | bytes 589832 | tf_op jit(solution)/shard_map/ppermute | solution.py:37
  114.4 8.9 %collective-permute-start.11 = (bf16[2,192,256]{2,1,0:T(8,128)(2,1)S(1)}, bf16[2,192,256]{2,1,0:T(8,128)(2,1)S(1)}, u32[]{:S(2)}, u32[]{:S(2)}) collective-permute-start(bf16[2,192,256]{2,1,0:T(8,128)(2,1)S(1)} %constant_dynamic-update-slice_fusion), channel_id=1, source_target_pairs={{0,2},{1,3},{2,0},{3,1},{4,6},{5,7},{6,4},{7,5},{8,10},{9,11},{10,... | collective-permute-start | bytes 589832 | tf_op jit(solution)/shard_map/ppermute | solution.py:37
  175.2 25.3 %all-to-all-start.2 = ((f32[8,192,256]{2,1,0:T(8,128)}), f32[8,192,256]{2,1,0:T(8,128)S(1)}, u32[]{:S(2)}, u32[]{:S(2)}) async-start(f32[8,192,256]{2,1,0:T(8,128)} %maximum_bitcast_fusion), calls=%async_computation.2 | async-start | bytes 3145728 | tf_op jit(solution)/shard_map/all_to_all | solution.py:188
  201.7 18.6 %all-to-all-start.3 = ((f32[32,1,384]{2,1,0:T(1,128)}), f32[32,1,384]{2,1,0:T(1,128)S(1)}, u32[]{:S(2)}, u32[]{:S(2)}) async-start(f32[32,1,384]{2,1,0:T(1,128)} %reshape.98), calls=%async_computation.3 | async-start | bytes 98304 | tf_op jit(solution)/shard_map/all_to_all | solution.py:191
  (14 other events, 382.3 us)

commit v2 on v1

v2 whole, which is shorter than its diff:
```python
import functools
import jax
import jax.numpy as jnp
from jax import lax
from jax.experimental import pallas as pl
from jax.experimental.pallas import tpu as pltpu
from jax.sharding import PartitionSpec as P

shift_value = 2.0
penalty = 2.5
both = ("row", "col")
f32 = jnp.float32
bf16 = jnp.bfloat16
lanes = 128
extra = 16


def pick(one_hot, values):
    return jnp.dot(
        one_hot.astype(values.dtype),
        values,
        precision=lax.Precision.HIGHEST if values.dtype == f32 else None,
        preferred_element_type=f32,
    ).astype(values.dtype)


z_hi, x_axis, core = ("row", 8, 4), ("row", 2, 4), ("row", 1, 2)
z_lo, y_axis = ("col", 4, 2), ("col", 1, 4)
offsets = {2: (0, 1), 4: (0, -1, 1, 2)}


def digit(axis):
    name, stride, length = axis
    return lax.axis_index(name) // stride % length


def turn(x, axis, step):
    name, stride, length = axis
    pairs = []
    for i in range(lax.axis_size(name)):
        d = i // stride % length
        pairs.append((i, i + ((d + step) % length - d) * stride))
    return lax.ppermute(x, name, pairs)


def gather_digit(x, axis):
    moved = [turn(x, axis, -offset) for offset in offsets[axis[2]][1:]]
    return jnp.stack([x] + moved)


def gather_rows(x):
    out = gather_digit(gather_digit(x, z_hi), x_axis)
    out = out.reshape((-1,) + x.shape)
    return out, turn(out, core, 1)


def gather_cols(x):
    out = gather_digit(gather_digit(x, z_lo), y_axis)
    return out.reshape((-1,) + x.shape)


def to_column(x, rows, cols, per):
    return lax.ppermute(
        x,
        both,
        [
            (r * cols + c, ((r % per) * cols + c) * cols + r // per)
            for r in range(rows)
            for c in range(cols)
        ],
    )


def three_parts(x):
    high = lax.reduce_precision(x, 8, 7)
    middle = lax.reduce_precision(x - high, 8, 7)
    low = x - high - middle
    return jnp.stack([high, middle, low]).astype(bf16)


def three_sum(parts):
    return parts[0] + parts[1] + parts[2]


def weights_kernel(block, width, is_q, *refs):
    if is_q:
        place, own, other, around, multiplier, hamiltonian, out, right, left = refs
    else:
        (place, own, other, around, multiplier, segments, ph_segments, lengths, out, scale, right, left) = refs
    zh, xx, cc, zl, yy = (place[i] for i in range(5))
    ids = []
    for xr, xo in enumerate(offsets[4]):
        for cr in range(2):
            k = xr * 2 + cr
            source = own if cr == 0 else other
            c = lax.rem(xx + xo + 4, 4) * 2 + (cc if cr == 0 else 1 - cc)
            ids.append(c)
            for zr, zo in enumerate(offsets[4]):
                j = lax.rem(zh + zo + 4, 4)
                right[pl.ds(pl.multiple_of(j * block, block), block), k * lanes : (k + 1) * lanes] = source[
                    xr * 4 + zr, :block, :
                ]
            dz = jnp.where(c // 4 == zl, 0, 1)
            dy = lax.rem(lax.rem(c, 4) - yy + 4, 4)
            dy = jnp.where(dy == 0, 0, jnp.where(dy == 3, 1, dy + 1))
            left[:, k * lanes : (k + 1) * lanes] = around[dy * 2 + dz, :block, :]
    gram = lax.dot_general(
        left[...], right[...], (((1,), (1,)), ((), ())), preferred_element_type=f32
    )
    row = lax.broadcasted_iota(jnp.int32, (block, width), 0)
    col = lax.broadcasted_iota(jnp.int32, (block, width), 1)
    on_diag = row + ((zh * 8 + xx * 2 + cc) * block - (zl * 4 + yy) * width) == col
    if is_q:
        diagonal = shift_value
    else:
        total = jnp.zeros((extra, lanes), f32)
        for source in (own, other):
            for b in range(16):
                total = total + source[b, block:, :].astype(f32)
        mean_d = (total[0:1] + total[1:2] + total[2:3]) / lengths[...]
        mean_u = (total[3:4] + total[4:5] + total[5:6]) / lengths[...]
        diagonal = jnp.sum(ph_segments[...] * (2.0 * mean_d), axis=1, keepdims=True)
        scale[...] = jnp.sum(
            segments[...] * (2.0 * (mean_u + penalty * mean_d)), axis=1, keepdims=True
        )
    resid = jnp.where(on_diag, diagonal, 0.0) - gram
    weight = (multiplier[...].astype(f32) + penalty * resid).astype(bf16)
    term = -2.0 * jnp.dot(weight, right[...], preferred_element_type=f32)
    if is_q:
        energy = 2.0 * jnp.dot(hamiltonian[...], right[...], preferred_element_type=f32)
        lane = lax.broadcasted_iota(jnp.int32, energy.shape, 1)
        term = term + jnp.where(lax.rem(lane, lanes) < lanes // 2, energy, 0.0)
    for k, c in enumerate(ids):
        out[c] = term[:, k * lanes : (k + 1) * lanes]


def apply_weights(is_q, *args):
    block, width = args[4].shape
    cols = 8
    shapes = [jax.ShapeDtypeStruct((cols, block, lanes), f32)]
    if not is_q:
        shapes.append(jax.ShapeDtypeStruct((block, 1), f32))
    vmem = pl.BlockSpec(memory_space=pltpu.VMEM)
    return pl.pallas_call(
        functools.partial(weights_kernel, block, width, is_q),
        out_shape=shapes,
        in_specs=[pl.BlockSpec(memory_space=pltpu.SMEM)] + [vmem] * (len(args) - 1),
        out_specs=[vmem] * len(shapes),
        scratch_shapes=[
            pltpu.VMEM((width, cols * lanes), bf16),
            pltpu.VMEM((block, cols * lanes), bf16),
        ],
        compiler_params=pltpu.CompilerParams(vmem_limit_bytes=40 * 1024 * 1024),
        name="weights_q" if is_q else "weights_g",
    )(*args)


def local(
    density_factor,
    hole_factor,
    ph_factor,
    hamiltonian,
    multiplier_q,
    multiplier_g,
    ph_perm,
    block_lengths,
):
    rows, cols = lax.axis_size("row"), lax.axis_size("col")
    row_index = lax.axis_index("row")
    col_index = lax.axis_index("col")
    block, part = density_factor.shape
    width = multiplier_q.shape[1]
    per = width // block
    place = jnp.stack([digit(axis) for axis in (z_hi, x_axis, core, z_lo, y_axis)]).astype(jnp.int32)
    row_ids = row_index * block + jnp.arange(block, dtype=jnp.int32)
    col_ids = col_index * width + jnp.arange(width, dtype=jnp.int32)
    on_diag = row_ids[:, None] == col_ids[None, :]
    mine = lax.dynamic_slice_in_dim(ph_perm, row_index * block, block)

    places = jnp.arange(rows * block, dtype=jnp.int32)
    target = jnp.sum(jnp.where(ph_perm[None, :] == row_ids[:, None], places[None, :], 0), axis=1)
    order = jnp.sum((target[None, :] < target[:, None]).astype(jnp.int32), axis=1)
    spot = jnp.arange(block, dtype=jnp.int32)
    send = spot[:, None] == order[None, :]
    source = mine // block
    earlier = (source[None, :] == source[:, None]) & (spot[None, :] < spot[:, None])
    slot = source * (block // rows) + jnp.sum(earlier.astype(jnp.int32), axis=1)
    receive = slot[:, None] == spot[None, :]

    lengths = jnp.concatenate(
        [block_lengths, jnp.zeros((lanes - block_lengths.shape[0],), jnp.int32)]
    )
    lane = jnp.arange(lanes, dtype=jnp.int32)
    ends = jnp.sum(jnp.where(lane[:, None] >= lane[None, :], lengths[None, :], 0), axis=1)
    starts = ends - lengths
    segments = ((row_ids[:, None] >= starts) & (row_ids[:, None] < ends)).astype(f32)
    ph_segments = ((mine[:, None] >= starts) & (mine[:, None] < ends)).astype(f32)
    density_sq = jnp.sum(jnp.square(density_factor.astype(f32)), axis=1)
    ph_sq = jnp.sum(jnp.square(ph_factor.astype(f32)), axis=1)
    mult_diag = jnp.sum(jnp.where(on_diag, multiplier_g.astype(f32), 0.0), axis=1)
    stat_d = jnp.sum(segments * density_sq[:, None], axis=0)
    stat_u = jnp.sum(ph_segments * (mult_diag - penalty * ph_sq)[:, None], axis=0)

    def stat_rows(d, u):
        rest = jnp.zeros((extra - 6, lanes), bf16)
        return jnp.concatenate([three_parts(d), three_parts(u), rest])

    pair_local = jnp.concatenate([density_factor, hole_factor], axis=1)
    own_q, other_q = gather_rows(to_column(pair_local, rows, cols, per))
    around_q = gather_cols(jnp.concatenate([pair_local, stat_rows(stat_d, stat_u)]))
    stats = jnp.sum(around_q[:, block:].astype(f32), axis=0)
    stats = stat_rows(three_sum(stats[0:3]), three_sum(stats[3:6]))

    leaving = pick(send, density_factor)
    density_ph = pick(receive, lax.all_to_all(leaving, "row", 0, 0, tiled=True))
    ph_local = jnp.concatenate([density_ph, ph_factor], axis=1)
    own_g, other_g = gather_rows(jnp.concatenate([to_column(ph_local, rows, cols, per), stats]))
    around_g = gather_cols(ph_local)

    (parts_q,) = apply_weights(True, place, own_q, other_q, around_q, multiplier_q, hamiltonian)
    parts_g, scale_rows = apply_weights(
        False,
        place,
        own_g,
        other_g,
        around_g,
        multiplier_g,
        segments,
        ph_segments,
        jnp.maximum(lengths, 1).astype(f32)[None, :],
    )
    done_g = jnp.sum(lax.all_to_all(parts_g, "col", 0, 0), axis=0)
    done_q = jnp.sum(lax.all_to_all(parts_q, "col", 0, 0), axis=0)

    back = pick(receive.T, done_g[:, :part])
    returned = pick(send.T, lax.all_to_all(back, "row", 0, 0, tiled=True))
    grad_density = done_q[:, :part] + 2.0 * scale_rows * density_factor.astype(f32) + returned
    return (grad_density, done_q[:, part:], done_g[:, part:])


def solution(mesh):
    return jax.shard_map(
        local,
        mesh=mesh,
        in_specs=(
            P("row", "col"),
            P("row", "col"),
            P("row", "col"),
            P("row", "col"),
            P("row", "col"),
            P("row", "col"),
            P(),
            P(),
        ),
        out_specs=(P("row", "col"), P("row", "col"), P("row", "col")),
        check_vma=False,
    )
```

time: 224 us -> 158 us (0.71)
  local copies, waits for them, and re-layouts: 51.1 us -> 12.1 us
  waiting for transfers between devices: 73.1 us -> 52.1 us
  matrix products: 12.6 us -> 1.71 us
  Pallas kernels: 0 us -> 6.4 us
  other arithmetic: 13.2 us -> 9.1 us
  starting transfers between devices: 71.2 us -> 74.2 us
    ppermute x22, waiting for transfers between devices: 37.3 us -> 26.1 us  [turn(): return lax.ppermute(x, name, pairs)]
    broadcast_in_dim x9 -> x0, local copies, waits for them, and re-layouts: 10.5 us -> none  [the longest x4 6.07 us: gather_digit(): value[None]]
    all_to_all x3, waiting for transfers between devices: 27.7 us -> 17.9 us  [the longest x1 9.33 us: local(): density_ph = pick(receive, lax.all_to_all(leaving, 'row', 0, 0, tiled=True))]
    dot_general x6 -> x0, matrix products: 9.34 us -> none  [the longest x1 3.17 us: local(): jnp.dot(weight_q, pair_col, preferred_element_type=f32)]
    slice x6 -> x2, local copies, waits for them, and re-layouts: 8.91 us -> 0.17 us  [local(): return (grad_density, done_q[:, part:], done_g[:, part:])]
    reshape x3 -> x0, local copies, waits for them, and re-layouts: 7.43 us -> none  [the longest x1 2.85 us: local(): jnp.swapaxes(column[..., :2 * part], 1, 2).reshape(width, cols * 2 * part)]
    dynamic_update_slice x15 -> x0, local copies, waits for them, and re-layouts: 7.32 us -> none  [gather_digit(): lax.dynamic_update_slice_in_dim(out, value[None], (here + offset) % axis[...]
    pallas_call x0 -> x2, Pallas kernels: none -> 6.4 us  [apply_weights(): pl.pallas_call(functools.partial(weights_kernel, block, width, is_q), out...]
  transfers between devices with their start and end apart: 27 -> 28, of which waited for: 17 -> 14; matrix products, arithmetic and copies ran while one was open for 12% -> 11% of each run, Pallas kernels for 0% -> 4%
where the time goes in v2:
time: 158 us; the launch traced here: 157 us
  starting transfers between devices  74.2 us (47%)
  waiting for transfers between devices  52.1 us (33%)
  local copies, waits for them, and re-layouts  12.1 us (8%)
  other arithmetic  9.1 us (6%)
  Pallas kernels  6.4 us (4%)
  matrix products  1.71 us (1%)
    ppermute x22, starting transfers between devices, turn(): return lax.ppermute(x, name, pairs)  35.5 us
    ppermute x22, waiting for transfers between devices, turn(): return lax.ppermute(x, name, pairs)  26.1 us
    all_to_all x1, starting transfers between devices, local(): returned = pick(send.T, lax.all_to_all(back, 'row', 0, 0, tiled=True))  10.9 us
    ppermute x2, starting transfers between devices, to_column(): lax.ppermute(x, both, [(r * cols + c, (r % per * cols + c) * cols + r //...  9.56 us
    all_to_all x1, starting transfers between devices, local(): density_ph = pick(receive, lax.all_to_all(leaving, 'row', 0, 0, tiled=True))  9.48 us
    all_to_all x1, waiting for transfers between devices, local(): density_ph = pick(receive, lax.all_to_all(leaving, 'row', 0, 0, tiled=True))  9.33 us
    all_to_all x1, waiting for transfers between devices, local(): done_g = jnp.sum(lax.all_to_all(parts_g, 'col', 0, 0), axis=0)  8.59 us
    all_to_all x1, waiting for transfers between devices, local(): returned = pick(send.T, lax.all_to_all(back, 'row', 0, 0, tiled=True))  8.05 us
  transfers between devices with their start and end apart: 28, of which 14 were waited for; matrix products, arithmetic and copies ran while one was open for 11% of the time, Pallas kernels for 4%

profile of v2, /device:TPU:1, one launch (start us, length us, event | category | flops | bytes accessed | tf_op | source)
XLA Modules:
  0.0 156.7 jit_solution(16203894533188730334)
XLA Ops:
  2.2 6.3 %collective-permute-start = (bf16[192,128]{0,1:T(8,128)(2,1)S(1)}, bf16[192,128]{0,1:T(8,128)(2,1)S(1)}, u32[]{:S(2)}, u32[]{:S(2)}) collective-permute-start(bf16[192,128]{0,1:T(8,128)(2,1)S(1)} %constant_dynamic-update-slice_fusion), channel_id=1, source_target_pairs={{0,0},{1,8},{2,16},{3,24},{4,32},{5,40},{6,48},{7,56},{8,64},{9,72... | collective-permute-start | bytes 147464 | tf_op jit(solution)/shard_map/ppermute | solution.py:63
  14.7 2.8 %collective-permute-start.8 = (bf16[208,128]{0,1:T(8,128)(2,1)S(1)}, bf16[208,128]{0,1:T(8,128)(2,1)S(1)}, u32[]{:S(2)}, u32[]{:S(2)}) collective-permute-start(bf16[208,128]{0,1:T(8,128)(2,1)S(1)} %concatenate.19), channel_id=1, source_target_pairs={{0,4},{1,5},{2,6},{3,7},{4,0},{5,1},{6,2},{7,3},{8,12},{9,13},{10,... | collective-permute-start | bytes 159752 | tf_op jit(solution)/shard_map/ppermute | solution.py:43
  19.6 9.5 %all-to-all-start.1 = ((bf16[32,2,192]{2,1,0:T(2,128)(2,1)}), bf16[32,2,192]{2,1,0:T(2,128)(2,1)S(1)}, u32[]{:S(2)}, u32[]{:S(2)}) async-start(bf16[32,2,192]{2,1,0:T(2,128)(2,1)} %reshape.101), calls=%async_computation.1 | async-start | bytes 65536 | tf_op jit(solution)/shard_map/all_to_all | solution.py:215
  29.5 9.3 %all-to-all-done.1 = bf16[32,2,192]{2,1,0:T(2,128)(2,1)S(1)} async-done(((bf16[32,2,192]{2,1,0:T(2,128)(2,1)}), bf16[32,2,192]{2,1,0:T(2,128)(2,1)S(1)}, u32[]{:S(2)}, u32[]{:S(2)}) %all-to-all-start.1) | async-done | bytes 24608 | tf_op jit(solution)/shard_map/all_to_all | solution.py:215
  39.6 3.2 %collective-permute-start.2 = (bf16[192,128]{0,1:T(8,128)(2,1)S(1)}, bf16[192,128]{0,1:T(8,128)(2,1)S(1)}, u32[]{:S(2)}, u32[]{:S(2)}) collective-permute-start(bf16[192,128]{0,1:T(8,128)(2,1)S(1)} %collective-permute-done), channel_id=1, source_target_pairs={{0,192},{8,200},{16,208},{24,216},{32,224},{40,232},{48,240},{56,2... | collective-permute-start | bytes 147464 | tf_op jit(solution)/shard_map/ppermute | solution.py:43
  43.3 2.7 %collective-permute-start.10 = (bf16[2,208,128]{1,2,0:T(8,128)(2,1)S(1)}, bf16[2,208,128]{1,2,0:T(8,128)(2,1)S(1)}, u32[]{:S(2)}, u32[]{:S(2)}) collective-permute-start(bf16[2,208,128]{1,2,0:T(8,128)(2,1)S(1)} %get-tuple-element.31), channel_id=1, source_target_pairs={{0,3},{1,0},{2,1},{3,2},{4,7},{5,4},{6,5},{7,6},{8,11},{9,8},{10,9... | collective-permute-start | bytes 319496 | tf_op jit(solution)/shard_map/ppermute | solution.py:43
  47.7 2.5 %collective-permute-done.3 = bf16[192,128]{0,1:T(8,128)(2,1)S(1)} collective-permute-done((bf16[192,128]{0,1:T(8,128)(2,1)S(1)}, bf16[192,128]{0,1:T(8,128)(2,1)S(1)}, u32[]{:S(2)}, u32[]{:S(2)}) %collective-permute-start.3) | collective-permute-done | bytes 49184 | tf_op jit(solution)/shard_map/ppermute | solution.py:43
  50.6 2.4 %collective-permute-start.5 = (bf16[4,192,128]{1,2,0:T(8,128)(2,1)S(1)}, bf16[4,192,128]{1,2,0:T(8,128)(2,1)S(1)}, u32[]{:S(2)}, u32[]{:S(2)}) collective-permute-start(bf16[4,192,128]{1,2,0:T(8,128)(2,1)S(1)} %get-tuple-element.25), channel_id=1, source_target_pairs={{0,48},{8,56},{16,0},{24,8},{32,16},{40,24},{48,32},{56,40},{64,11... | collective-permute-start | bytes 589832 | tf_op jit(solution)/shard_map/ppermute | solution.py:43
  53.7 3.3 %collective-permute-start.12 = (bf16[192,128]{0,1:T(8,128)(2,1)}, bf16[192,128]{0,1:T(8,128)(2,1)}, u32[]{:S(2)}, u32[]{:S(2)}) collective-permute-start(bf16[192,128]{0,1:T(8,128)(2,1)} %get-tuple-element.35), channel_id=1, source_target_pairs={{0,0},{1,8},{2,16},{3,24},{4,32},{5,40},{6,48},{7,56},{8,64},{9,72... | collective-permute-start | bytes 147464 | tf_op jit(solution)/shard_map/ppermute | solution.py:63
  58.4 4.4 %collective-permute-done.6 = bf16[4,192,128]{1,2,0:T(8,128)(2,1)S(1)} collective-permute-done((bf16[4,192,128]{1,2,0:T(8,128)(2,1)S(1)}, bf16[4,192,128]{1,2,0:T(8,128)(2,1)S(1)}, u32[]{:S(2)}, u32[]{:S(2)}) %collective-permute-start.6) | collective-permute-done | bytes 196640 | tf_op jit(solution)/shard_map/ppermute | solution.py:43
  63.8 4.5 %collective-permute-start.7 = (bf16[16,192,128]{2,1,0:T(8,128)(2,1)S(1)}, bf16[16,192,128]{2,1,0:T(8,128)(2,1)S(1)}, u32[]{:S(2)}, u32[]{:S(2)}) collective-permute-start(bf16[16,192,128]{2,1,0:T(8,128)(2,1)S(1)} %bitcast.63), channel_id=1, source_target_pairs={{0,8},{8,0},{16,24},{24,16},{32,40},{40,32},{48,56},{56,48},{64,72... | collective-permute-start | bytes 2359304 | tf_op jit(solution)/shard_map/ppermute | solution.py:43
  70.5 3.6 %collective-permute-start.14 = (bf16[208,128]{0,1:T(8,128)(2,1)S(1)}, bf16[208,128]{0,1:T(8,128)(2,1)S(1)}, u32[]{:S(2)}, u32[]{:S(2)}) collective-permute-start(bf16[208,128]{0,1:T(8,128)(2,1)S(1)} %concatenate.21), channel_id=1, source_target_pairs={{0,192},{8,200},{16,208},{24,216},{32,224},{40,232},{48,240},{56,2... | collective-permute-start | bytes 159752 | tf_op jit(solution)/shard_map/ppermute | solution.py:43
  74.1 3.4 %weights_q.1 = f32[8,192,128]{2,1,0:T(8,128)} custom-call(s32[5]{0:T(128)S(1)} %stack.151.refs_0_, bf16[16,192,128]{2,1,0:T(8,128)(2,1)S(1)} %bitcast.64, bf16[16,192,128]{2,1,0:T(8,128)(2,1)S(1)} %collective-permute-done.7.refs_2_, bf16[8,208,128]{2,1,0:T(8,128)(2,1)S(1)} %bitcast.66, bf16[192,768]{1,0:T(8,128)(2,1)S(1)} %copy-done.1, ...), custom_call_target="tpu_custom_call" | custom-call | tf_op jit(solution)/shard_map/weights_q/pallas_call | solution.py:144
  77.4 5.1 %all-to-all-start = ((f32[8,192,128]{2,1,0:T(8,128)}), f32[8,192,128]{2,1,0:T(8,128)S(1)}, u32[]{:S(2)}, u32[]{:S(2)}) async-start(f32[8,192,128]{2,1,0:T(8,128)} %weights_q.1), calls=%async_computation | async-start | bytes 1572864 | tf_op jit(solution)/shard_map/all_to_all | solution.py:233
  87.3 3.6 %collective-permute-done.16 = bf16[4,208,128]{1,2,0:T(8,128)(2,1)S(1)} collective-permute-done((bf16[4,208,128]{1,2,0:T(8,128)(2,1)S(1)}, bf16[4,208,128]{1,2,0:T(8,128)(2,1)S(1)}, u32[]{:S(2)}, u32[]{:S(2)}) %collective-permute-start.16) | collective-permute-done | bytes 213024 | tf_op jit(solution)/shard_map/ppermute | solution.py:43
  91.2 6.4 %collective-permute-done.18 = bf16[4,208,128]{1,2,0:T(8,128)(2,1)S(1)} collective-permute-done((bf16[4,208,128]{1,2,0:T(8,128)(2,1)S(1)}, bf16[4,208,128]{1,2,0:T(8,128)(2,1)S(1)}, u32[]{:S(2)}, u32[]{:S(2)}) %collective-permute-start.18) | collective-permute-done | bytes 213024 | tf_op jit(solution)/shard_map/ppermute | solution.py:43
  98.4 2.8 %collective-permute-start.19 = (bf16[16,208,128]{2,1,0:T(8,128)(2,1)S(1)}, bf16[16,208,128]{2,1,0:T(8,128)(2,1)S(1)}, u32[]{:S(2)}, u32[]{:S(2)}) collective-permute-start(bf16[16,208,128]{2,1,0:T(8,128)(2,1)S(1)} %bitcast.61), channel_id=1, source_target_pairs={{0,8},{8,0},{16,24},{24,16},{32,40},{40,32},{48,56},{56,48},{64,72... | collective-permute-start | bytes 2555912 | tf_op jit(solution)/shard_map/ppermute | solution.py:43
  102.6 2.4 %collective-permute-done.20 = bf16[192,128]{0,1:T(8,128)(2,1)S(1)} collective-permute-done((bf16[192,128]{0,1:T(8,128)(2,1)}, bf16[192,128]{0,1:T(8,128)(2,1)S(1)}, u32[]{:S(2)}, u32[]{:S(2)}) %collective-permute-start.20) | collective-permute-done | bytes 49184 | tf_op jit(solution)/shard_map/ppermute | solution.py:43
  110.7 4.1 %collective-permute-done.23 = bf16[2,192,128]{1,2,0:T(8,128)(2,1)S(1)} collective-permute-done((bf16[2,192,128]{1,2,0:T(8,128)(2,1)S(1)}, bf16[2,192,128]{1,2,0:T(8,128)(2,1)S(1)}, u32[]{:S(2)}, u32[]{:S(2)}) %collective-permute-start.23) | collective-permute-done | bytes 98336 | tf_op jit(solution)/shard_map/ppermute | solution.py:43
  117.1 3.0 %weights_g.1 = (f32[8,192,128]{2,1,0:T(8,128)}, f32[192,1]{1,0:T(8,128)S(1)}) custom-call(s32[5]{0:T(128)S(1)} %stack.151.refs_0_, bf16[16,208,128]{2,1,0:T(8,128)(2,1)S(1)} %bitcast.62, bf16[16,208,128]{2,1,0:T(8,128)(2,1)S(1)} %collective-permute-done.19.refs_2_, bf16[8,192,128]{2,1,0:T(8,128)(2,1)S(1)} %bitcast.67, bf16[192,768]{1,0:T(8,128)(2,1)S(1)} %copy-done, ...), custom_call_target="tpu_custom_call" | custom-call | tf_op jit(solution)/shard_map/weights_g/pallas_call | solution.py:144
  120.2 3.6 %all-to-all-start.2 = ((f32[8,192,128]{2,1,0:T(8,128)}), f32[8,192,128]{2,1,0:T(8,128)S(1)}, u32[]{:S(2)}, u32[]{:S(2)}) async-start(f32[8,192,128]{2,1,0:T(8,128)} %get-tuple-element.6), calls=%async_computation.2 | async-start | bytes 1572864 | tf_op jit(solution)/shard_map/all_to_all | solution.py:232
  124.0 8.6 %all-to-all-done.2 = f32[8,192,128]{2,1,0:T(8,128)S(1)} async-done(((f32[8,192,128]{2,1,0:T(8,128)}), f32[8,192,128]{2,1,0:T(8,128)S(1)}, u32[]{:S(2)}, u32[]{:S(2)}) %all-to-all-start.2) | async-done | bytes 786464 | tf_op jit(solution)/shard_map/all_to_all | solution.py:232
  133.8 10.9 %all-to-all-start.3 = ((f32[32,1,384]{2,1,0:T(1,128)}), f32[32,1,384]{2,1,0:T(1,128)S(1)}, u32[]{:S(2)}, u32[]{:S(2)}) async-start(f32[32,1,384]{2,1,0:T(1,128)} %reshape.103), calls=%async_computation.3 | async-start | bytes 98304 | tf_op jit(solution)/shard_map/all_to_all | solution.py:236
  146.4 8.1 %all-to-all-done.3 = f32[32,1,384]{2,1,0:T(1,128)S(1)} async-done(((f32[32,1,384]{2,1,0:T(1,128)}), f32[32,1,384]{2,1,0:T(1,128)S(1)}, u32[]{:S(2)}, u32[]{:S(2)}) %all-to-all-start.3) | async-done | bytes 49184 | tf_op jit(solution)/shard_map/all_to_all | solution.py:236
  (121 shorter events, 39.1 us)
Async XLA Ops:
  2.2 36.9 %collective-permute-start = (bf16[192,128]{0,1:T(8,128)(2,1)S(1)}, bf16[192,128]{0,1:T(8,128)(2,1)S(1)}, u32[]{:S(2)}, u32[]{:S(2)}) collective-permute-start(bf16[192,128]{0,1:T(8,128)(2,1)S(1)} %constant_dynamic-update-slice_fusion), channel_id=1, source_target_pairs={{0,0},{1,8},{2,16},{3,24},{4,32},{5,40},{6,48},{7,56},{8,64},{9,72... | collective-permute-start | bytes 147464 | tf_op jit(solution)/shard_map/ppermute | solution.py:63
  14.7 28.5 %collective-permute-start.8 = (bf16[208,128]{0,1:T(8,128)(2,1)S(1)}, bf16[208,128]{0,1:T(8,128)(2,1)S(1)}, u32[]{:S(2)}, u32[]{:S(2)}) collective-permute-start(bf16[208,128]{0,1:T(8,128)(2,1)S(1)} %concatenate.19), channel_id=1, source_target_pairs={{0,4},{1,5},{2,6},{3,7},{4,0},{5,1},{6,2},{7,3},{8,12},{9,13},{10,... | collective-permute-start | bytes 159752 | tf_op jit(solution)/shard_map/ppermute | solution.py:43
  19.6 19.2 %all-to-all-start.1 = ((bf16[32,2,192]{2,1,0:T(2,128)(2,1)}), bf16[32,2,192]{2,1,0:T(2,128)(2,1)S(1)}, u32[]{:S(2)}, u32[]{:S(2)}) async-start(bf16[32,2,192]{2,1,0:T(2,128)(2,1)} %reshape.101), calls=%async_computation.1 | async-start | bytes 65536 | tf_op jit(solution)/shard_map/all_to_all | solution.py:215
  39.6 8.0 %collective-permute-start.2 = (bf16[192,128]{0,1:T(8,128)(2,1)S(1)}, bf16[192,128]{0,1:T(8,128)(2,1)S(1)}, u32[]{:S(2)}, u32[]{:S(2)}) collective-permute-start(bf16[192,128]{0,1:T(8,128)(2,1)S(1)} %collective-permute-done), channel_id=1, source_target_pairs={{0,192},{8,200},{16,208},{24,216},{32,224},{40,232},{48,240},{56,2... | collective-permute-start | bytes 147464 | tf_op jit(solution)/shard_map/ppermute | solution.py:43
  42.8 7.4 %collective-permute-start.3 = (bf16[192,128]{0,1:T(8,128)(2,1)S(1)}, bf16[192,128]{0,1:T(8,128)(2,1)S(1)}, u32[]{:S(2)}, u32[]{:S(2)}) collective-permute-start(bf16[192,128]{0,1:T(8,128)(2,1)S(1)} %collective-permute-done), channel_id=1, source_target_pairs={{0,128},{8,136},{16,144},{24,152},{32,160},{40,168},{48,176},{56,1... | collective-permute-start | bytes 147464 | tf_op jit(solution)/shard_map/ppermute | solution.py:43
  43.2 9.8 %collective-permute-start.9 = (bf16[2,208,128]{1,2,0:T(8,128)(2,1)S(1)}, bf16[2,208,128]{1,2,0:T(8,128)(2,1)S(1)}, u32[]{:S(2)}, u32[]{:S(2)}) collective-permute-start(bf16[2,208,128]{1,2,0:T(8,128)(2,1)S(1)} %get-tuple-element.31), channel_id=1, source_target_pairs={{0,1},{1,2},{2,3},{3,0},{4,5},{5,6},{6,7},{7,4},{8,9},{9,10},{10,1... | collective-permute-start | bytes 319496 | tf_op jit(solution)/shard_map/ppermute | solution.py:43
  43.3 10.3 %collective-permute-start.10 = (bf16[2,208,128]{1,2,0:T(8,128)(2,1)S(1)}, bf16[2,208,128]{1,2,0:T(8,128)(2,1)S(1)}, u32[]{:S(2)}, u32[]{:S(2)}) collective-permute-start(bf16[2,208,128]{1,2,0:T(8,128)(2,1)S(1)} %get-tuple-element.31), channel_id=1, source_target_pairs={{0,3},{1,0},{2,1},{3,2},{4,7},{5,4},{6,5},{7,6},{8,11},{9,8},{10,9... | collective-permute-start | bytes 319496 | tf_op jit(solution)/shard_map/ppermute | solution.py:43
  46.0 11.0 %collective-permute-start.11 = (bf16[2,208,128]{1,2,0:T(8,128)(2,1)S(1)}, bf16[2,208,128]{1,2,0:T(8,128)(2,1)S(1)}, u32[]{:S(2)}, u32[]{:S(2)}) collective-permute-start(bf16[2,208,128]{1,2,0:T(8,128)(2,1)S(1)} %get-tuple-element.31), channel_id=1, source_target_pairs={{0,2},{1,3},{2,0},{3,1},{4,6},{5,7},{6,4},{7,5},{8,10},{9,11},{10,... | collective-permute-start | bytes 319496 | tf_op jit(solution)/shard_map/ppermute | solution.py:43
  50.3 7.1 %collective-permute-start.4 = (bf16[4,192,128]{1,2,0:T(8,128)(2,1)S(1)}, bf16[4,192,128]{1,2,0:T(8,128)(2,1)S(1)}, u32[]{:S(2)}, u32[]{:S(2)}) collective-permute-start(bf16[4,192,128]{1,2,0:T(8,128)(2,1)S(1)} %get-tuple-element.25), channel_id=1, source_target_pairs={{0,16},{8,24},{16,32},{24,40},{32,48},{40,56},{48,0},{56,8},{64,80... | collective-permute-start | bytes 589832 | tf_op jit(solution)/shard_map/ppermute | solution.py:43
  50.6 7.8 %collective-permute-start.5 = (bf16[4,192,128]{1,2,0:T(8,128)(2,1)S(1)}, bf16[4,192,128]{1,2,0:T(8,128)(2,1)S(1)}, u32[]{:S(2)}, u32[]{:S(2)}) collective-permute-start(bf16[4,192,128]{1,2,0:T(8,128)(2,1)S(1)} %get-tuple-element.25), channel_id=1, source_target_pairs={{0,48},{8,56},{16,0},{24,8},{32,16},{40,24},{48,32},{56,40},{64,11... | collective-permute-start | bytes 589832 | tf_op jit(solution)/shard_map/ppermute | solution.py:43
  53.0 9.8 %collective-permute-start.6 = (bf16[4,192,128]{1,2,0:T(8,128)(2,1)S(1)}, bf16[4,192,128]{1,2,0:T(8,128)(2,1)S(1)}, u32[]{:S(2)}, u32[]{:S(2)}) collective-permute-start(bf16[4,192,128]{1,2,0:T(8,128)(2,1)S(1)} %get-tuple-element.25), channel_id=1, source_target_pairs={{0,32},{8,40},{16,48},{24,56},{32,0},{40,8},{48,16},{56,24},{64,96... | collective-permute-start | bytes 589832 | tf_op jit(solution)/shard_map/ppermute | solution.py:43
  53.7 15.6 %collective-permute-start.12 = (bf16[192,128]{0,1:T(8,128)(2,1)}, bf16[192,128]{0,1:T(8,128)(2,1)}, u32[]{:S(2)}, u32[]{:S(2)}) collective-permute-start(bf16[192,128]{0,1:T(8,128)(2,1)} %get-tuple-element.35), channel_id=1, source_target_pairs={{0,0},{1,8},{2,16},{3,24},{4,32},{5,40},{6,48},{7,56},{8,64},{9,72... | collective-permute-start | bytes 147464 | tf_op jit(solution)/shard_map/ppermute | solution.py:63
  63.8 10.3 %collective-permute-start.7 = (bf16[16,192,128]{2,1,0:T(8,128)(2,1)S(1)}, bf16[16,192,128]{2,1,0:T(8,128)(2,1)S(1)}, u32[]{:S(2)}, u32[]{:S(2)}) collective-permute-start(bf16[16,192,128]{2,1,0:T(8,128)(2,1)S(1)} %bitcast.63), channel_id=1, source_target_pairs={{0,8},{8,0},{16,24},{24,16},{32,40},{40,32},{48,56},{56,48},{64,72... | collective-permute-start | bytes 2359304 | tf_op jit(solution)/shard_map/ppermute | solution.py:43
  70.2 12.4 %collective-permute-start.13 = (bf16[208,128]{0,1:T(8,128)(2,1)S(1)}, bf16[208,128]{0,1:T(8,128)(2,1)S(1)}, u32[]{:S(2)}, u32[]{:S(2)}) collective-permute-start(bf16[208,128]{0,1:T(8,128)(2,1)S(1)} %concatenate.21), channel_id=1, source_target_pairs={{0,64},{8,72},{16,80},{24,88},{32,96},{40,104},{48,112},{56,120},{... | collective-permute-start | bytes 159752 | tf_op jit(solution)/shard_map/ppermute | solution.py:43
  70.5 12.1 %collective-permute-start.14 = (bf16[208,128]{0,1:T(8,128)(2,1)S(1)}, bf16[208,128]{0,1:T(8,128)(2,1)S(1)}, u32[]{:S(2)}, u32[]{:S(2)}) collective-permute-start(bf16[208,128]{0,1:T(8,128)(2,1)S(1)} %concatenate.21), channel_id=1, source_target_pairs={{0,192},{8,200},{16,208},{24,216},{32,224},{40,232},{48,240},{56,2... | collective-permute-start | bytes 159752 | tf_op jit(solution)/shard_map/ppermute | solution.py:43
  74.1 8.8 %collective-permute-start.15 = (bf16[208,128]{0,1:T(8,128)(2,1)S(1)}, bf16[208,128]{0,1:T(8,128)(2,1)S(1)}, u32[]{:S(2)}, u32[]{:S(2)}) collective-permute-start(bf16[208,128]{0,1:T(8,128)(2,1)S(1)} %concatenate.21), channel_id=1, source_target_pairs={{0,128},{8,136},{16,144},{24,152},{32,160},{40,168},{48,176},{56,1... | collective-permute-start | bytes 159752 | tf_op jit(solution)/shard_map/ppermute | solution.py:43
  77.4 42.7 %all-to-all-start = ((f32[8,192,128]{2,1,0:T(8,128)}), f32[8,192,128]{2,1,0:T(8,128)S(1)}, u32[]{:S(2)}, u32[]{:S(2)}) async-start(f32[8,192,128]{2,1,0:T(8,128)} %weights_q.1), calls=%async_computation | async-start | bytes 1572864 | tf_op jit(solution)/shard_map/all_to_all | solution.py:233
  83.0 7.9 %collective-permute-start.16 = (bf16[4,208,128]{1,2,0:T(8,128)(2,1)S(1)}, bf16[4,208,128]{1,2,0:T(8,128)(2,1)S(1)}, u32[]{:S(2)}, u32[]{:S(2)}) collective-permute-start(bf16[4,208,128]{1,2,0:T(8,128)(2,1)S(1)} %get-tuple-element.27), channel_id=1, source_target_pairs={{0,16},{8,24},{16,32},{24,40},{32,48},{40,56},{48,0},{56,8},{64,80... | collective-permute-start | bytes 638984 | tf_op jit(solution)/shard_map/ppermute | solution.py:43
  84.1 7.1 %collective-permute-start.17 = (bf16[4,208,128]{1,2,0:T(8,128)(2,1)S(1)}, bf16[4,208,128]{1,2,0:T(8,128)(2,1)S(1)}, u32[]{:S(2)}, u32[]{:S(2)}) collective-permute-start(bf16[4,208,128]{1,2,0:T(8,128)(2,1)S(1)} %get-tuple-element.27), channel_id=1, source_target_pairs={{0,48},{8,56},{16,0},{24,8},{32,16},{40,24},{48,32},{56,40},{64,11... | collective-permute-start | bytes 638984 | tf_op jit(solution)/shard_map/ppermute | solution.py:43
  86.2 11.3 %collective-permute-start.18 = (bf16[4,208,128]{1,2,0:T(8,128)(2,1)S(1)}, bf16[4,208,128]{1,2,0:T(8,128)(2,1)S(1)}, u32[]{:S(2)}, u32[]{:S(2)}) collective-permute-start(bf16[4,208,128]{1,2,0:T(8,128)(2,1)S(1)} %get-tuple-element.27), channel_id=1, source_target_pairs={{0,32},{8,40},{16,48},{24,56},{32,0},{40,8},{48,16},{56,24},{64,96... | collective-permute-start | bytes 638984 | tf_op jit(solution)/shard_map/ppermute | solution.py:43
  98.4 18.7 %collective-permute-start.19 = (bf16[16,208,128]{2,1,0:T(8,128)(2,1)S(1)}, bf16[16,208,128]{2,1,0:T(8,128)(2,1)S(1)}, u32[]{:S(2)}, u32[]{:S(2)}) collective-permute-start(bf16[16,208,128]{2,1,0:T(8,128)(2,1)S(1)} %bitcast.61), channel_id=1, source_target_pairs={{0,8},{8,0},{16,24},{24,16},{32,40},{40,32},{48,56},{56,48},{64,72... | collective-permute-start | bytes 2555912 | tf_op jit(solution)/shard_map/ppermute | solution.py:43
  107.9 7.0 %collective-permute-start.23 = (bf16[2,192,128]{1,2,0:T(8,128)(2,1)S(1)}, bf16[2,192,128]{1,2,0:T(8,128)(2,1)S(1)}, u32[]{:S(2)}, u32[]{:S(2)}) collective-permute-start(bf16[2,192,128]{1,2,0:T(8,128)(2,1)S(1)} %get-tuple-element.29), channel_id=1, source_target_pairs={{0,2},{1,3},{2,0},{3,1},{4,6},{5,7},{6,4},{7,5},{8,10},{9,11},{10,... | collective-permute-start | bytes 294920 | tf_op jit(solution)/shard_map/ppermute | solution.py:43
  120.2 12.4 %all-to-all-start.2 = ((f32[8,192,128]{2,1,0:T(8,128)}), f32[8,192,128]{2,1,0:T(8,128)S(1)}, u32[]{:S(2)}, u32[]{:S(2)}) async-start(f32[8,192,128]{2,1,0:T(8,128)} %get-tuple-element.6), calls=%async_computation.2 | async-start | bytes 1572864 | tf_op jit(solution)/shard_map/all_to_all | solution.py:232
  133.8 20.7 %all-to-all-start.3 = ((f32[32,1,384]{2,1,0:T(1,128)}), f32[32,1,384]{2,1,0:T(1,128)S(1)}, u32[]{:S(2)}, u32[]{:S(2)}) async-start(f32[32,1,384]{2,1,0:T(1,128)} %reshape.103), calls=%async_computation.3 | async-start | bytes 98304 | tf_op jit(solution)/shard_map/all_to_all | solution.py:236
  (10 other events, 123.4 us)

commit v3 on v0

v3 whole, which is shorter than its diff:
```python
import jax
import jax.numpy as jnp
from jax import lax
from jax.experimental import pallas as pl
from jax.experimental.pallas import tpu as pltpu
from jax.sharding import PartitionSpec as P

shift_value = 2.0
penalty = 2.5
both = ("row", "col")
f32 = jnp.float32
bf16 = jnp.bfloat16
i32 = jnp.int32
lanes = 128
half = 64
group = 8
extra = 16
vmem = pl.BlockSpec(memory_space=pltpu.VMEM)
hbm = pl.BlockSpec(memory_space=pltpu.MemorySpace.HBM)
smem = pl.BlockSpec(memory_space=pltpu.SMEM)


z_hi, x_axis, core = ("row", 8, 4), ("row", 2, 4), ("row", 1, 2)
z_lo, y_axis = ("col", 4, 2), ("col", 1, 4)
offsets = (0, -1, 1, 2)


def digit(axis):
    name, stride, length = axis
    return lax.axis_index(name) // stride % length


def turn(x, axis, step):
    name, stride, length = axis
    pairs = []
    for i in range(lax.axis_size(name)):
        d = i // stride % length
        pairs.append((i, i + ((d + step) % length - d) * stride))
    return lax.ppermute(x, name, pairs)


def gather_digit(x, axis):
    return jnp.stack([x] + [turn(x, axis, -offset) for offset in offsets[1:]])


def gather_cols(x):
    two = jnp.stack([x, turn(x, z_lo, 1)])
    return [two] + [turn(two, y_axis, -offset) for offset in offsets[1:]]


def to_column(x, rows, cols, per):
    pairs = []
    for r in range(rows):
        for c in range(cols):
            pairs.append((r * cols + c, ((r % per) * cols + c) * cols + r // per))
    return lax.ppermute(x, both, pairs)


def iota(shape, axis):
    return lax.broadcasted_iota(i32, shape, axis)


def column_of(row, n):
    return jnp.sum(jnp.where(iota((n, n), 0) == iota((n, n), 1), row, 0), axis=1, keepdims=True)


def row_of(column, n):
    return jnp.sum(jnp.where(iota((n, n), 0) == iota((n, n), 1), column, 0), axis=0, keepdims=True)


def over_block(x):
    return ((x >> 6) * 21846) >> 16


def one_hot(condition, dtype=bf16):
    return jnp.where(condition, 1.0, 0.0).astype(dtype)


def transposed_dot(left, right):
    return lax.dot_general(left, right, (((1,), (1,)), ((), ())), preferred_element_type=f32)


def exact_dot(left, right):
    return jnp.dot(left, right, precision=lax.Precision.HIGHEST, preferred_element_type=f32)


def three_parts(value):
    pieces = []
    for _ in range(3):
        piece = value.astype(bf16).astype(f32)
        pieces.append(piece)
        value = value - piece
    return pieces


def block_of(perm, b, n):
    at = lax.div(b * n, lanes)
    two = jnp.concatenate([perm[pl.ds(at, 1), :], perm[pl.ds(at + 1, 1), :]], axis=1)
    return jnp.where(b * n == at * lanes, two[:, :n], two[:, lanes // 2 : lanes // 2 + n])


def rank_in_block(mine, n):
    column = column_of(mine, n)
    source = over_block(column)
    earlier = (over_block(mine) == source) & (iota((n, n), 1) < iota((n, n), 0))
    return column, source, jnp.sum(jnp.where(earlier, 1, 0), axis=1, keepdims=True)


def routes_kernel(
    place,
    perm,
    lengths,
    density_far,
    hole_far,
    ph_far,
    multiplier_far,
    leaving,
    local,
    send,
    receive,
    receive_across,
    segments,
    ph_segments,
    density,
    hole,
    ph,
    multiplier,
    sems,
):
    fars = (density_far, hole_far, ph_far, multiplier_far)
    copies = [
        pltpu.make_async_copy(far, here, sems.at[i])
        for i, (far, here) in enumerate(zip(fars, (density, hole, ph, multiplier)))
    ]
    for copy in copies:
        copy.start()
    part, block = density.shape
    width = multiplier.shape[1]
    padded = receive_across.shape[0]
    rows = padded // group
    r, c = place[3], place[4]
    square = (block, block)
    ids = r * block + iota((block, 1), 0)
    target = jnp.zeros((block, lanes), i32)
    for g in range(perm.shape[0]):
        target = target + jnp.where(
            perm[g : g + 1, :] == ids, iota((block, lanes), 1) + g * lanes, 0
        )
    target = jnp.sum(target, axis=1, keepdims=True)
    target_row = row_of(target, block)
    spot = jnp.sum(jnp.where(target < target_row, 1, 0), axis=0, keepdims=True)
    spot = spot + (group - block // rows) * over_block(target_row)
    send[...] = one_hot(iota((block, padded), 1) == column_of(spot, block))

    mine_column, source, rank = rank_in_block(block_of(perm, r, block), block)
    slot = source * group + rank
    receive[...] = one_hot(iota((block, padded), 1) == slot)
    receive_across[...] = one_hot(iota((padded, block), 0) == row_of(slot, block))

    for copy in copies:
        copy.wait()
    eye = one_hot(iota(square, 0) == iota(square, 1))
    blank = jnp.zeros((lanes - part, block), bf16)
    pair = transposed_dot(eye, jnp.concatenate([density[...], hole[...]], axis=0))
    tail = transposed_dot(eye, jnp.concatenate([blank, ph[...]], axis=0))
    local[0] = pair.astype(bf16)
    local[1] = tail.astype(bf16)
    gone = transposed_dot(
        one_hot(iota((padded, block), 0) == spot), jnp.concatenate([density[...], blank], axis=0)
    )

    sizes = jnp.concatenate(
        [lengths[...].astype(f32), jnp.zeros((1, lanes - lengths.shape[1]), f32)], axis=1
    )
    upper = one_hot(iota((lanes, lanes), 0) <= iota((lanes, lanes), 1))
    ends = jnp.dot(
        jnp.broadcast_to(sizes, (8, lanes)).astype(bf16), upper, preferred_element_type=f32
    )[0:1]
    starts = ends - sizes
    positions = ids.astype(f32)
    ph_positions = mine_column.astype(f32)
    inside = one_hot((positions >= starts) & (positions < ends), f32)
    ph_inside = one_hot((ph_positions >= starts) & (ph_positions < ends), f32)
    segments[...] = inside
    ph_segments[...] = ph_inside
    first = iota((block, lanes), 1) < half
    density_sq = jnp.sum(jnp.where(first, pair * pair, 0.0), axis=1, keepdims=True)
    on_diag = iota((block, width), 0) + (r * block - c * width) == iota((block, width), 1)
    share = jnp.sum(jnp.where(on_diag, multiplier[...].astype(f32), 0.0), axis=1, keepdims=True)
    share = share - penalty * jnp.sum(tail * tail, axis=1, keepdims=True)
    pieces = three_parts(jnp.sum(inside * density_sq, axis=0, keepdims=True)) + three_parts(
        jnp.sum(ph_inside * share, axis=0, keepdims=True)
    )
    at = iota((padded, lanes), 0) & (group - 1)
    late = iota((padded, lanes), 1) >= half
    for row, piece in enumerate(pieces):
        gone = jnp.where((at == row) & late, pltpu.roll(piece, half, 1), gone)
    leaving[...] = gone.astype(bf16)


def rows_kernel(incoming, receive, local, body, longer):
    block = local.shape[1]
    values = jnp.dot(receive[...], incoming[...], preferred_element_type=f32)
    values = jnp.where(iota(values.shape, 1) < half, values, local[1].astype(f32)).astype(bf16)
    sums = jnp.zeros((group, lanes), f32)
    arrived = incoming[...].astype(f32)
    for g in range(arrived.shape[0] // group):
        sums = sums + arrived[g * group : (g + 1) * group]
    sums = pltpu.roll(sums, half, 1)
    at = iota((extra, lanes), 0)
    tile = jnp.zeros((extra, lanes), f32)
    for k in range(2):
        value = sums[3 * k : 3 * k + 1] + sums[3 * k + 1 : 3 * k + 2] + sums[3 * k + 2 : 3 * k + 3]
        for i, piece in enumerate(three_parts(value)):
            tile = jnp.where(at == 3 * k + i, piece, tile)
    for out in (body, longer):
        out[:block] = local[0]
        out[block : 2 * block] = values
    longer[2 * block :] = tile.astype(bf16)


def halves_side_by_side(top, bottom, first):
    low = iota(top.shape, 1) < half
    if first:
        return jnp.where(low, top, pltpu.roll(bottom, half, 1))
    return jnp.where(low, pltpu.roll(top, half, 1), bottom)


def rows_again(packed, first):
    turned = pltpu.roll(packed, half, 1)
    return jnp.concatenate([packed, turned] if first else [turned, packed], axis=0)


def sum_parts(parts):
    total = parts[0]
    for k in range(1, parts.shape[0]):
        total = total + parts[k]
    return total


def diagonal_of(place, shape):
    block, width = shape
    return iota(shape, 0) + (place[3] * block - place[4] * width) == iota(shape, 1)


def places_of(place, own, other):
    zh, xx, cc = place[0], place[1], place[2]
    for cr, source in enumerate((own, other)):
        for xr, xo in enumerate(offsets):
            from_col = ((xx + xo) & 3) * 2 + (cc if cr == 0 else 1 - cc)
            for zr, zo in enumerate(offsets):
                yield cr, xr * 4 + zr, source, from_col, (zh + zo) & 3


def column_at(place, y_place, z_place):
    return ((place[4] + offsets[y_place]) & 3) + (((place[4] >> 2) + z_place) & 1) * 4


def fill(place, own, other, around, base, right, left, by_col):
    block = left.shape[0]
    ids = []
    for cr, b, source, from_col, j in places_of(place, own, other):
        k = cr * 4 + b // 4
        right[pl.ds(pl.multiple_of(j * block, block), block), k * lanes : (k + 1) * lanes] = source[
            b, base : base + block, :
        ]
        if b % 4 == 0:
            ids.append(from_col)
    for y_place, source in enumerate(around):
        for z_place in range(2):
            by_col[column_at(place, y_place, z_place)] = source[z_place, base : base + block]
    for k, from_col in enumerate(ids):
        left[:, k * lanes : (k + 1) * lanes] = by_col[from_col]
    return ids


def g_kernel(
    place, own, other, a0, a1, a2, a3, multiplier, segments, ph_segments, lengths,
    out, more, scale, right, left, by_col,
):
    block, width = multiplier.shape
    around = (a0, a1, a2, a3)
    ids = fill(place, own, other, around, block, right, left, by_col)
    sums = jnp.zeros((extra, lanes), f32)
    for source in around:
        for z_place in range(2):
            sums = sums + source[z_place, 2 * block :].astype(f32)
    blank = jnp.ones((1, lanes - lengths.shape[1]), f32)
    sizes = jnp.concatenate([lengths[...].astype(f32), blank], axis=1)
    mean_d = (sums[0:1] + sums[1:2] + sums[2:3]) / sizes
    mean_u = (sums[3:4] + sums[4:5] + sums[5:6]) / sizes
    shifts = jnp.sum(ph_segments[...] * (2.0 * mean_d), axis=1, keepdims=True)
    scale[...] = jnp.sum(
        segments[...] * (2.0 * (mean_u + penalty * mean_d)), axis=1, keepdims=True
    )
    gram = transposed_dot(left[...], right[...])
    resid = jnp.where(diagonal_of(place, multiplier.shape), shifts, 0.0) - gram
    weight = (multiplier[...].astype(f32) + penalty * resid).astype(bf16)
    term = -2.0 * jnp.dot(weight, right[...], preferred_element_type=f32)
    for k, from_col in enumerate(ids):
        top = term[: block // 2, k * lanes : (k + 1) * lanes]
        bottom = term[block // 2 :, k * lanes : (k + 1) * lanes]
        out[from_col] = halves_side_by_side(top, bottom, True)
        more[from_col] = halves_side_by_side(top, bottom, False)


def q_kernel(
    place, own, other, a0, a1, a2, a3, multiplier, hamiltonian, more,
    keep, away, right, left, by_col, by_col_out,
):
    block, width = multiplier.shape
    ids = fill(place, own, other, (a0, a1, a2, a3), 0, right, left, by_col)
    gram = transposed_dot(left[...], right[...])
    resid = jnp.where(diagonal_of(place, multiplier.shape), shift_value, 0.0) - gram
    weight = (multiplier[...].astype(f32) + penalty * resid).astype(bf16)
    term = -2.0 * jnp.dot(weight, right[...], preferred_element_type=f32)
    energy = 2.0 * jnp.dot(hamiltonian[...], right[...], preferred_element_type=f32)
    term = term + jnp.where((iota(energy.shape, 1) & (lanes - 1)) < half, energy, 0.0)
    for k, from_col in enumerate(ids):
        by_col_out[from_col] = term[:, k * lanes : (k + 1) * lanes]
    for z_place, out in enumerate((keep, away)):
        for y_place in range(4):
            from_col = column_at(place, y_place, z_place)
            out[y_place, :block, :] = by_col_out[from_col]
            out[y_place, block:, :] = more[from_col]


def back_kernel(parts, receive_across, back):
    total = rows_again(sum_parts(parts), True)
    back[...] = exact_dot(receive_across[...].astype(f32), total)


def add_kernel(keep, came, *outs):
    for k, out in enumerate(outs):
        out[...] = keep[k] + came[k]


def last_kernel(p0, p1, p2, p3, returned, send, local, scale, density, hole, ph):
    block = local.shape[1]
    total = p0[...] + p1[...] + p2[...] + p3[...]
    ph[...] = rows_again(total[block:], False).T[half:]
    total = total[:block]
    more = exact_dot(send[...].astype(f32), returned[...])
    more = more + 2.0 * scale[...] * local[0].astype(f32)
    total = jnp.where(iota(total.shape, 1) < half, total + more, total).T
    density[...] = total[:half]
    hole[...] = total[half:]


def call(kernel, name, shapes, args, scratch=(), scalars=True, far=(), copies=0, room=8):
    return pl.pallas_call(
        kernel,
        out_shape=[jax.ShapeDtypeStruct(s, d) for s, d in shapes],
        in_specs=[smem] * scalars
        + [hbm if i in far else vmem for i in range(scalars, len(args))],
        out_specs=[vmem] * len(shapes),
        scratch_shapes=[pltpu.VMEM(s, d) for s, d in scratch]
        + [pltpu.SemaphoreType.DMA((copies,))] * (copies > 0),
        compiler_params=pltpu.CompilerParams(vmem_limit_bytes=room * 1024 * 1024),
        name=name,
    )(*args)


def local(
    density_factor,
    hole_factor,
    ph_factor,
    hamiltonian,
    multiplier_q,
    multiplier_g,
    ph_perm,
    block_lengths,
):
    rows, cols = lax.axis_size("row"), lax.axis_size("col")
    block, part = density_factor.shape
    width = multiplier_q.shape[1]
    per = width // block
    padded = rows * group
    place = jnp.stack(
        [digit(axis) for axis in (z_hi, x_axis, core)]
        + [lax.axis_index("row"), lax.axis_index("col")]
    ).astype(i32)
    lengths = block_lengths[None, :]
    perm = ph_perm.reshape(-1, lanes)
    leaving, mine, send, receive, receive_across, segments, ph_segments = call(
        routes_kernel,
        "routes",
        [
            ((padded, lanes), bf16),
            ((2, block, lanes), bf16),
            ((block, padded), bf16),
            ((block, padded), bf16),
            ((padded, block), bf16),
            ((block, lanes), f32),
            ((block, lanes), f32),
        ],
        (place, perm, lengths, density_factor.T, hole_factor.T, ph_factor.T, multiplier_g),
        [((part, block), bf16)] * 3 + [((block, width), bf16)],
        far=(3, 4, 5, 6),
        copies=4,
        room=60,
    )
    incoming = lax.all_to_all(leaving.reshape(rows, group, lanes), "row", 0, 0)
    tall = 2 * block
    body, longer = call(
        rows_kernel,
        "rows",
        [((tall, lanes), bf16), ((tall + extra, lanes), bf16)],
        (incoming.reshape(padded, lanes), receive, mine),
        scalars=False,
    )
    piece = to_column(body, rows, cols, per)
    near = gather_digit(piece, z_hi)
    own = gather_digit(near, x_axis).reshape(16, tall, lanes)
    around = gather_cols(longer)
    own, around = lax.optimization_barrier((own, around))
    other = turn(own, core, 1)
    gathered = (place, own, other, *around)
    shared = [
        ((width, cols * lanes), bf16),
        ((block, cols * lanes), bf16),
        ((cols, block, lanes), bf16),
    ]
    parts_e, parts_f, scale = call(
        g_kernel,
        "weights_g",
        [((cols, block // 2, lanes), f32), ((cols, block // 2, lanes), f32), ((block, 1), f32)],
        (*gathered, multiplier_g, segments, ph_segments, lengths),
        shared,
        room=16,
    )
    long = block + block // 2
    keep, away = call(
        q_kernel,
        "weights_q",
        [((4, long, lanes), f32)] * 2,
        (*gathered, multiplier_q, hamiltonian, parts_f),
        shared + [((cols, block, lanes), f32)],
        room=16,
    )
    parts_e, keep, away = lax.optimization_barrier((parts_e, keep, away))
    sums_e = lax.all_to_all(parts_e, "col", 0, 0)
    came = turn(away, z_lo, 1)
    (back,) = call(
        back_kernel, "back", [((padded, lanes), f32)], (sums_e, receive_across), scalars=False
    )
    returned = lax.all_to_all(back.reshape(rows, group, lanes), "row", 0, 0)
    parts = call(add_kernel, "add", [((long, lanes), f32)] * 4, (keep, came), scalars=False)
    parts = [parts[0]] + [turn(p, y_axis, o) for p, o in zip(parts[1:], offsets[1:])]
    grads = call(
        last_kernel,
        "gradients",
        [((part, block), f32)] * 3,
        (*parts, returned.reshape(padded, lanes), send, mine, scale),
        scalars=False,
    )
    return tuple(g.T for g in grads)


def solution(mesh):
    return jax.shard_map(
        local,
        mesh=mesh,
        in_specs=(
            P("row", "col"),
            P("row", "col"),
            P("row", "col"),
            P("row", "col"),
            P("row", "col"),
            P("row", "col"),
            P(),
            P(),
        ),
        out_specs=(P("row", "col"), P("row", "col"), P("row", "col")),
        check_vma=False,
    )
```

time: 628 us -> 126 us (0.20)
  waiting for transfers between devices: 434 us -> 42.1 us
  local copies, waits for them, and re-layouts: 101 us -> 2.5 us
  starting transfers between devices: 20.1 us -> 49.3 us
  other arithmetic: 22.5 us -> 0.29 us
  matrix products: 14.6 us -> 0 us
  between operations: 15.3 us -> 0.87 us
  Pallas kernels: 0 us -> 10.8 us
    unnamed x8 -> x0, waiting for transfers between devices: 240 us -> none
    all_gather x5 -> x0, waiting for transfers between devices: 137 us -> none  [the longest x1 49.3 us: local(): lax.all_gather(ph_local, 'row', axis=0, tiled=True)]
    gather x10 -> x0, local copies, waits for them, and re-layouts: 67.8 us -> none  [the longest x1 34.3 us: local(): shifted_ph = jnp.take(shifted, ph_perm)]
    reduce_scatter x1 -> x0, waiting for transfers between devices: 49.3 us -> none  [local(): lax.psum_scatter(jnp.concatenate([contract_rows(pair_rows, pair_local), c...]
    ppermute x0 -> x16, waiting for transfers between devices: none -> 35.1 us  [the longest x15 29.8 us: turn(): return lax.ppermute(x, name, pairs)]
    ppermute x0 -> x16, starting transfers between devices: none -> 30.2 us  [the longest x15 23.3 us: turn(): return lax.ppermute(x, name, pairs)]
    scatter x1 -> x0, local copies, waits for them, and re-layouts: 23.2 us -> none  [local(): weight_pair = jnp.zeros_like(weight_diag).at[ph_perm].set(weight_diag)]
    psum x1 -> x0, blocking collectives: 19.3 us -> none  [local(): lax.psum((density_sq, ph_sq, mult_diag), 'col')]
  transfers between devices with their start and end apart: 9 -> 18, of which waited for: 8 -> 12; matrix products, arithmetic and copies ran while one was open for 20% -> 0% of each run, Pallas kernels for 0% -> 1%
where the time goes in v3:
time: 126 us; the launch traced here: 125 us
  starting transfers between devices  49.3 us (39%)
  waiting for transfers between devices  42.1 us (33%)
  blocking collectives  18.8 us (15%)
  Pallas kernels  10.8 us (9%)
  local copies, waits for them, and re-layouts  2.5 us (2%)
    ppermute x15, waiting for transfers between devices, turn(): return lax.ppermute(x, name, pairs)  29.8 us
    ppermute x15, starting transfers between devices, turn(): return lax.ppermute(x, name, pairs)  23.3 us
    all_to_all x1, blocking collectives, local(): incoming = lax.all_to_all(leaving.reshape(rows, group, lanes), 'row', 0, 0)  18.8 us
    pallas_call x7, Pallas kernels, call(): pl.pallas_call(kernel, out_shape=[jax.ShapeDtypeStruct(s, d) for s, d in...  10.8 us
    all_to_all x1, starting transfers between devices, local(): returned = lax.all_to_all(back.reshape(rows, group, lanes), 'row', 0, 0)  10.3 us
    all_to_all x1, starting transfers between devices, local(): sums_e = lax.all_to_all(parts_e, 'col', 0, 0)  8.83 us
    all_to_all x1, waiting for transfers between devices, local(): sums_e = lax.all_to_all(parts_e, 'col', 0, 0)  7.03 us
    ppermute x1, starting transfers between devices, to_column(): return lax.ppermute(x, both, pairs)  6.88 us
  transfers between devices with their start and end apart: 18, of which 12 were waited for; matrix products, arithmetic and copies ran while one was open for 0% of the time, Pallas kernels for 1%

profile of v3, /device:TPU:64, one launch (start us, length us, event | category | flops | bytes accessed | tf_op | source)
XLA Modules:
  0.0 124.7 jit_solution(11771533481991326984)
XLA Ops:
  1.3 3.0 %routes.1 = (bf16[256,128]{1,0:T(8,128)(2,1)}, bf16[2,192,128]{2,1,0:T(8,128)(2,1)}, bf16[192,256]{1,0:T(8,128)(2,1)}, bf16[192,256]{1,0:T(8,128)(2,1)}, bf16[25...) custom-call(s32[5]{0:T(128)} %stack.62.place, s32[48,128]{1,0:T(8,128)} %bitcast.49, s32[1,48]{1,0:T(1,128)} %bitcast.35, ...), custom_call_target="tpu_custom_call" | custom-call | tf_op jit(solution)/shard_map/routes/pallas_call | solution.py:351
  4.3 18.8 %all_to_all.15 = bf16[32,8,128]{2,1,0:T(8,128)(2,1)S(1)} all-to-all(bf16[32,8,128]{2,1,0:T(8,128)(2,1)} %bitcast.45), channel_id=1, replica_groups=mesh['row'=32,'col'=8] {'row'}, dimensions={0} | all-to-all | bytes 131072 | tf_op jit(solution)/shard_map/all_to_all | solution.py:403
  25.0 6.9 %collective-permute-start = (bf16[384,128]{1,0:T(8,128)(2,1)S(1)}, bf16[384,128]{1,0:T(8,128)(2,1)S(1)}, u32[]{:S(2)}, u32[]{:S(2)}) collective-permute-start(bf16[384,128]{1,0:T(8,128)(2,1)S(1)} %get-tuple-element.35), channel_id=1, source_target_pairs={{0,0},{1,8},{2,16},{3,24},{4,32},{5,40},{6,48},{7,56},{8,64},{9,72... | collective-permute-start | bytes 294920 | tf_op jit(solution)/shard_map/ppermute | solution.py:56
  31.9 5.3 %collective-permute-done = bf16[384,128]{1,0:T(8,128)(2,1)S(1)} collective-permute-done((bf16[384,128]{1,0:T(8,128)(2,1)S(1)}, bf16[384,128]{1,0:T(8,128)(2,1)S(1)}, u32[]{:S(2)}, u32[]{:S(2)}) %collective-permute-start) | collective-permute-done | bytes 98336 | tf_op jit(solution)/shard_map/ppermute | solution.py:56
  39.4 2.8 %collective-permute-start.1 = (bf16[384,128]{1,0:T(8,128)(2,1)S(1)}, bf16[384,128]{1,0:T(8,128)(2,1)S(1)}, u32[]{:S(2)}, u32[]{:S(2)}) collective-permute-start(bf16[384,128]{1,0:T(8,128)(2,1)S(1)} %collective-permute-done), channel_id=1, source_target_pairs={{0,64},{8,72},{16,80},{24,88},{32,96},{40,104},{48,112},{56,120},{... | collective-permute-start | bytes 294920 | tf_op jit(solution)/shard_map/ppermute | solution.py:39
  42.2 4.2 %collective-permute-done.3 = bf16[384,128]{1,0:T(8,128)(2,1)S(1)} collective-permute-done((bf16[384,128]{1,0:T(8,128)(2,1)S(1)}, bf16[384,128]{1,0:T(8,128)(2,1)S(1)}, u32[]{:S(2)}, u32[]{:S(2)}) %collective-permute-start.3) | collective-permute-done | bytes 98336 | tf_op jit(solution)/shard_map/ppermute | solution.py:39
  46.4 3.2 %collective-permute-done.2 = bf16[384,128]{1,0:T(8,128)(2,1)S(1)} collective-permute-done((bf16[384,128]{1,0:T(8,128)(2,1)S(1)}, bf16[384,128]{1,0:T(8,128)(2,1)S(1)}, u32[]{:S(2)}, u32[]{:S(2)}) %collective-permute-start.2) | collective-permute-done | bytes 98336 | tf_op jit(solution)/shard_map/ppermute | solution.py:39
  49.7 2.8 %collective-permute-start.5 = (bf16[4,384,128]{2,1,0:T(8,128)(2,1)S(1)}, bf16[4,384,128]{2,1,0:T(8,128)(2,1)S(1)}, u32[]{:S(2)}, u32[]{:S(2)}) collective-permute-start(bf16[4,384,128]{2,1,0:T(8,128)(2,1)S(1)} %get-tuple-element.62), channel_id=1, source_target_pairs={{0,48},{8,56},{16,0},{24,8},{32,16},{40,24},{48,32},{56,40},{64,11... | collective-permute-start | bytes 1179656 | tf_op jit(solution)/shard_map/ppermute | solution.py:39
  52.5 2.3 %collective-permute-start.6 = (bf16[4,384,128]{2,1,0:T(8,128)(2,1)S(1)}, bf16[4,384,128]{2,1,0:T(8,128)(2,1)S(1)}, u32[]{:S(2)}, u32[]{:S(2)}) collective-permute-start(bf16[4,384,128]{2,1,0:T(8,128)(2,1)S(1)} %get-tuple-element.62), channel_id=1, source_target_pairs={{0,32},{8,40},{16,48},{24,56},{32,0},{40,8},{48,16},{56,24},{64,96... | collective-permute-start | bytes 1179656 | tf_op jit(solution)/shard_map/ppermute | solution.py:39
  54.8 2.7 %collective-permute-start.7 = (bf16[400,128]{1,0:T(8,128)(2,1)S(1)}, bf16[400,128]{1,0:T(8,128)(2,1)S(1)}, u32[]{:S(2)}, u32[]{:S(2)}) collective-permute-start(bf16[400,128]{1,0:T(8,128)(2,1)S(1)} %get-tuple-element.36), channel_id=1, source_target_pairs={{0,4},{1,5},{2,6},{3,7},{4,0},{5,1},{6,2},{7,3},{8,12},{9,13},{10,... | collective-permute-start | bytes 307208 | tf_op jit(solution)/shard_map/ppermute | solution.py:39
  57.5 2.6 %collective-permute-done.7 = bf16[400,128]{1,0:T(8,128)(2,1)S(1)} collective-permute-done((bf16[400,128]{1,0:T(8,128)(2,1)S(1)}, bf16[400,128]{1,0:T(8,128)(2,1)S(1)}, u32[]{:S(2)}, u32[]{:S(2)}) %collective-permute-start.7) | collective-permute-done | bytes 102432 | tf_op jit(solution)/shard_map/ppermute | solution.py:39
  60.2 4.3 %collective-permute-start.10 = (bf16[2,400,128]{2,1,0:T(8,128)(2,1)S(1)}, bf16[2,400,128]{2,1,0:T(8,128)(2,1)S(1)}, u32[]{:S(2)}, u32[]{:S(2)}) collective-permute-start(bf16[2,400,128]{2,1,0:T(8,128)(2,1)S(1)} %pad_maximum_fusion.2.a0), channel_id=1, source_target_pairs={{0,2},{1,3},{2,0},{3,1},{4,6},{5,7},{6,4},{7,5},{8,10},{9,11},{10,... | collective-permute-start | bytes 614408 | tf_op jit(solution)/shard_map/ppermute | solution.py:39
  64.5 2.1 %collective-permute-done.5 = bf16[4,384,128]{2,1,0:T(8,128)(2,1)S(1)} collective-permute-done((bf16[4,384,128]{2,1,0:T(8,128)(2,1)S(1)}, bf16[4,384,128]{2,1,0:T(8,128)(2,1)S(1)}, u32[]{:S(2)}, u32[]{:S(2)}) %collective-permute-start.5) | collective-permute-done | bytes 393248 | tf_op jit(solution)/shard_map/ppermute | solution.py:39
  66.6 3.4 %collective-permute-done.4 = bf16[4,384,128]{2,1,0:T(8,128)(2,1)S(1)} collective-permute-done((bf16[4,384,128]{2,1,0:T(8,128)(2,1)S(1)}, bf16[4,384,128]{2,1,0:T(8,128)(2,1)S(1)}, u32[]{:S(2)}, u32[]{:S(2)}) %collective-permute-start.4) | collective-permute-done | bytes 393248 | tf_op jit(solution)/shard_map/ppermute | solution.py:39
  70.2 2.4 %collective-permute-done.9.a2 = bf16[2,400,128]{2,1,0:T(8,128)(2,1)S(1)} collective-permute-done((bf16[2,400,128]{2,1,0:T(8,128)(2,1)S(1)}, bf16[2,400,128]{2,1,0:T(8,128)(2,1)S(1)}, u32[]{:S(2)}, u32[]{:S(2)}) %collective-permute-start.9) | collective-permute-done | bytes 204832 | tf_op jit(solution)/shard_map/ppermute | solution.py:39
  73.6 3.4 %collective-permute-done.11.other = bf16[16,384,128]{2,1,0:T(8,128)(2,1)S(1)} collective-permute-done((bf16[16,384,128]{2,1,0:T(8,128)(2,1)S(1)}, bf16[16,384,128]{2,1,0:T(8,128)(2,1)S(1)}, u32[]{:S(2)}, u32[]{:S(2)}) %collective-permute-start.11) | collective-permute-done | bytes 1572896 | tf_op jit(solution)/shard_map/ppermute | solution.py:39
  77.0 3.0 %weights_g.1 = (f32[8,96,128]{2,1,0:T(8,128)}, f32[8,96,128]{2,1,0:T(8,128)S(1)}, f32[192,1]{1,0:T(8,128)S(1)}) custom-call(s32[5]{0:T(128)S(1)} %copy-done.10, bf16[16,384,128]{2,1,0:T(8,128)(2,1)S(1)} %bitcast.30, bf16[16,384,128]{2,1,0:T(8,128)(2,1)S(1)} %collective-permute-done.11.other, bf16[2,400,128]{2,1,0:T(8,128)(2,1)S(1)} %pad_maximum_fusion.2.a0, ...), custom_call_target="tpu_custom_call" | custom-call | tf_op jit(solution)/shard_map/weights_g/pallas_call | solution.py:351
  80.0 2.5 %weights_q.1 = (f32[4,288,128]{2,1,0:T(8,128)S(1)}, f32[4,288,128]{2,1,0:T(8,128)S(1)}) custom-call(s32[5]{0:T(128)S(1)} %copy-done.10, bf16[16,384,128]{2,1,0:T(8,128)(2,1)S(1)} %bitcast.31, bf16[16,384,128]{2,1,0:T(8,128)(2,1)S(1)} %collective-permute-done.11.other, bf16[2,400,128]{2,1,0:T(8,128)(2,1)S(1)} %pad_maximum_fusion.2.a0, ...), custom_call_target="tpu_custom_call" | custom-call | tf_op jit(solution)/shard_map/weights_q/pallas_call | solution.py:351
  82.5 8.8 %all-to-all-start.1 = ((f32[8,96,128]{2,1,0:T(8,128)}), f32[8,96,128]{2,1,0:T(8,128)S(1)}, u32[]{:S(2)}, u32[]{:S(2)}) async-start(f32[8,96,128]{2,1,0:T(8,128)} %get-tuple-element.54), calls=%async_computation.1 | async-start | bytes 786432 | tf_op jit(solution)/shard_map/all_to_all | solution.py:442
  91.4 2.0 %collective-permute-start.12 = (f32[4,288,128]{2,1,0:T(8,128)S(1)}, f32[4,288,128]{2,1,0:T(8,128)S(1)}, u32[]{:S(2)}, u32[]{:S(2)}) collective-permute-start(f32[4,288,128]{2,1,0:T(8,128)S(1)} %get-tuple-element.49), channel_id=1, source_target_pairs={{0,4},{1,5},{2,6},{3,7},{4,0},{5,1},{6,2},{7,3},{8,12},{9,13},{10,... | collective-permute-start | bytes 1769480 | tf_op jit(solution)/shard_map/ppermute | solution.py:39
  93.4 7.0 %all-to-all-done.1.parts = f32[8,96,128]{2,1,0:T(8,128)S(1)} async-done(((f32[8,96,128]{2,1,0:T(8,128)}), f32[8,96,128]{2,1,0:T(8,128)S(1)}, u32[]{:S(2)}, u32[]{:S(2)}) %all-to-all-start.1) | async-done | bytes 393248 | tf_op jit(solution)/shard_map/all_to_all | solution.py:442
  101.5 10.3 %all-to-all-start.2 = ((f32[32,8,128]{2,1,0:T(8,128)}), f32[32,8,128]{2,1,0:T(8,128)S(1)}, u32[]{:S(2)}, u32[]{:S(2)}) async-start(f32[32,8,128]{2,1,0:T(8,128)} %bitcast.23), calls=%async_computation.2 | async-start | bytes 262144 | tf_op jit(solution)/shard_map/all_to_all | solution.py:447
  114.0 2.0 %collective-permute-start.15 = (f32[288,128]{1,0:T(8,128)S(1)}, f32[288,128]{1,0:T(8,128)S(1)}, u32[]{:S(2)}, u32[]{:S(2)}) collective-permute-start(f32[288,128]{1,0:T(8,128)S(1)} %get-tuple-element.53), channel_id=1, source_target_pairs={{0,2},{1,3},{2,0},{3,1},{4,6},{5,7},{6,4},{7,5},{8,10},{9,11},{10,... | collective-permute-start | bytes 442376 | tf_op jit(solution)/shard_map/ppermute | solution.py:39
  117.9 5.7 %collective-permute-done.14.p2 = f32[288,128]{1,0:T(8,128)S(1)} collective-permute-done((f32[288,128]{1,0:T(8,128)S(1)}, f32[288,128]{1,0:T(8,128)S(1)}, u32[]{:S(2)}, u32[]{:S(2)}) %collective-permute-start.14) | collective-permute-done | bytes 147488 | tf_op jit(solution)/shard_map/ppermute | solution.py:39
  (48 shorter events, 12.3 us)
Async XLA Ops:
  25.0 12.1 %collective-permute-start = (bf16[384,128]{1,0:T(8,128)(2,1)S(1)}, bf16[384,128]{1,0:T(8,128)(2,1)S(1)}, u32[]{:S(2)}, u32[]{:S(2)}) collective-permute-start(bf16[384,128]{1,0:T(8,128)(2,1)S(1)} %get-tuple-element.35), channel_id=1, source_target_pairs={{0,0},{1,8},{2,16},{3,24},{4,32},{5,40},{6,48},{7,56},{8,64},{9,72... | collective-permute-start | bytes 294920 | tf_op jit(solution)/shard_map/ppermute | solution.py:56
  37.2 9.2 %collective-permute-start.3 = (bf16[384,128]{1,0:T(8,128)(2,1)S(1)}, bf16[384,128]{1,0:T(8,128)(2,1)S(1)}, u32[]{:S(2)}, u32[]{:S(2)}) collective-permute-start(bf16[384,128]{1,0:T(8,128)(2,1)S(1)} %collective-permute-done), channel_id=1, source_target_pairs={{0,128},{8,136},{16,144},{24,152},{32,160},{40,168},{48,176},{56,1... | collective-permute-start | bytes 294920 | tf_op jit(solution)/shard_map/ppermute | solution.py:39
  38.1 11.5 %collective-permute-start.2 = (bf16[384,128]{1,0:T(8,128)(2,1)S(1)}, bf16[384,128]{1,0:T(8,128)(2,1)S(1)}, u32[]{:S(2)}, u32[]{:S(2)}) collective-permute-start(bf16[384,128]{1,0:T(8,128)(2,1)S(1)} %collective-permute-done), channel_id=1, source_target_pairs={{0,192},{8,200},{16,208},{24,216},{32,224},{40,232},{48,240},{56,2... | collective-permute-start | bytes 294920 | tf_op jit(solution)/shard_map/ppermute | solution.py:39
  39.4 10.2 %collective-permute-start.1 = (bf16[384,128]{1,0:T(8,128)(2,1)S(1)}, bf16[384,128]{1,0:T(8,128)(2,1)S(1)}, u32[]{:S(2)}, u32[]{:S(2)}) collective-permute-start(bf16[384,128]{1,0:T(8,128)(2,1)S(1)} %collective-permute-done), channel_id=1, source_target_pairs={{0,64},{8,72},{16,80},{24,88},{32,96},{40,104},{48,112},{56,120},{... | collective-permute-start | bytes 294920 | tf_op jit(solution)/shard_map/ppermute | solution.py:39
  49.7 16.9 %collective-permute-start.5 = (bf16[4,384,128]{2,1,0:T(8,128)(2,1)S(1)}, bf16[4,384,128]{2,1,0:T(8,128)(2,1)S(1)}, u32[]{:S(2)}, u32[]{:S(2)}) collective-permute-start(bf16[4,384,128]{2,1,0:T(8,128)(2,1)S(1)} %get-tuple-element.62), channel_id=1, source_target_pairs={{0,48},{8,56},{16,0},{24,8},{32,16},{40,24},{48,32},{56,40},{64,11... | collective-permute-start | bytes 1179656 | tf_op jit(solution)/shard_map/ppermute | solution.py:39
  52.5 17.5 %collective-permute-start.4 = (bf16[4,384,128]{2,1,0:T(8,128)(2,1)S(1)}, bf16[4,384,128]{2,1,0:T(8,128)(2,1)S(1)}, u32[]{:S(2)}, u32[]{:S(2)}) collective-permute-start(bf16[4,384,128]{2,1,0:T(8,128)(2,1)S(1)} %get-tuple-element.62), channel_id=1, source_target_pairs={{0,16},{8,24},{16,32},{24,40},{32,48},{40,56},{48,0},{56,8},{64,80... | collective-permute-start | bytes 1179656 | tf_op jit(solution)/shard_map/ppermute | solution.py:39
  52.5 17.5 %collective-permute-start.6 = (bf16[4,384,128]{2,1,0:T(8,128)(2,1)S(1)}, bf16[4,384,128]{2,1,0:T(8,128)(2,1)S(1)}, u32[]{:S(2)}, u32[]{:S(2)}) collective-permute-start(bf16[4,384,128]{2,1,0:T(8,128)(2,1)S(1)} %get-tuple-element.62), channel_id=1, source_target_pairs={{0,32},{8,40},{16,48},{24,56},{32,0},{40,8},{48,16},{56,24},{64,96... | collective-permute-start | bytes 1179656 | tf_op jit(solution)/shard_map/ppermute | solution.py:39
  54.8 5.4 %collective-permute-start.7 = (bf16[400,128]{1,0:T(8,128)(2,1)S(1)}, bf16[400,128]{1,0:T(8,128)(2,1)S(1)}, u32[]{:S(2)}, u32[]{:S(2)}) collective-permute-start(bf16[400,128]{1,0:T(8,128)(2,1)S(1)} %get-tuple-element.36), channel_id=1, source_target_pairs={{0,4},{1,5},{2,6},{3,7},{4,0},{5,1},{6,2},{7,3},{8,12},{9,13},{10,... | collective-permute-start | bytes 307208 | tf_op jit(solution)/shard_map/ppermute | solution.py:39
  60.2 10.1 %collective-permute-start.10 = (bf16[2,400,128]{2,1,0:T(8,128)(2,1)S(1)}, bf16[2,400,128]{2,1,0:T(8,128)(2,1)S(1)}, u32[]{:S(2)}, u32[]{:S(2)}) collective-permute-start(bf16[2,400,128]{2,1,0:T(8,128)(2,1)S(1)} %pad_maximum_fusion.2.a0), channel_id=1, source_target_pairs={{0,2},{1,3},{2,0},{3,1},{4,6},{5,7},{6,4},{7,5},{8,10},{9,11},{10,... | collective-permute-start | bytes 614408 | tf_op jit(solution)/shard_map/ppermute | solution.py:39
  64.5 8.1 %collective-permute-start.9 = (bf16[2,400,128]{2,1,0:T(8,128)(2,1)S(1)}, bf16[2,400,128]{2,1,0:T(8,128)(2,1)S(1)}, u32[]{:S(2)}, u32[]{:S(2)}) collective-permute-start(bf16[2,400,128]{2,1,0:T(8,128)(2,1)S(1)} %pad_maximum_fusion.2.a0), channel_id=1, source_target_pairs={{0,3},{1,0},{2,1},{3,2},{4,7},{5,4},{6,5},{7,6},{8,11},{9,8},{10,9... | collective-permute-start | bytes 614408 | tf_op jit(solution)/shard_map/ppermute | solution.py:39
  66.6 7.0 %collective-permute-start.8 = (bf16[2,400,128]{2,1,0:T(8,128)(2,1)S(1)}, bf16[2,400,128]{2,1,0:T(8,128)(2,1)S(1)}, u32[]{:S(2)}, u32[]{:S(2)}) collective-permute-start(bf16[2,400,128]{2,1,0:T(8,128)(2,1)S(1)} %pad_maximum_fusion.2.a0), channel_id=1, source_target_pairs={{0,1},{1,2},{2,3},{3,0},{4,5},{5,6},{6,7},{7,4},{8,9},{9,10},{10,1... | collective-permute-start | bytes 614408 | tf_op jit(solution)/shard_map/ppermute | solution.py:39
  70.0 7.0 %copy-start.8 = (f32[192,128]{1,0:T(8,128)S(1)}, f32[192,128]{1,0:T(8,128)}, u32[]{:S(2)}) copy-start(f32[192,128]{1,0:T(8,128)} %get-tuple-element.42.segments) | copy-start | bytes 294916
  70.0 7.0 %copy-start.9 = (f32[192,128]{1,0:T(8,128)S(1)}, f32[192,128]{1,0:T(8,128)}, u32[]{:S(2)}) copy-start(f32[192,128]{1,0:T(8,128)} %get-tuple-element.43.ph_segments) | copy-start | bytes 294916
  70.0 7.0 %copy-start.10 = (s32[5]{0:T(128)S(1)}, s32[5]{0:T(128)}, u32[]{:S(2)}) copy-start(s32[5]{0:T(128)} %stack.62.place) | copy-start | bytes 64
  73.6 3.4 %collective-permute-start.11 = (bf16[16,384,128]{2,1,0:T(8,128)(2,1)S(1)}, bf16[16,384,128]{2,1,0:T(8,128)(2,1)S(1)}, u32[]{:S(2)}, u32[]{:S(2)}) collective-permute-start(bf16[16,384,128]{2,1,0:T(8,128)(2,1)S(1)} %bitcast.29), channel_id=1, source_target_pairs={{0,8},{8,0},{16,24},{24,16},{32,40},{40,32},{48,56},{56,48},{64,72... | collective-permute-start | bytes 4718600 | tf_op jit(solution)/shard_map/ppermute | solution.py:39
  80.0 20.4 %copy-start.5 = (bf16[256,192]{1,0:T(8,128)(2,1)S(1)}, bf16[256,192]{1,0:T(8,128)(2,1)}, u32[]{:S(2)}) copy-start(bf16[256,192]{1,0:T(8,128)(2,1)} %get-tuple-element.55.receive_across) | copy-start | bytes 294916
  82.5 41.1 %copy-start.2 = (bf16[2,192,128]{2,1,0:T(8,128)(2,1)S(1)}, bf16[2,192,128]{2,1,0:T(8,128)(2,1)}, u32[]{:S(2)}) copy-start(bf16[2,192,128]{2,1,0:T(8,128)(2,1)} %get-tuple-element.34.local) | copy-start | bytes 294916
  82.5 41.1 %copy-start.7 = (bf16[192,256]{1,0:T(8,128)(2,1)S(1)}, bf16[192,256]{1,0:T(8,128)(2,1)}, u32[]{:S(2)}) copy-start(bf16[192,256]{1,0:T(8,128)(2,1)} %get-tuple-element.56.send) | copy-start | bytes 294916
  82.5 17.9 %all-to-all-start.1 = ((f32[8,96,128]{2,1,0:T(8,128)}), f32[8,96,128]{2,1,0:T(8,128)S(1)}, u32[]{:S(2)}, u32[]{:S(2)}) async-start(f32[8,96,128]{2,1,0:T(8,128)} %get-tuple-element.54), calls=%async_computation.1 | async-start | bytes 786432 | tf_op jit(solution)/shard_map/all_to_all | solution.py:442
  91.4 20.4 %collective-permute-start.12 = (f32[4,288,128]{2,1,0:T(8,128)S(1)}, f32[4,288,128]{2,1,0:T(8,128)S(1)}, u32[]{:S(2)}, u32[]{:S(2)}) collective-permute-start(f32[4,288,128]{2,1,0:T(8,128)S(1)} %get-tuple-element.49), channel_id=1, source_target_pairs={{0,4},{1,5},{2,6},{3,7},{4,0},{5,1},{6,2},{7,3},{8,12},{9,13},{10,... | collective-permute-start | bytes 1769480 | tf_op jit(solution)/shard_map/ppermute | solution.py:39
  101.5 22.1 %all-to-all-start.2 = ((f32[32,8,128]{2,1,0:T(8,128)}), f32[32,8,128]{2,1,0:T(8,128)S(1)}, u32[]{:S(2)}, u32[]{:S(2)}) async-start(f32[32,8,128]{2,1,0:T(8,128)} %bitcast.23), calls=%async_computation.2 | async-start | bytes 262144 | tf_op jit(solution)/shard_map/all_to_all | solution.py:447
  111.9 6.0 %collective-permute-start.13 = (f32[288,128]{1,0:T(8,128)S(1)}, f32[288,128]{1,0:T(8,128)S(1)}, u32[]{:S(2)}, u32[]{:S(2)}) collective-permute-start(f32[288,128]{1,0:T(8,128)S(1)} %get-tuple-element.51), channel_id=1, source_target_pairs={{0,3},{1,0},{2,1},{3,2},{4,7},{5,4},{6,5},{7,6},{8,11},{9,8},{10,9... | collective-permute-start | bytes 442376 | tf_op jit(solution)/shard_map/ppermute | solution.py:39
  113.7 9.8 %collective-permute-start.14 = (f32[288,128]{1,0:T(8,128)S(1)}, f32[288,128]{1,0:T(8,128)S(1)}, u32[]{:S(2)}, u32[]{:S(2)}) collective-permute-start(f32[288,128]{1,0:T(8,128)S(1)} %get-tuple-element.52), channel_id=1, source_target_pairs={{0,1},{1,2},{2,3},{3,0},{4,5},{5,6},{6,7},{7,4},{8,9},{9,10},{10,1... | collective-permute-start | bytes 442376 | tf_op jit(solution)/shard_map/ppermute | solution.py:39
  114.0 9.6 %collective-permute-start.15 = (f32[288,128]{1,0:T(8,128)S(1)}, f32[288,128]{1,0:T(8,128)S(1)}, u32[]{:S(2)}, u32[]{:S(2)}) collective-permute-start(f32[288,128]{1,0:T(8,128)S(1)} %get-tuple-element.53), channel_id=1, source_target_pairs={{0,2},{1,3},{2,0},{3,1},{4,6},{5,7},{6,4},{7,5},{8,10},{9,11},{10,... | collective-permute-start | bytes 442376 | tf_op jit(solution)/shard_map/ppermute | solution.py:39
  (6 other events, 21.8 us)

commit v4 on v3

--- a/solution.py
+++ b/solution.py
@@ -39,8 +39,15 @@
     return lax.ppermute(x, name, pairs)
 
 
-def gather_digit(x, axis):
-    return jnp.stack([x] + [turn(x, axis, -offset) for offset in offsets[1:]])
+def around_digit(x, axis):
+    return [x] + [turn(x, axis, -offset) for offset in offsets[1:]]
+
+
+def around_ring(x, axis, way):
+    near = turn(x, axis, way)
+    other = turn(x, axis, -way)
+    far = turn(near, axis, way)
+    return [x, near, other, far] if way == 1 else [x, other, near, far]
 
 
 def gather_cols(x):
@@ -243,29 +250,19 @@
     return iota(shape, 0) + (place[3] * block - place[4] * width) == iota(shape, 1)
 
 
-def places_of(place, own, other):
-    zh, xx, cc = place[0], place[1], place[2]
-    for cr, source in enumerate((own, other)):
-        for xr, xo in enumerate(offsets):
-            from_col = ((xx + xo) & 3) * 2 + (cc if cr == 0 else 1 - cc)
-            for zr, zo in enumerate(offsets):
-                yield cr, xr * 4 + zr, source, from_col, (zh + zo) & 3
-
-
 def column_at(place, y_place, z_place):
     return ((place[4] + offsets[y_place]) & 3) + (((place[4] >> 2) + z_place) & 1) * 4
 
 
-def fill(place, own, other, around, base, right, left, by_col):
+def fill(place, blocks, around, second, right, left, by_col):
     block = left.shape[0]
-    ids = []
-    for cr, b, source, from_col, j in places_of(place, own, other):
-        k = cr * 4 + b // 4
-        right[pl.ds(pl.multiple_of(j * block, block), block), k * lanes : (k + 1) * lanes] = source[
-            b, base : base + block, :
-        ]
-        if b % 4 == 0:
-            ids.append(from_col)
+    base = second * block
+    zh, xx, cc = place[0], place[1], place[2]
+    ids = [((xx + o) & 3) * 2 + other for other in (cc, 1 - cc) for o in offsets]
+    for k, source in enumerate(blocks):
+        for z_place, o in enumerate(offsets):
+            rows = pl.ds(pl.multiple_of(((zh + o) & 3) * block, block), block)
+            right[rows, k * lanes : (k + 1) * lanes] = source[second * 4 + z_place]
     for y_place, source in enumerate(around):
         for z_place in range(2):
             by_col[column_at(place, y_place, z_place)] = source[z_place, base : base + block]
@@ -274,13 +271,12 @@
     return ids
 
 
-def g_kernel(
-    place, own, other, a0, a1, a2, a3, multiplier, segments, ph_segments, lengths,
-    out, more, scale, right, left, by_col,
-):
+def g_kernel(*refs):
+    place, *blocks = refs[:9]
+    around = refs[9:13]
+    multiplier, segments, ph_segments, lengths, out, more, scale, right, left, by_col = refs[13:]
     block, width = multiplier.shape
-    around = (a0, a1, a2, a3)
-    ids = fill(place, own, other, around, block, right, left, by_col)
+    ids = fill(place, blocks, around, 1, right, left, by_col)
     sums = jnp.zeros((extra, lanes), f32)
     for source in around:
         for z_place in range(2):
@@ -304,12 +300,12 @@
         more[from_col] = halves_side_by_side(top, bottom, False)
 
 
-def q_kernel(
-    place, own, other, a0, a1, a2, a3, multiplier, hamiltonian, more,
-    keep, away, right, left, by_col, by_col_out,
-):
+def q_kernel(*refs):
+    place, *blocks = refs[:9]
+    around = refs[9:13]
+    multiplier, hamiltonian, more, keep, away, right, left, by_col, by_col_out = refs[13:]
     block, width = multiplier.shape
-    ids = fill(place, own, other, (a0, a1, a2, a3), 0, right, left, by_col)
+    ids = fill(place, blocks, around, 0, right, left, by_col)
     gram = transposed_dot(left[...], right[...])
     resid = jnp.where(diagonal_of(place, multiplier.shape), shift_value, 0.0) - gram
     weight = (multiplier[...].astype(f32) + penalty * resid).astype(bf16)
@@ -321,8 +317,8 @@
     for z_place, out in enumerate((keep, away)):
         for y_place in range(4):
             from_col = column_at(place, y_place, z_place)
-            out[y_place, :block, :] = by_col_out[from_col]
-            out[y_place, block:, :] = more[from_col]
+            out[y_place, :block] = by_col_out[from_col]
+            out[y_place, block:] = more[from_col]
 
 
 def back_kernel(parts, receive_across, back):
@@ -410,12 +406,15 @@
         scalars=False,
     )
     piece = to_column(body, rows, cols, per)
-    near = gather_digit(piece, z_hi)
-    own = gather_digit(near, x_axis).reshape(16, tall, lanes)
+    near = around_digit(piece, z_hi)
+    pair_near = jnp.stack([b[:block] for b in near])
+    ph_near = jnp.stack([b[block:] for b in near])
     around = gather_cols(longer)
-    own, around = lax.optimization_barrier((own, around))
-    other = turn(own, core, 1)
-    gathered = (place, own, other, *around)
+    pair_own = around_ring(pair_near, x_axis, 1)
+    ph_own = around_ring(ph_near, x_axis, -1)
+    joined = [jnp.concatenate(b) for b in zip(pair_own, ph_own)]
+    joined[3], around = lax.optimization_barrier((joined[3], around))
+    blocks = joined + [turn(b, core, 1) for b in joined]
     shared = [
         ((width, cols * lanes), bf16),
         ((block, cols * lanes), bf16),
@@ -425,7 +424,7 @@
         g_kernel,
         "weights_g",
         [((cols, block // 2, lanes), f32), ((cols, block // 2, lanes), f32), ((block, 1), f32)],
-        (*gathered, multiplier_g, segments, ph_segments, lengths),
+        (place, *blocks, *around, multiplier_g, segments, ph_segments, lengths),
         shared,
         room=16,
     )
@@ -434,24 +433,24 @@
         q_kernel,
         "weights_q",
         [((4, long, lanes), f32)] * 2,
-        (*gathered, multiplier_q, hamiltonian, parts_f),
+        (place, *blocks, *around, multiplier_q, hamiltonian, parts_f),
         shared + [((cols, block, lanes), f32)],
         room=16,
     )
     parts_e, keep, away = lax.optimization_barrier((parts_e, keep, away))
     sums_e = lax.all_to_all(parts_e, "col", 0, 0)
     came = turn(away, z_lo, 1)
+    parts = call(add_kernel, "add", [((long, lanes), f32)] * 4, (keep, came), scalars=False)
+    sums = [parts[0]] + [turn(p, y_axis, o) for p, o in zip(parts[1:], offsets[1:])]
     (back,) = call(
         back_kernel, "back", [((padded, lanes), f32)], (sums_e, receive_across), scalars=False
     )
     returned = lax.all_to_all(back.reshape(rows, group, lanes), "row", 0, 0)
-    parts = call(add_kernel, "add", [((long, lanes), f32)] * 4, (keep, came), scalars=False)
-    parts = [parts[0]] + [turn(p, y_axis, o) for p, o in zip(parts[1:], offsets[1:])]
     grads = call(
         last_kernel,
         "gradients",
         [((part, block), f32)] * 3,
-        (*parts, returned.reshape(padded, lanes), send, mine, scale),
+        (*sums, returned.reshape(padded, lanes), send, mine, scale),
         scalars=False,
     )
     return tuple(g.T for g in grads)

time: 126 us -> 123 us (0.976)
  waiting for transfers between devices: 42.1 us -> 39.1 us
  starting transfers between devices: 49.3 us -> 50.6 us
    ppermute x15 -> x21, starting transfers between devices: 23.3 us -> 33.2 us  [turn(): return lax.ppermute(x, name, pairs)]
    all_to_all x1, starting transfers between devices: 10.3 us -> 5.04 us  [local(): returned = lax.all_to_all(back.reshape(rows, group, lanes), 'row', 0, 0)]
    all_to_all x1, starting transfers between devices: 8.83 us -> 5.52 us  [local(): sums_e = lax.all_to_all(parts_e, 'col', 0, 0)]
    ppermute x1, waiting for transfers between devices: 5.26 us -> 2.62 us  [to_column(): return lax.ppermute(x, both, pairs)]
    ppermute x15 -> x21, waiting for transfers between devices: 29.8 us -> 29.4 us  [turn(): return lax.ppermute(x, name, pairs)]
  transfers between devices with their start and end apart: 18 -> 24, of which waited for: 12 -> 11; matrix products, arithmetic and copies ran while one was open for 0% -> 0% of each run, Pallas kernels for 1% -> 1%
where the time goes in v4:
time: 123 us
  starting transfers between devices  50.6 us (41%)
  waiting for transfers between devices  39.1 us (32%)
  blocking collectives  18.9 us (15%)
  Pallas kernels  10.8 us (9%)
  local copies, waits for them, and re-layouts  2.45 us (2%)
    ppermute x21, starting transfers between devices, turn(): return lax.ppermute(x, name, pairs)  33.2 us
    ppermute x21, waiting for transfers between devices, turn(): return lax.ppermute(x, name, pairs)  29.4 us
    all_to_all x1, blocking collectives, local(): incoming = lax.all_to_all(leaving.reshape(rows, group, lanes), 'row', 0, 0)  18.9 us
    pallas_call x7, Pallas kernels, call(): pl.pallas_call(kernel, out_shape=[jax.ShapeDtypeStruct(s, d) for s, d in...  10.8 us
    all_to_all x1, waiting for transfers between devices, local(): sums_e = lax.all_to_all(parts_e, 'col', 0, 0)  7.02 us
    ppermute x1, starting transfers between devices, to_column(): return lax.ppermute(x, both, pairs)  6.87 us
    all_to_all x1, starting transfers between devices, local(): sums_e = lax.all_to_all(parts_e, 'col', 0, 0)  5.52 us
    all_to_all x1, starting transfers between devices, local(): returned = lax.all_to_all(back.reshape(rows, group, lanes), 'row', 0, 0)  5.04 us
  transfers between devices with their start and end apart: 24, of which 11 were waited for; matrix products, arithmetic and copies ran while one was open for 0% of the time, Pallas kernels for 1%

profile of v4, /device:TPU:64, one launch (start us, length us, event | category | flops | bytes accessed | tf_op | source)
XLA Modules:
  0.0 122.9 jit_solution(17271101645155428550)
XLA Ops:
  1.4 3.0 %routes.1 = (bf16[256,128]{1,0:T(8,128)(2,1)}, bf16[2,192,128]{2,1,0:T(8,128)(2,1)}, bf16[192,256]{1,0:T(8,128)(2,1)}, bf16[192,256]{1,0:T(8,128)(2,1)}, bf16[25...) custom-call(s32[5]{0:T(128)} %stack.62.place.refs_0_, s32[48,128]{1,0:T(8,128)} %bitcast.61, ...), custom_call_target="tpu_custom_call" | custom-call | tf_op jit(solution)/shard_map/routes/pallas_call | solution.py:347
  4.3 18.9 %all_to_all.15 = bf16[32,8,128]{2,1,0:T(8,128)(2,1)S(1)} all-to-all(bf16[32,8,128]{2,1,0:T(8,128)(2,1)} %bitcast.57), channel_id=1, replica_groups=mesh['row'=32,'col'=8] {'row'}, dimensions={0} | all-to-all | bytes 131072 | tf_op jit(solution)/shard_map/all_to_all | solution.py:399
  24.3 6.9 %collective-permute-start = (bf16[384,128]{1,0:T(8,128)(2,1)S(1)}, bf16[384,128]{1,0:T(8,128)(2,1)S(1)}, u32[]{:S(2)}, u32[]{:S(2)}) collective-permute-start(bf16[384,128]{1,0:T(8,128)(2,1)S(1)} %get-tuple-element.35), channel_id=1, source_target_pairs={{0,0},{1,8},{2,16},{3,24},{4,32},{5,40},{6,48},{7,56},{8,64},{9,72... | collective-permute-start | bytes 294920 | tf_op jit(solution)/shard_map/ppermute | solution.py:63
  31.2 2.0 %collective-permute-start.10 = (bf16[400,128]{1,0:T(8,128)(2,1)S(1)}, bf16[400,128]{1,0:T(8,128)(2,1)S(1)}, u32[]{:S(2)}, u32[]{:S(2)}) collective-permute-start(bf16[400,128]{1,0:T(8,128)(2,1)S(1)} %get-tuple-element.36), channel_id=1, source_target_pairs={{0,4},{1,5},{2,6},{3,7},{4,0},{5,1},{6,2},{7,3},{8,12},{9,13},{10,... | collective-permute-start | bytes 307208 | tf_op jit(solution)/shard_map/ppermute | solution.py:39
  33.2 2.6 %collective-permute-done = bf16[384,128]{1,0:T(8,128)(2,1)S(1)} collective-permute-done((bf16[384,128]{1,0:T(8,128)(2,1)S(1)}, bf16[384,128]{1,0:T(8,128)(2,1)S(1)}, u32[]{:S(2)}, u32[]{:S(2)}) %collective-permute-start) | collective-permute-done | bytes 98336 | tf_op jit(solution)/shard_map/ppermute | solution.py:63
  35.8 2.0 %collective-permute-start.3 = (bf16[384,128]{1,0:T(8,128)(2,1)S(1)}, bf16[384,128]{1,0:T(8,128)(2,1)S(1)}, u32[]{:S(2)}, u32[]{:S(2)}) collective-permute-start(bf16[384,128]{1,0:T(8,128)(2,1)S(1)} %collective-permute-done), channel_id=1, source_target_pairs={{0,128},{8,136},{16,144},{24,152},{32,160},{40,168},{48,176},{56,1... | collective-permute-start | bytes 294920 | tf_op jit(solution)/shard_map/ppermute | solution.py:39
  39.6 2.3 %collective-permute-start.1 = (bf16[384,128]{1,0:T(8,128)(2,1)S(1)}, bf16[384,128]{1,0:T(8,128)(2,1)S(1)}, u32[]{:S(2)}, u32[]{:S(2)}) collective-permute-start(bf16[384,128]{1,0:T(8,128)(2,1)S(1)} %collective-permute-done), channel_id=1, source_target_pairs={{0,64},{8,72},{16,80},{24,88},{32,96},{40,104},{48,112},{56,120},{... | collective-permute-start | bytes 294920 | tf_op jit(solution)/shard_map/ppermute | solution.py:39
  41.9 6.6 %collective-permute-start.13 = (bf16[2,400,128]{2,1,0:T(8,128)(2,1)S(1)}, bf16[2,400,128]{2,1,0:T(8,128)(2,1)S(1)}, u32[]{:S(2)}, u32[]{:S(2)}) collective-permute-start(bf16[2,400,128]{2,1,0:T(8,128)(2,1)S(1)} %pad_maximum_fusion.1.refs_9_), channel_id=1, source_target_pairs={{0,2},{1,3},{2,0},{3,1},{4,6},{5,7},{6,4},{7,5},{8,10},{9,11},{10,... | collective-permute-start | bytes 614408 | tf_op jit(solution)/shard_map/ppermute | solution.py:39
  52.2 2.1 %collective-permute-start.7 = (bf16[4,192,128]{2,1,0:T(8,128)(2,1)S(1)}, bf16[4,192,128]{2,1,0:T(8,128)(2,1)S(1)}, u32[]{:S(2)}, u32[]{:S(2)}) collective-permute-start(bf16[4,192,128]{2,1,0:T(8,128)(2,1)S(1)} %pad_maximum_fusion.3), channel_id=1, source_target_pairs={{0,48},{8,56},{16,0},{24,8},{32,16},{40,24},{48,32},{56,40},{64,11... | collective-permute-start | bytes 589832 | tf_op jit(solution)/shard_map/ppermute | solution.py:39
  54.5 3.6 %collective-permute-done.4 = bf16[4,192,128]{2,1,0:T(8,128)(2,1)S(1)} collective-permute-done((bf16[4,192,128]{2,1,0:T(8,128)(2,1)S(1)}, bf16[4,192,128]{2,1,0:T(8,128)(2,1)S(1)}, u32[]{:S(2)}, u32[]{:S(2)}) %collective-permute-start.4) | collective-permute-done | bytes 196640 | tf_op jit(solution)/shard_map/ppermute | solution.py:39
  59.9 2.7 %collective-permute-start.9 = (bf16[4,192,128]{2,1,0:T(8,128)(2,1)S(1)}, bf16[4,192,128]{2,1,0:T(8,128)(2,1)S(1)}, u32[]{:S(2)}, u32[]{:S(2)}) collective-permute-start(bf16[4,192,128]{2,1,0:T(8,128)(2,1)S(1)} %collective-permute-done.7), channel_id=1, source_target_pairs={{0,48},{8,56},{16,0},{24,8},{32,16},{40,24},{48,32},{56,40},{64,11... | collective-permute-start | bytes 589832 | tf_op jit(solution)/shard_map/ppermute | solution.py:39
  62.6 3.7 %collective-permute-done.5 = bf16[4,192,128]{2,1,0:T(8,128)(2,1)S(1)} collective-permute-done((bf16[4,192,128]{2,1,0:T(8,128)(2,1)S(1)}, bf16[4,192,128]{2,1,0:T(8,128)(2,1)S(1)}, u32[]{:S(2)}, u32[]{:S(2)}) %collective-permute-start.5) | collective-permute-done | bytes 196640 | tf_op jit(solution)/shard_map/ppermute | solution.py:39
  66.4 1.9 %collective-permute-start.11 = (bf16[2,400,128]{2,1,0:T(8,128)(2,1)S(1)}, bf16[2,400,128]{2,1,0:T(8,128)(2,1)S(1)}, u32[]{:S(2)}, u32[]{:S(2)}) collective-permute-start(bf16[2,400,128]{2,1,0:T(8,128)(2,1)S(1)} %pad_maximum_fusion.1.refs_9_), channel_id=1, source_target_pairs={{0,1},{1,2},{2,3},{3,0},{4,5},{5,6},{6,7},{7,4},{8,9},{9,10},{10,1... | collective-permute-start | bytes 614408 | tf_op jit(solution)/shard_map/ppermute | solution.py:39
  69.4 7.1 %collective-permute-done.11.refs_10_ = bf16[2,400,128]{2,1,0:T(8,128)(2,1)S(1)} collective-permute-done((bf16[2,400,128]{2,1,0:T(8,128)(2,1)S(1)}, bf16[2,400,128]{2,1,0:T(8,128)(2,1)S(1)}, u32[]{:S(2)}, u32[]{:S(2)}) %collective-permute-start.11) | collective-permute-done | bytes 204832 | tf_op jit(solution)/shard_map/ppermute | solution.py:39
  78.9 3.0 %weights_g.1 = (f32[8,96,128]{2,1,0:T(8,128)}, f32[8,96,128]{2,1,0:T(8,128)S(1)}, f32[192,1]{1,0:T(8,128)S(1)}) custom-call(s32[5]{0:T(128)S(1)} %copy-done.9, bf16[8,192,128]{2,1,0:T(8,128)(2,1)S(1)} %constant_dynamic-update-slice_fusion.refs_1_, bf16[8,192,128]{2,1,0:T(8,128)(2,1)S(1)} %constant_dynamic-update-slice_fusion.8.refs_2_, ...), custom_call_target="tpu_custom_call" | custom-call | tf_op jit(solution)/shard_map/weights_g/pallas_call | solution.py:347
  81.8 2.5 %weights_q.1 = (f32[4,288,128]{2,1,0:T(8,128)S(1)}, f32[4,288,128]{2,1,0:T(8,128)S(1)}) custom-call(s32[5]{0:T(128)S(1)} %copy-done.9, bf16[8,192,128]{2,1,0:T(8,128)(2,1)S(1)} %constant_dynamic-update-slice_fusion.refs_1_, bf16[8,192,128]{2,1,0:T(8,128)(2,1)S(1)} %constant_dynamic-update-slice_fusion.8.refs_2_, ...), custom_call_target="tpu_custom_call" | custom-call | tf_op jit(solution)/shard_map/weights_q/pallas_call | solution.py:347
  84.3 5.5 %all-to-all-start.1 = ((f32[8,96,128]{2,1,0:T(8,128)}), f32[8,96,128]{2,1,0:T(8,128)S(1)}, u32[]{:S(2)}, u32[]{:S(2)}) async-start(f32[8,96,128]{2,1,0:T(8,128)} %get-tuple-element.54), calls=%async_computation.1 | async-start | bytes 786432 | tf_op jit(solution)/shard_map/all_to_all | solution.py:441
  89.9 2.0 %collective-permute-start.18 = (f32[4,288,128]{2,1,0:T(8,128)S(1)}, f32[4,288,128]{2,1,0:T(8,128)S(1)}, u32[]{:S(2)}, u32[]{:S(2)}) collective-permute-start(f32[4,288,128]{2,1,0:T(8,128)S(1)} %get-tuple-element.49), channel_id=1, source_target_pairs={{0,4},{1,5},{2,6},{3,7},{4,0},{5,1},{6,2},{7,3},{8,12},{9,13},{10,... | collective-permute-start | bytes 1769480 | tf_op jit(solution)/shard_map/ppermute | solution.py:39
  91.9 7.0 %all-to-all-done.1.parts = f32[8,96,128]{2,1,0:T(8,128)S(1)} async-done(((f32[8,96,128]{2,1,0:T(8,128)}), f32[8,96,128]{2,1,0:T(8,128)S(1)}, u32[]{:S(2)}, u32[]{:S(2)}) %all-to-all-start.1) | async-done | bytes 393248 | tf_op jit(solution)/shard_map/all_to_all | solution.py:441
  100.0 5.0 %all-to-all-start.2 = ((f32[32,8,128]{2,1,0:T(8,128)}), f32[32,8,128]{2,1,0:T(8,128)S(1)}, u32[]{:S(2)}, u32[]{:S(2)}) async-start(f32[32,8,128]{2,1,0:T(8,128)} %bitcast.22), calls=%async_computation.2 | async-start | bytes 262144 | tf_op jit(solution)/shard_map/all_to_all | solution.py:448
  105.1 5.8 %collective-permute-done.18.came = f32[4,288,128]{2,1,0:T(8,128)S(1)} collective-permute-done((f32[4,288,128]{2,1,0:T(8,128)S(1)}, f32[4,288,128]{2,1,0:T(8,128)S(1)}, u32[]{:S(2)}, u32[]{:S(2)}) %collective-permute-start.18) | collective-permute-done | bytes 589856 | tf_op jit(solution)/shard_map/ppermute | solution.py:39
  110.9 3.0 %collective-permute-start.19 = (f32[288,128]{1,0:T(8,128)S(1)}, f32[288,128]{1,0:T(8,128)S(1)}, u32[]{:S(2)}, u32[]{:S(2)}) collective-permute-start(f32[288,128]{1,0:T(8,128)S(1)} %get-tuple-element.51), channel_id=1, source_target_pairs={{0,3},{1,0},{2,1},{3,2},{4,7},{5,4},{6,5},{7,6},{8,11},{9,8},{10,9... | collective-permute-start | bytes 442376 | tf_op jit(solution)/shard_map/ppermute | solution.py:39
  113.9 2.3 %collective-permute-start.21 = (f32[288,128]{1,0:T(8,128)S(1)}, f32[288,128]{1,0:T(8,128)S(1)}, u32[]{:S(2)}, u32[]{:S(2)}) collective-permute-start(f32[288,128]{1,0:T(8,128)S(1)} %get-tuple-element.53), channel_id=1, source_target_pairs={{0,2},{1,3},{2,0},{3,1},{4,6},{5,7},{6,4},{7,5},{8,10},{9,11},{10,... | collective-permute-start | bytes 442376 | tf_op jit(solution)/shard_map/ppermute | solution.py:39
  117.8 4.0 %collective-permute-done.20.p2 = f32[288,128]{1,0:T(8,128)S(1)} collective-permute-done((f32[288,128]{1,0:T(8,128)S(1)}, f32[288,128]{1,0:T(8,128)S(1)}, u32[]{:S(2)}, u32[]{:S(2)}) %collective-permute-start.20) | collective-permute-done | bytes 147488 | tf_op jit(solution)/shard_map/ppermute | solution.py:39
  (75 shorter events, 16.4 us)
Async XLA Ops:
  24.3 11.5 %collective-permute-start = (bf16[384,128]{1,0:T(8,128)(2,1)S(1)}, bf16[384,128]{1,0:T(8,128)(2,1)S(1)}, u32[]{:S(2)}, u32[]{:S(2)}) collective-permute-start(bf16[384,128]{1,0:T(8,128)(2,1)S(1)} %get-tuple-element.35), channel_id=1, source_target_pairs={{0,0},{1,8},{2,16},{3,24},{4,32},{5,40},{6,48},{7,56},{8,64},{9,72... | collective-permute-start | bytes 294920 | tf_op jit(solution)/shard_map/ppermute | solution.py:63
  31.2 10.7 %collective-permute-start.10 = (bf16[400,128]{1,0:T(8,128)(2,1)S(1)}, bf16[400,128]{1,0:T(8,128)(2,1)S(1)}, u32[]{:S(2)}, u32[]{:S(2)}) collective-permute-start(bf16[400,128]{1,0:T(8,128)(2,1)S(1)} %get-tuple-element.36), channel_id=1, source_target_pairs={{0,4},{1,5},{2,6},{3,7},{4,0},{5,1},{6,2},{7,3},{8,12},{9,13},{10,... | collective-permute-start | bytes 307208 | tf_op jit(solution)/shard_map/ppermute | solution.py:39
  35.8 14.2 %collective-permute-start.3 = (bf16[384,128]{1,0:T(8,128)(2,1)S(1)}, bf16[384,128]{1,0:T(8,128)(2,1)S(1)}, u32[]{:S(2)}, u32[]{:S(2)}) collective-permute-start(bf16[384,128]{1,0:T(8,128)(2,1)S(1)} %collective-permute-done), channel_id=1, source_target_pairs={{0,128},{8,136},{16,144},{24,152},{32,160},{40,168},{48,176},{56,1... | collective-permute-start | bytes 294920 | tf_op jit(solution)/shard_map/ppermute | solution.py:39
  37.8 12.2 %collective-permute-start.2 = (bf16[384,128]{1,0:T(8,128)(2,1)S(1)}, bf16[384,128]{1,0:T(8,128)(2,1)S(1)}, u32[]{:S(2)}, u32[]{:S(2)}) collective-permute-start(bf16[384,128]{1,0:T(8,128)(2,1)S(1)} %collective-permute-done), channel_id=1, source_target_pairs={{0,192},{8,200},{16,208},{24,216},{32,224},{40,232},{48,240},{56,2... | collective-permute-start | bytes 294920 | tf_op jit(solution)/shard_map/ppermute | solution.py:39
  39.6 10.4 %collective-permute-start.1 = (bf16[384,128]{1,0:T(8,128)(2,1)S(1)}, bf16[384,128]{1,0:T(8,128)(2,1)S(1)}, u32[]{:S(2)}, u32[]{:S(2)}) collective-permute-start(bf16[384,128]{1,0:T(8,128)(2,1)S(1)} %collective-permute-done), channel_id=1, source_target_pairs={{0,64},{8,72},{16,80},{24,88},{32,96},{40,104},{48,112},{56,120},{... | collective-permute-start | bytes 294920 | tf_op jit(solution)/shard_map/ppermute | solution.py:39
  41.9 27.2 %collective-permute-start.13 = (bf16[2,400,128]{2,1,0:T(8,128)(2,1)S(1)}, bf16[2,400,128]{2,1,0:T(8,128)(2,1)S(1)}, u32[]{:S(2)}, u32[]{:S(2)}) collective-permute-start(bf16[2,400,128]{2,1,0:T(8,128)(2,1)S(1)} %pad_maximum_fusion.1.refs_9_), channel_id=1, source_target_pairs={{0,2},{1,3},{2,0},{3,1},{4,6},{5,7},{6,4},{7,5},{8,10},{9,11},{10,... | collective-permute-start | bytes 614408 | tf_op jit(solution)/shard_map/ppermute | solution.py:39
  48.6 20.8 %collective-permute-start.12 = (bf16[2,400,128]{2,1,0:T(8,128)(2,1)S(1)}, bf16[2,400,128]{2,1,0:T(8,128)(2,1)S(1)}, u32[]{:S(2)}, u32[]{:S(2)}) collective-permute-start(bf16[2,400,128]{2,1,0:T(8,128)(2,1)S(1)} %pad_maximum_fusion.1.refs_9_), channel_id=1, source_target_pairs={{0,3},{1,0},{2,1},{3,2},{4,7},{5,4},{6,5},{7,6},{8,11},{9,8},{10,9... | collective-permute-start | bytes 614408 | tf_op jit(solution)/shard_map/ppermute | solution.py:39
  50.1 8.0 %collective-permute-start.6 = (bf16[4,192,128]{2,1,0:T(8,128)(2,1)S(1)}, bf16[4,192,128]{2,1,0:T(8,128)(2,1)S(1)}, u32[]{:S(2)}, u32[]{:S(2)}) collective-permute-start(bf16[4,192,128]{2,1,0:T(8,128)(2,1)S(1)} %pad_maximum_fusion.2), channel_id=1, source_target_pairs={{0,48},{8,56},{16,0},{24,8},{32,16},{40,24},{48,32},{56,40},{64,11... | collective-permute-start | bytes 589832 | tf_op jit(solution)/shard_map/ppermute | solution.py:39
  51.0 7.1 %collective-permute-start.4 = (bf16[4,192,128]{2,1,0:T(8,128)(2,1)S(1)}, bf16[4,192,128]{2,1,0:T(8,128)(2,1)S(1)}, u32[]{:S(2)}, u32[]{:S(2)}) collective-permute-start(bf16[4,192,128]{2,1,0:T(8,128)(2,1)S(1)} %pad_maximum_fusion.2), channel_id=1, source_target_pairs={{0,16},{8,24},{16,32},{24,40},{32,48},{40,56},{48,0},{56,8},{64,80... | collective-permute-start | bytes 589832 | tf_op jit(solution)/shard_map/ppermute | solution.py:39
  52.2 7.7 %collective-permute-start.7 = (bf16[4,192,128]{2,1,0:T(8,128)(2,1)S(1)}, bf16[4,192,128]{2,1,0:T(8,128)(2,1)S(1)}, u32[]{:S(2)}, u32[]{:S(2)}) collective-permute-start(bf16[4,192,128]{2,1,0:T(8,128)(2,1)S(1)} %pad_maximum_fusion.3), channel_id=1, source_target_pairs={{0,48},{8,56},{16,0},{24,8},{32,16},{40,24},{48,32},{56,40},{64,11... | collective-permute-start | bytes 589832 | tf_op jit(solution)/shard_map/ppermute | solution.py:39
  58.1 8.3 %collective-permute-start.5 = (bf16[4,192,128]{2,1,0:T(8,128)(2,1)S(1)}, bf16[4,192,128]{2,1,0:T(8,128)(2,1)S(1)}, u32[]{:S(2)}, u32[]{:S(2)}) collective-permute-start(bf16[4,192,128]{2,1,0:T(8,128)(2,1)S(1)} %pad_maximum_fusion.3), channel_id=1, source_target_pairs={{0,16},{8,24},{16,32},{24,40},{32,48},{40,56},{48,0},{56,8},{64,80... | collective-permute-start | bytes 589832 | tf_op jit(solution)/shard_map/ppermute | solution.py:39
  58.1 10.3 %collective-permute-start.8 = (bf16[4,192,128]{2,1,0:T(8,128)(2,1)S(1)}, bf16[4,192,128]{2,1,0:T(8,128)(2,1)S(1)}, u32[]{:S(2)}, u32[]{:S(2)}) collective-permute-start(bf16[4,192,128]{2,1,0:T(8,128)(2,1)S(1)} %collective-permute-done.4), channel_id=1, source_target_pairs={{0,16},{8,24},{16,32},{24,40},{32,48},{40,56},{48,0},{56,8},{64,80... | collective-permute-start | bytes 589832 | tf_op jit(solution)/shard_map/ppermute | solution.py:39
  59.9 8.7 %collective-permute-start.9 = (bf16[4,192,128]{2,1,0:T(8,128)(2,1)S(1)}, bf16[4,192,128]{2,1,0:T(8,128)(2,1)S(1)}, u32[]{:S(2)}, u32[]{:S(2)}) collective-permute-start(bf16[4,192,128]{2,1,0:T(8,128)(2,1)S(1)} %collective-permute-done.7), channel_id=1, source_target_pairs={{0,48},{8,56},{16,0},{24,8},{32,16},{40,24},{48,32},{56,40},{64,11... | collective-permute-start | bytes 589832 | tf_op jit(solution)/shard_map/ppermute | solution.py:39
  66.4 10.1 %collective-permute-start.11 = (bf16[2,400,128]{2,1,0:T(8,128)(2,1)S(1)}, bf16[2,400,128]{2,1,0:T(8,128)(2,1)S(1)}, u32[]{:S(2)}, u32[]{:S(2)}) collective-permute-start(bf16[2,400,128]{2,1,0:T(8,128)(2,1)S(1)} %pad_maximum_fusion.1.refs_9_), channel_id=1, source_target_pairs={{0,1},{1,2},{2,3},{3,0},{4,5},{5,6},{6,7},{7,4},{8,9},{9,10},{10,1... | collective-permute-start | bytes 614408 | tf_op jit(solution)/shard_map/ppermute | solution.py:39
  68.5 8.0 %collective-permute-start.14 = (bf16[8,192,128]{2,1,0:T(8,128)(2,1)S(1)}, bf16[8,192,128]{2,1,0:T(8,128)(2,1)S(1)}, u32[]{:S(2)}, u32[]{:S(2)}) collective-permute-start(bf16[8,192,128]{2,1,0:T(8,128)(2,1)S(1)} %constant_dynamic-update-slice_fusion.refs_1_), channel_id=1, source_target_pairs={{0,8},{8,0},{16,24},{24,16},{32,40},{40,32},{48,56},{56,48},{64,72... | collective-permute-start | bytes 1179656 | tf_op jit(solution)/shard_map/ppermute | solution.py:39
  68.6 7.9 %collective-permute-start.15 = (bf16[8,192,128]{2,1,0:T(8,128)(2,1)S(1)}, bf16[8,192,128]{2,1,0:T(8,128)(2,1)S(1)}, u32[]{:S(2)}, u32[]{:S(2)}) collective-permute-start(bf16[8,192,128]{2,1,0:T(8,128)(2,1)S(1)} %constant_dynamic-update-slice_fusion.8.refs_2_), channel_id=1, source_target_pairs={{0,8},{8,0},{16,24},{24,16},{32,40},{40,32},{48,56},{56,48},{64,72... | collective-permute-start | bytes 1179656 | tf_op jit(solution)/shard_map/ppermute | solution.py:39
  69.2 7.3 %collective-permute-start.16 = (bf16[8,192,128]{2,1,0:T(8,128)(2,1)S(1)}, bf16[8,192,128]{2,1,0:T(8,128)(2,1)S(1)}, u32[]{:S(2)}, u32[]{:S(2)}) collective-permute-start(bf16[8,192,128]{2,1,0:T(8,128)(2,1)S(1)} %constant_dynamic-update-slice_fusion.10.refs_3_), channel_id=1, source_target_pairs={{0,8},{8,0},{16,24},{24,16},{32,40},{40,32},{48,56},{56,48},{64,72... | collective-permute-start | bytes 1179656 | tf_op jit(solution)/shard_map/ppermute | solution.py:39
  76.5 1.7 %collective-permute-start.17 = (bf16[8,192,128]{2,1,0:T(8,128)(2,1)S(1)}, bf16[8,192,128]{2,1,0:T(8,128)(2,1)S(1)}, u32[]{:S(2)}, u32[]{:S(2)}) collective-permute-start(bf16[8,192,128]{2,1,0:T(8,128)(2,1)S(1)} %pad_maximum_fusion.refs_4_), channel_id=1, source_target_pairs={{0,8},{8,0},{16,24},{24,16},{32,40},{40,32},{48,56},{56,48},{64,72... | collective-permute-start | bytes 1179656 | tf_op jit(solution)/shard_map/ppermute | solution.py:39
  84.3 14.6 %all-to-all-start.1 = ((f32[8,96,128]{2,1,0:T(8,128)}), f32[8,96,128]{2,1,0:T(8,128)S(1)}, u32[]{:S(2)}, u32[]{:S(2)}) async-start(f32[8,96,128]{2,1,0:T(8,128)} %get-tuple-element.54), calls=%async_computation.1 | async-start | bytes 786432 | tf_op jit(solution)/shard_map/all_to_all | solution.py:441
  89.9 21.0 %collective-permute-start.18 = (f32[4,288,128]{2,1,0:T(8,128)S(1)}, f32[4,288,128]{2,1,0:T(8,128)S(1)}, u32[]{:S(2)}, u32[]{:S(2)}) collective-permute-start(f32[4,288,128]{2,1,0:T(8,128)S(1)} %get-tuple-element.49), channel_id=1, source_target_pairs={{0,4},{1,5},{2,6},{3,7},{4,0},{5,1},{6,2},{7,3},{8,12},{9,13},{10,... | collective-permute-start | bytes 1769480 | tf_op jit(solution)/shard_map/ppermute | solution.py:39
  100.0 21.8 %all-to-all-start.2 = ((f32[32,8,128]{2,1,0:T(8,128)}), f32[32,8,128]{2,1,0:T(8,128)S(1)}, u32[]{:S(2)}, u32[]{:S(2)}) async-start(f32[32,8,128]{2,1,0:T(8,128)} %bitcast.22), calls=%async_computation.2 | async-start | bytes 262144 | tf_op jit(solution)/shard_map/all_to_all | solution.py:448
  110.9 6.9 %collective-permute-start.19 = (f32[288,128]{1,0:T(8,128)S(1)}, f32[288,128]{1,0:T(8,128)S(1)}, u32[]{:S(2)}, u32[]{:S(2)}) collective-permute-start(f32[288,128]{1,0:T(8,128)S(1)} %get-tuple-element.51), channel_id=1, source_target_pairs={{0,3},{1,0},{2,1},{3,2},{4,7},{5,4},{6,5},{7,6},{8,11},{9,8},{10,9... | collective-permute-start | bytes 442376 | tf_op jit(solution)/shard_map/ppermute | solution.py:39
  113.9 7.9 %collective-permute-start.20 = (f32[288,128]{1,0:T(8,128)S(1)}, f32[288,128]{1,0:T(8,128)S(1)}, u32[]{:S(2)}, u32[]{:S(2)}) collective-permute-start(f32[288,128]{1,0:T(8,128)S(1)} %get-tuple-element.52), channel_id=1, source_target_pairs={{0,1},{1,2},{2,3},{3,0},{4,5},{5,6},{6,7},{7,4},{8,9},{9,10},{10,1... | collective-permute-start | bytes 442376 | tf_op jit(solution)/shard_map/ppermute | solution.py:39
  113.9 7.9 %collective-permute-start.21 = (f32[288,128]{1,0:T(8,128)S(1)}, f32[288,128]{1,0:T(8,128)S(1)}, u32[]{:S(2)}, u32[]{:S(2)}) collective-permute-start(f32[288,128]{1,0:T(8,128)S(1)} %get-tuple-element.53), channel_id=1, source_target_pairs={{0,2},{1,3},{2,0},{3,1},{4,6},{5,7},{6,4},{7,5},{8,10},{9,11},{10,... | collective-permute-start | bytes 442376 | tf_op jit(solution)/shard_map/ppermute | solution.py:39
  (11 other events, 88.2 us)

commit v5 on v4

--- a/solution.py
+++ b/solution.py
@@ -48,11 +48,6 @@
     other = turn(x, axis, -way)
     far = turn(near, axis, way)
     return [x, near, other, far] if way == 1 else [x, other, near, far]
-
-
-def gather_cols(x):
-    two = jnp.stack([x, turn(x, z_lo, 1)])
-    return [two] + [turn(two, y_axis, -offset) for offset in offsets[1:]]
 
 
 def to_column(x, rows, cols, per):
@@ -409,9 +404,11 @@
     near = around_digit(piece, z_hi)
     pair_near = jnp.stack([b[:block] for b in near])
     ph_near = jnp.stack([b[block:] for b in near])
-    around = gather_cols(longer)
+    two = jnp.stack([longer, turn(longer, z_lo, 1)])
     pair_own = around_ring(pair_near, x_axis, 1)
     ph_own = around_ring(ph_near, x_axis, -1)
+    pair_own[1], two = lax.optimization_barrier((pair_own[1], two))
+    around = around_digit(two, y_axis)
     joined = [jnp.concatenate(b) for b in zip(pair_own, ph_own)]
     joined[3], around = lax.optimization_barrier((joined[3], around))
     blocks = joined + [turn(b, core, 1) for b in joined]

time: 123 us -> 121 us (0.984)
  waiting for transfers between devices: 39.1 us -> 37.6 us
    all_to_all x1, starting transfers between devices: 5.52 us -> 3.94 us  [local(): sums_e = lax.all_to_all(parts_e, 'col', 0, 0)]
    all_to_all x1, starting transfers between devices: 5.04 us -> 6.56 us  [local(): returned = lax.all_to_all(back.reshape(rows, group, lanes), 'row', 0, 0)]
    ppermute x21, waiting for transfers between devices: 29.4 us -> 28 us  [turn(): return lax.ppermute(x, name, pairs)]
where the time goes in v5:
time: 121 us
  starting transfers between devices  49.7 us (41%)
  waiting for transfers between devices  37.6 us (31%)
  blocking collectives  18.9 us (16%)
  Pallas kernels  10.8 us (9%)
  local copies, waits for them, and re-layouts  2.44 us (2%)
    ppermute x21, starting transfers between devices, turn(): return lax.ppermute(x, name, pairs)  32.3 us
    ppermute x21, waiting for transfers between devices, turn(): return lax.ppermute(x, name, pairs)  28 us
    all_to_all x1, blocking collectives, local(): incoming = lax.all_to_all(leaving.reshape(rows, group, lanes), 'row', 0, 0)  18.9 us
    pallas_call x7, Pallas kernels, call(): pl.pallas_call(kernel, out_shape=[jax.ShapeDtypeStruct(s, d) for s, d in...  10.8 us
    all_to_all x1, waiting for transfers between devices, local(): sums_e = lax.all_to_all(parts_e, 'col', 0, 0)  7.02 us
    ppermute x1, starting transfers between devices, to_column(): return lax.ppermute(x, both, pairs)  6.87 us
    all_to_all x1, starting transfers between devices, local(): returned = lax.all_to_all(back.reshape(rows, group, lanes), 'row', 0, 0)  6.56 us
    all_to_all x1, starting transfers between devices, local(): sums_e = lax.all_to_all(parts_e, 'col', 0, 0)  3.94 us
  transfers between devices with their start and end apart: 24, of which 11 were waited for; matrix products, arithmetic and copies ran while one was open for 0% of the time, Pallas kernels for 1%

profile of v5, /device:TPU:64, one launch (start us, length us, event | category | flops | bytes accessed | tf_op | source)
XLA Modules:
  0.0 120.5 jit_solution(7116917933567892350)
XLA Ops:
  1.4 3.0 %routes.1 = (bf16[256,128]{1,0:T(8,128)(2,1)}, bf16[2,192,128]{2,1,0:T(8,128)(2,1)}, bf16[192,256]{1,0:T(8,128)(2,1)}, bf16[192,256]{1,0:T(8,128)(2,1)}, bf16[25...) custom-call(s32[5]{0:T(128)} %stack.62.place.refs_0_, s32[48,128]{1,0:T(8,128)} %bitcast.61, ...), custom_call_target="tpu_custom_call" | custom-call | tf_op jit(solution)/shard_map/routes/pallas_call | solution.py:342
  4.3 18.9 %all_to_all.15 = bf16[32,8,128]{2,1,0:T(8,128)(2,1)S(1)} all-to-all(bf16[32,8,128]{2,1,0:T(8,128)(2,1)} %bitcast.57), channel_id=1, replica_groups=mesh['row'=32,'col'=8] {'row'}, dimensions={0} | all-to-all | bytes 131072 | tf_op jit(solution)/shard_map/all_to_all | solution.py:394
  24.3 6.9 %collective-permute-start = (bf16[384,128]{1,0:T(8,128)(2,1)S(1)}, bf16[384,128]{1,0:T(8,128)(2,1)S(1)}, u32[]{:S(2)}, u32[]{:S(2)}) collective-permute-start(bf16[384,128]{1,0:T(8,128)(2,1)S(1)} %get-tuple-element.37), channel_id=1, source_target_pairs={{0,0},{1,8},{2,16},{3,24},{4,32},{5,40},{6,48},{7,56},{8,64},{9,72... | collective-permute-start | bytes 294920 | tf_op jit(solution)/shard_map/ppermute | solution.py:58
  31.2 2.0 %collective-permute-start.5 = (bf16[400,128]{1,0:T(8,128)(2,1)S(1)}, bf16[400,128]{1,0:T(8,128)(2,1)S(1)}, u32[]{:S(2)}, u32[]{:S(2)}) collective-permute-start(bf16[400,128]{1,0:T(8,128)(2,1)S(1)} %get-tuple-element.38), channel_id=1, source_target_pairs={{0,4},{1,5},{2,6},{3,7},{4,0},{5,1},{6,2},{7,3},{8,12},{9,13},{10,... | collective-permute-start | bytes 307208 | tf_op jit(solution)/shard_map/ppermute | solution.py:39
  33.2 2.6 %collective-permute-done = bf16[384,128]{1,0:T(8,128)(2,1)S(1)} collective-permute-done((bf16[384,128]{1,0:T(8,128)(2,1)S(1)}, bf16[384,128]{1,0:T(8,128)(2,1)S(1)}, u32[]{:S(2)}, u32[]{:S(2)}) %collective-permute-start) | collective-permute-done | bytes 98336 | tf_op jit(solution)/shard_map/ppermute | solution.py:58
  39.6 2.3 %collective-permute-start.1 = (bf16[384,128]{1,0:T(8,128)(2,1)S(1)}, bf16[384,128]{1,0:T(8,128)(2,1)S(1)}, u32[]{:S(2)}, u32[]{:S(2)}) collective-permute-start(bf16[384,128]{1,0:T(8,128)(2,1)S(1)} %collective-permute-done), channel_id=1, source_target_pairs={{0,64},{8,72},{16,80},{24,88},{32,96},{40,104},{48,112},{56,120},{... | collective-permute-start | bytes 294920 | tf_op jit(solution)/shard_map/ppermute | solution.py:39
  41.9 2.9 %collective-permute-done.3 = bf16[384,128]{1,0:T(8,128)(2,1)S(1)} collective-permute-done((bf16[384,128]{1,0:T(8,128)(2,1)S(1)}, bf16[384,128]{1,0:T(8,128)(2,1)S(1)}, u32[]{:S(2)}, u32[]{:S(2)}) %collective-permute-start.3) | collective-permute-done | bytes 98336 | tf_op jit(solution)/shard_map/ppermute | solution.py:39
  44.9 4.2 %collective-permute-done.2 = bf16[384,128]{1,0:T(8,128)(2,1)S(1)} collective-permute-done((bf16[384,128]{1,0:T(8,128)(2,1)S(1)}, bf16[384,128]{1,0:T(8,128)(2,1)S(1)}, u32[]{:S(2)}, u32[]{:S(2)}) %collective-permute-start.2) | collective-permute-done | bytes 98336 | tf_op jit(solution)/shard_map/ppermute | solution.py:39
  51.3 2.8 %collective-permute-start.8 = (bf16[4,192,128]{2,1,0:T(8,128)(2,1)S(1)}, bf16[4,192,128]{2,1,0:T(8,128)(2,1)S(1)}, u32[]{:S(2)}, u32[]{:S(2)}) collective-permute-start(bf16[4,192,128]{2,1,0:T(8,128)(2,1)S(1)} %pad_maximum_fusion.3), channel_id=1, source_target_pairs={{0,48},{8,56},{16,0},{24,8},{32,16},{40,24},{48,32},{56,40},{64,11... | collective-permute-start | bytes 589832 | tf_op jit(solution)/shard_map/ppermute | solution.py:39
  54.2 5.5 %collective-permute-done.4 = bf16[4,192,128]{2,1,0:T(8,128)(2,1)S(1)} collective-permute-done((bf16[4,192,128]{2,1,0:T(8,128)(2,1)S(1)}, bf16[4,192,128]{2,1,0:T(8,128)(2,1)S(1)}, u32[]{:S(2)}, u32[]{:S(2)}) %collective-permute-start.4) | collective-permute-done | bytes 196640 | tf_op jit(solution)/shard_map/ppermute | solution.py:39
  59.7 6.2 %collective-permute-start.13 = (bf16[2,400,128]{2,1,0:T(8,128)(2,1)S(1)}, bf16[2,400,128]{2,1,0:T(8,128)(2,1)S(1)}, u32[]{:S(2)}, u32[]{:S(2)}) collective-permute-start(bf16[2,400,128]{2,1,0:T(8,128)(2,1)S(1)} %pad_maximum_fusion.1.refs_9_), channel_id=1, source_target_pairs={{0,2},{1,3},{2,0},{3,1},{4,6},{5,7},{6,4},{7,5},{8,10},{9,11},{10,... | collective-permute-start | bytes 614408 | tf_op jit(solution)/shard_map/ppermute | solution.py:39
  66.0 3.2 %collective-permute-start.10 = (bf16[4,192,128]{2,1,0:T(8,128)(2,1)S(1)}, bf16[4,192,128]{2,1,0:T(8,128)(2,1)S(1)}, u32[]{:S(2)}, u32[]{:S(2)}) collective-permute-start(bf16[4,192,128]{2,1,0:T(8,128)(2,1)S(1)} %collective-permute-done.8), channel_id=1, source_target_pairs={{0,48},{8,56},{16,0},{24,8},{32,16},{40,24},{48,32},{56,40},{64,11... | collective-permute-start | bytes 589832 | tf_op jit(solution)/shard_map/ppermute | solution.py:39
  69.3 2.1 %collective-permute-start.11 = (bf16[2,400,128]{2,1,0:T(8,128)(2,1)S(1)}, bf16[2,400,128]{2,1,0:T(8,128)(2,1)S(1)}, u32[]{:S(2)}, u32[]{:S(2)}) collective-permute-start(bf16[2,400,128]{2,1,0:T(8,128)(2,1)S(1)} %pad_maximum_fusion.1.refs_9_), channel_id=1, source_target_pairs={{0,1},{1,2},{2,3},{3,0},{4,5},{5,6},{6,7},{7,4},{8,9},{9,10},{10,1... | collective-permute-start | bytes 614408 | tf_op jit(solution)/shard_map/ppermute | solution.py:39
  73.6 2.8 %collective-permute-done.11.refs_10_ = bf16[2,400,128]{2,1,0:T(8,128)(2,1)S(1)} collective-permute-done((bf16[2,400,128]{2,1,0:T(8,128)(2,1)S(1)}, bf16[2,400,128]{2,1,0:T(8,128)(2,1)S(1)}, u32[]{:S(2)}, u32[]{:S(2)}) %collective-permute-start.11) | collective-permute-done | bytes 204832 | tf_op jit(solution)/shard_map/ppermute | solution.py:39
  78.8 3.0 %weights_g.1 = (f32[8,96,128]{2,1,0:T(8,128)}, f32[8,96,128]{2,1,0:T(8,128)S(1)}, f32[192,1]{1,0:T(8,128)S(1)}) custom-call(s32[5]{0:T(128)S(1)} %copy-done.9, bf16[8,192,128]{2,1,0:T(8,128)(2,1)S(1)} %constant_dynamic-update-slice_fusion.refs_1_, bf16[8,192,128]{2,1,0:T(8,128)(2,1)S(1)} %constant_dynamic-update-slice_fusion.8.refs_2_, ...), custom_call_target="tpu_custom_call" | custom-call | tf_op jit(solution)/shard_map/weights_g/pallas_call | solution.py:342
  81.7 2.5 %weights_q.1 = (f32[4,288,128]{2,1,0:T(8,128)S(1)}, f32[4,288,128]{2,1,0:T(8,128)S(1)}) custom-call(s32[5]{0:T(128)S(1)} %copy-done.9, bf16[8,192,128]{2,1,0:T(8,128)(2,1)S(1)} %constant_dynamic-update-slice_fusion.refs_1_, bf16[8,192,128]{2,1,0:T(8,128)(2,1)S(1)} %constant_dynamic-update-slice_fusion.8.refs_2_, ...), custom_call_target="tpu_custom_call" | custom-call | tf_op jit(solution)/shard_map/weights_q/pallas_call | solution.py:342
  84.2 3.9 %all-to-all-start.1 = ((f32[8,96,128]{2,1,0:T(8,128)}), f32[8,96,128]{2,1,0:T(8,128)S(1)}, u32[]{:S(2)}, u32[]{:S(2)}) async-start(f32[8,96,128]{2,1,0:T(8,128)} %get-tuple-element.58), calls=%async_computation.1 | async-start | bytes 786432 | tf_op jit(solution)/shard_map/all_to_all | solution.py:438
  88.2 2.0 %collective-permute-start.18 = (f32[4,288,128]{2,1,0:T(8,128)S(1)}, f32[4,288,128]{2,1,0:T(8,128)S(1)}, u32[]{:S(2)}, u32[]{:S(2)}) collective-permute-start(f32[4,288,128]{2,1,0:T(8,128)S(1)} %get-tuple-element.53), channel_id=1, source_target_pairs={{0,4},{1,5},{2,6},{3,7},{4,0},{5,1},{6,2},{7,3},{8,12},{9,13},{10,... | collective-permute-start | bytes 1769480 | tf_op jit(solution)/shard_map/ppermute | solution.py:39
  90.2 7.0 %all-to-all-done.1.parts = f32[8,96,128]{2,1,0:T(8,128)S(1)} async-done(((f32[8,96,128]{2,1,0:T(8,128)}), f32[8,96,128]{2,1,0:T(8,128)S(1)}, u32[]{:S(2)}, u32[]{:S(2)}) %all-to-all-start.1) | async-done | bytes 393248 | tf_op jit(solution)/shard_map/all_to_all | solution.py:438
  98.3 6.6 %all-to-all-start.2 = ((f32[32,8,128]{2,1,0:T(8,128)}), f32[32,8,128]{2,1,0:T(8,128)S(1)}, u32[]{:S(2)}, u32[]{:S(2)}) async-start(f32[32,8,128]{2,1,0:T(8,128)} %bitcast.22), calls=%async_computation.2 | async-start | bytes 262144 | tf_op jit(solution)/shard_map/all_to_all | solution.py:445
  104.9 3.5 %collective-permute-done.18.came = f32[4,288,128]{2,1,0:T(8,128)S(1)} collective-permute-done((f32[4,288,128]{2,1,0:T(8,128)S(1)}, f32[4,288,128]{2,1,0:T(8,128)S(1)}, u32[]{:S(2)}, u32[]{:S(2)}) %collective-permute-start.18) | collective-permute-done | bytes 589856 | tf_op jit(solution)/shard_map/ppermute | solution.py:39
  108.5 2.8 %collective-permute-start.19 = (f32[288,128]{1,0:T(8,128)S(1)}, f32[288,128]{1,0:T(8,128)S(1)}, u32[]{:S(2)}, u32[]{:S(2)}) collective-permute-start(f32[288,128]{1,0:T(8,128)S(1)} %get-tuple-element.55), channel_id=1, source_target_pairs={{0,3},{1,0},{2,1},{3,2},{4,7},{5,4},{6,5},{7,6},{8,11},{9,8},{10,9... | collective-permute-start | bytes 442376 | tf_op jit(solution)/shard_map/ppermute | solution.py:39
  111.3 2.3 %collective-permute-start.21 = (f32[288,128]{1,0:T(8,128)S(1)}, f32[288,128]{1,0:T(8,128)S(1)}, u32[]{:S(2)}, u32[]{:S(2)}) collective-permute-start(f32[288,128]{1,0:T(8,128)S(1)} %get-tuple-element.57), channel_id=1, source_target_pairs={{0,2},{1,3},{2,0},{3,1},{4,6},{5,7},{6,4},{7,5},{8,10},{9,11},{10,... | collective-permute-start | bytes 442376 | tf_op jit(solution)/shard_map/ppermute | solution.py:39
  115.5 3.9 %collective-permute-done.20.p2 = f32[288,128]{1,0:T(8,128)S(1)} collective-permute-done((f32[288,128]{1,0:T(8,128)S(1)}, f32[288,128]{1,0:T(8,128)S(1)}, u32[]{:S(2)}, u32[]{:S(2)}) %collective-permute-start.20) | collective-permute-done | bytes 147488 | tf_op jit(solution)/shard_map/ppermute | solution.py:39
  (75 shorter events, 16.7 us)
Async XLA Ops:
  24.3 11.5 %collective-permute-start = (bf16[384,128]{1,0:T(8,128)(2,1)S(1)}, bf16[384,128]{1,0:T(8,128)(2,1)S(1)}, u32[]{:S(2)}, u32[]{:S(2)}) collective-permute-start(bf16[384,128]{1,0:T(8,128)(2,1)S(1)} %get-tuple-element.37), channel_id=1, source_target_pairs={{0,0},{1,8},{2,16},{3,24},{4,32},{5,40},{6,48},{7,56},{8,64},{9,72... | collective-permute-start | bytes 294920 | tf_op jit(solution)/shard_map/ppermute | solution.py:58
  31.2 10.7 %collective-permute-start.5 = (bf16[400,128]{1,0:T(8,128)(2,1)S(1)}, bf16[400,128]{1,0:T(8,128)(2,1)S(1)}, u32[]{:S(2)}, u32[]{:S(2)}) collective-permute-start(bf16[400,128]{1,0:T(8,128)(2,1)S(1)} %get-tuple-element.38), channel_id=1, source_target_pairs={{0,4},{1,5},{2,6},{3,7},{4,0},{5,1},{6,2},{7,3},{8,12},{9,13},{10,... | collective-permute-start | bytes 307208 | tf_op jit(solution)/shard_map/ppermute | solution.py:39
  35.8 9.0 %collective-permute-start.3 = (bf16[384,128]{1,0:T(8,128)(2,1)S(1)}, bf16[384,128]{1,0:T(8,128)(2,1)S(1)}, u32[]{:S(2)}, u32[]{:S(2)}) collective-permute-start(bf16[384,128]{1,0:T(8,128)(2,1)S(1)} %collective-permute-done), channel_id=1, source_target_pairs={{0,128},{8,136},{16,144},{24,152},{32,160},{40,168},{48,176},{56,1... | collective-permute-start | bytes 294920 | tf_op jit(solution)/shard_map/ppermute | solution.py:39
  37.8 11.3 %collective-permute-start.2 = (bf16[384,128]{1,0:T(8,128)(2,1)S(1)}, bf16[384,128]{1,0:T(8,128)(2,1)S(1)}, u32[]{:S(2)}, u32[]{:S(2)}) collective-permute-start(bf16[384,128]{1,0:T(8,128)(2,1)S(1)} %collective-permute-done), channel_id=1, source_target_pairs={{0,192},{8,200},{16,208},{24,216},{32,224},{40,232},{48,240},{56,2... | collective-permute-start | bytes 294920 | tf_op jit(solution)/shard_map/ppermute | solution.py:39
  39.6 9.5 %collective-permute-start.1 = (bf16[384,128]{1,0:T(8,128)(2,1)S(1)}, bf16[384,128]{1,0:T(8,128)(2,1)S(1)}, u32[]{:S(2)}, u32[]{:S(2)}) collective-permute-start(bf16[384,128]{1,0:T(8,128)(2,1)S(1)} %collective-permute-done), channel_id=1, source_target_pairs={{0,64},{8,72},{16,80},{24,88},{32,96},{40,104},{48,112},{56,120},{... | collective-permute-start | bytes 294920 | tf_op jit(solution)/shard_map/ppermute | solution.py:39
  49.1 16.8 %collective-permute-start.7 = (bf16[4,192,128]{2,1,0:T(8,128)(2,1)S(1)}, bf16[4,192,128]{2,1,0:T(8,128)(2,1)S(1)}, u32[]{:S(2)}, u32[]{:S(2)}) collective-permute-start(bf16[4,192,128]{2,1,0:T(8,128)(2,1)S(1)} %pad_maximum_fusion.2), channel_id=1, source_target_pairs={{0,48},{8,56},{16,0},{24,8},{32,16},{40,24},{48,32},{56,40},{64,11... | collective-permute-start | bytes 589832 | tf_op jit(solution)/shard_map/ppermute | solution.py:39
  50.7 9.0 %collective-permute-start.4 = (bf16[4,192,128]{2,1,0:T(8,128)(2,1)S(1)}, bf16[4,192,128]{2,1,0:T(8,128)(2,1)S(1)}, u32[]{:S(2)}, u32[]{:S(2)}) collective-permute-start(bf16[4,192,128]{2,1,0:T(8,128)(2,1)S(1)} %pad_maximum_fusion.2), channel_id=1, source_target_pairs={{0,16},{8,24},{16,32},{24,40},{32,48},{40,56},{48,0},{56,8},{64,80... | collective-permute-start | bytes 589832 | tf_op jit(solution)/shard_map/ppermute | solution.py:39
  51.3 14.8 %collective-permute-start.8 = (bf16[4,192,128]{2,1,0:T(8,128)(2,1)S(1)}, bf16[4,192,128]{2,1,0:T(8,128)(2,1)S(1)}, u32[]{:S(2)}, u32[]{:S(2)}) collective-permute-start(bf16[4,192,128]{2,1,0:T(8,128)(2,1)S(1)} %pad_maximum_fusion.3), channel_id=1, source_target_pairs={{0,48},{8,56},{16,0},{24,8},{32,16},{40,24},{48,32},{56,40},{64,11... | collective-permute-start | bytes 589832 | tf_op jit(solution)/shard_map/ppermute | solution.py:39
  54.0 15.3 %collective-permute-start.6 = (bf16[4,192,128]{2,1,0:T(8,128)(2,1)S(1)}, bf16[4,192,128]{2,1,0:T(8,128)(2,1)S(1)}, u32[]{:S(2)}, u32[]{:S(2)}) collective-permute-start(bf16[4,192,128]{2,1,0:T(8,128)(2,1)S(1)} %pad_maximum_fusion.3), channel_id=1, source_target_pairs={{0,16},{8,24},{16,32},{24,40},{32,48},{40,56},{48,0},{56,8},{64,80... | collective-permute-start | bytes 589832 | tf_op jit(solution)/shard_map/ppermute | solution.py:39
  59.7 13.8 %collective-permute-start.13 = (bf16[2,400,128]{2,1,0:T(8,128)(2,1)S(1)}, bf16[2,400,128]{2,1,0:T(8,128)(2,1)S(1)}, u32[]{:S(2)}, u32[]{:S(2)}) collective-permute-start(bf16[2,400,128]{2,1,0:T(8,128)(2,1)S(1)} %pad_maximum_fusion.1.refs_9_), channel_id=1, source_target_pairs={{0,2},{1,3},{2,0},{3,1},{4,6},{5,7},{6,4},{7,5},{8,10},{9,11},{10,... | collective-permute-start | bytes 614408 | tf_op jit(solution)/shard_map/ppermute | solution.py:39
  65.9 7.7 %collective-permute-start.12 = (bf16[2,400,128]{2,1,0:T(8,128)(2,1)S(1)}, bf16[2,400,128]{2,1,0:T(8,128)(2,1)S(1)}, u32[]{:S(2)}, u32[]{:S(2)}) collective-permute-start(bf16[2,400,128]{2,1,0:T(8,128)(2,1)S(1)} %pad_maximum_fusion.1.refs_9_), channel_id=1, source_target_pairs={{0,3},{1,0},{2,1},{3,2},{4,7},{5,4},{6,5},{7,6},{8,11},{9,8},{10,9... | collective-permute-start | bytes 614408 | tf_op jit(solution)/shard_map/ppermute | solution.py:39
  65.9 7.0 %collective-permute-start.9 = (bf16[4,192,128]{2,1,0:T(8,128)(2,1)S(1)}, bf16[4,192,128]{2,1,0:T(8,128)(2,1)S(1)}, u32[]{:S(2)}, u32[]{:S(2)}) collective-permute-start(bf16[4,192,128]{2,1,0:T(8,128)(2,1)S(1)} %collective-permute-done.4), channel_id=1, source_target_pairs={{0,16},{8,24},{16,32},{24,40},{32,48},{40,56},{48,0},{56,8},{64,80... | collective-permute-start | bytes 589832 | tf_op jit(solution)/shard_map/ppermute | solution.py:39
  66.0 6.9 %collective-permute-start.10 = (bf16[4,192,128]{2,1,0:T(8,128)(2,1)S(1)}, bf16[4,192,128]{2,1,0:T(8,128)(2,1)S(1)}, u32[]{:S(2)}, u32[]{:S(2)}) collective-permute-start(bf16[4,192,128]{2,1,0:T(8,128)(2,1)S(1)} %collective-permute-done.8), channel_id=1, source_target_pairs={{0,48},{8,56},{16,0},{24,8},{32,16},{40,24},{48,32},{56,40},{64,11... | collective-permute-start | bytes 589832 | tf_op jit(solution)/shard_map/ppermute | solution.py:39
  69.3 7.0 %collective-permute-start.11 = (bf16[2,400,128]{2,1,0:T(8,128)(2,1)S(1)}, bf16[2,400,128]{2,1,0:T(8,128)(2,1)S(1)}, u32[]{:S(2)}, u32[]{:S(2)}) collective-permute-start(bf16[2,400,128]{2,1,0:T(8,128)(2,1)S(1)} %pad_maximum_fusion.1.refs_9_), channel_id=1, source_target_pairs={{0,1},{1,2},{2,3},{3,0},{4,5},{5,6},{6,7},{7,4},{8,9},{9,10},{10,1... | collective-permute-start | bytes 614408 | tf_op jit(solution)/shard_map/ppermute | solution.py:39
  72.9 3.5 %collective-permute-start.14 = (bf16[8,192,128]{2,1,0:T(8,128)(2,1)S(1)}, bf16[8,192,128]{2,1,0:T(8,128)(2,1)S(1)}, u32[]{:S(2)}, u32[]{:S(2)}) collective-permute-start(bf16[8,192,128]{2,1,0:T(8,128)(2,1)S(1)} %constant_dynamic-update-slice_fusion.refs_1_), channel_id=1, source_target_pairs={{0,8},{8,0},{16,24},{24,16},{32,40},{40,32},{48,56},{56,48},{64,72... | collective-permute-start | bytes 1179656 | tf_op jit(solution)/shard_map/ppermute | solution.py:39
  72.9 3.5 %collective-permute-start.15 = (bf16[8,192,128]{2,1,0:T(8,128)(2,1)S(1)}, bf16[8,192,128]{2,1,0:T(8,128)(2,1)S(1)}, u32[]{:S(2)}, u32[]{:S(2)}) collective-permute-start(bf16[8,192,128]{2,1,0:T(8,128)(2,1)S(1)} %constant_dynamic-update-slice_fusion.8.refs_2_), channel_id=1, source_target_pairs={{0,8},{8,0},{16,24},{24,16},{32,40},{40,32},{48,56},{56,48},{64,72... | collective-permute-start | bytes 1179656 | tf_op jit(solution)/shard_map/ppermute | solution.py:39
  73.5 2.9 %collective-permute-start.16 = (bf16[8,192,128]{2,1,0:T(8,128)(2,1)S(1)}, bf16[8,192,128]{2,1,0:T(8,128)(2,1)S(1)}, u32[]{:S(2)}, u32[]{:S(2)}) collective-permute-start(bf16[8,192,128]{2,1,0:T(8,128)(2,1)S(1)} %constant_dynamic-update-slice_fusion.10.refs_3_), channel_id=1, source_target_pairs={{0,8},{8,0},{16,24},{24,16},{32,40},{40,32},{48,56},{56,48},{64,72... | collective-permute-start | bytes 1179656 | tf_op jit(solution)/shard_map/ppermute | solution.py:39
  76.4 1.7 %collective-permute-start.17 = (bf16[8,192,128]{2,1,0:T(8,128)(2,1)S(1)}, bf16[8,192,128]{2,1,0:T(8,128)(2,1)S(1)}, u32[]{:S(2)}, u32[]{:S(2)}) collective-permute-start(bf16[8,192,128]{2,1,0:T(8,128)(2,1)S(1)} %pad_maximum_fusion.refs_4_), channel_id=1, source_target_pairs={{0,8},{8,0},{16,24},{24,16},{32,40},{40,32},{48,56},{56,48},{64,72... | collective-permute-start | bytes 1179656 | tf_op jit(solution)/shard_map/ppermute | solution.py:39
  84.2 13.0 %all-to-all-start.1 = ((f32[8,96,128]{2,1,0:T(8,128)}), f32[8,96,128]{2,1,0:T(8,128)S(1)}, u32[]{:S(2)}, u32[]{:S(2)}) async-start(f32[8,96,128]{2,1,0:T(8,128)} %get-tuple-element.58), calls=%async_computation.1 | async-start | bytes 786432 | tf_op jit(solution)/shard_map/all_to_all | solution.py:438
  88.2 20.2 %collective-permute-start.18 = (f32[4,288,128]{2,1,0:T(8,128)S(1)}, f32[4,288,128]{2,1,0:T(8,128)S(1)}, u32[]{:S(2)}, u32[]{:S(2)}) collective-permute-start(f32[4,288,128]{2,1,0:T(8,128)S(1)} %get-tuple-element.53), channel_id=1, source_target_pairs={{0,4},{1,5},{2,6},{3,7},{4,0},{5,1},{6,2},{7,3},{8,12},{9,13},{10,... | collective-permute-start | bytes 1769480 | tf_op jit(solution)/shard_map/ppermute | solution.py:39
  98.3 21.1 %all-to-all-start.2 = ((f32[32,8,128]{2,1,0:T(8,128)}), f32[32,8,128]{2,1,0:T(8,128)S(1)}, u32[]{:S(2)}, u32[]{:S(2)}) async-start(f32[32,8,128]{2,1,0:T(8,128)} %bitcast.22), calls=%async_computation.2 | async-start | bytes 262144 | tf_op jit(solution)/shard_map/all_to_all | solution.py:445
  108.5 7.1 %collective-permute-start.19 = (f32[288,128]{1,0:T(8,128)S(1)}, f32[288,128]{1,0:T(8,128)S(1)}, u32[]{:S(2)}, u32[]{:S(2)}) collective-permute-start(f32[288,128]{1,0:T(8,128)S(1)} %get-tuple-element.55), channel_id=1, source_target_pairs={{0,3},{1,0},{2,1},{3,2},{4,7},{5,4},{6,5},{7,6},{8,11},{9,8},{10,9... | collective-permute-start | bytes 442376 | tf_op jit(solution)/shard_map/ppermute | solution.py:39
  111.3 8.2 %collective-permute-start.20 = (f32[288,128]{1,0:T(8,128)S(1)}, f32[288,128]{1,0:T(8,128)S(1)}, u32[]{:S(2)}, u32[]{:S(2)}) collective-permute-start(f32[288,128]{1,0:T(8,128)S(1)} %get-tuple-element.56), channel_id=1, source_target_pairs={{0,1},{1,2},{2,3},{3,0},{4,5},{5,6},{6,7},{7,4},{8,9},{9,10},{10,1... | collective-permute-start | bytes 442376 | tf_op jit(solution)/shard_map/ppermute | solution.py:39
  111.3 8.2 %collective-permute-start.21 = (f32[288,128]{1,0:T(8,128)S(1)}, f32[288,128]{1,0:T(8,128)S(1)}, u32[]{:S(2)}, u32[]{:S(2)}) collective-permute-start(f32[288,128]{1,0:T(8,128)S(1)} %get-tuple-element.57), channel_id=1, source_target_pairs={{0,2},{1,3},{2,0},{3,1},{4,6},{5,7},{6,4},{7,5},{8,10},{9,11},{10,... | collective-permute-start | bytes 442376 | tf_op jit(solution)/shard_map/ppermute | solution.py:39
  (11 other events, 74.5 us)

commit v6 on v5

--- a/solution.py
+++ b/solution.py
@@ -54,7 +54,9 @@
     pairs = []
     for r in range(rows):
         for c in range(cols):
-            pairs.append((r * cols + c, ((r % per) * cols + c) * cols + r // per))
+            x_here = r // 2 % 4
+            x_there = x_here if c % 2 == 0 else 3 - x_here
+            pairs.append((r * cols + c, (c // 2 * 8 + x_there * 2 + r % 2) * cols + r // per))
     return lax.ppermute(x, both, pairs)
 
 
@@ -249,15 +251,21 @@
     return ((place[4] + offsets[y_place]) & 3) + (((place[4] >> 2) + z_place) & 1) * 4
 
 
-def fill(place, blocks, around, second, right, left, by_col):
+def fill(place, blocks, around, second, right, left, by_col, apart):
     block = left.shape[0]
     base = second * block
     zh, xx, cc = place[0], place[1], place[2]
-    ids = [((xx + o) & 3) * 2 + other for other in (cc, 1 - cc) for o in offsets]
+    ids = [((zh + o) & 3) * 2 + b for o in offsets for b in range(2)]
     for k, source in enumerate(blocks):
-        for z_place, o in enumerate(offsets):
-            rows = pl.ds(pl.multiple_of(((zh + o) & 3) * block, block), block)
-            right[rows, k * lanes : (k + 1) * lanes] = source[second * 4 + z_place]
+        x = (xx + offsets[k % 4]) & 3
+        other = cc if k < 4 else 1 - cc
+        mirrored = jnp.where((x >> 1) == (place[4] & 1), 0, 1)
+        j = (jnp.where(mirrored == 0, x, 3 - x) & 1) * 2 + other
+        rows = pl.ds(pl.multiple_of(j * block, block), block)
+        for z_place in range(4):
+            apart[z_place * 2 + mirrored, rows, :] = source[second * 4 + z_place]
+    for k in range(len(ids)):
+        right[:, k * lanes : (k + 1) * lanes] = apart[k]
     for y_place, source in enumerate(around):
         for z_place in range(2):
             by_col[column_at(place, y_place, z_place)] = source[z_place, base : base + block]
@@ -269,9 +277,9 @@
 def g_kernel(*refs):
     place, *blocks = refs[:9]
     around = refs[9:13]
-    multiplier, segments, ph_segments, lengths, out, more, scale, right, left, by_col = refs[13:]
+    multiplier, segments, ph_segments, lengths, out, more, scale, right, left, by_col, apart = refs[13:]
     block, width = multiplier.shape
-    ids = fill(place, blocks, around, 1, right, left, by_col)
+    ids = fill(place, blocks, around, 1, right, left, by_col, apart)
     sums = jnp.zeros((extra, lanes), f32)
     for source in around:
         for z_place in range(2):
@@ -298,9 +306,9 @@
 def q_kernel(*refs):
     place, *blocks = refs[:9]
     around = refs[9:13]
-    multiplier, hamiltonian, more, keep, away, right, left, by_col, by_col_out = refs[13:]
+    multiplier, hamiltonian, more, keep, away, right, left, by_col, apart, by_col_out = refs[13:]
     block, width = multiplier.shape
-    ids = fill(place, blocks, around, 0, right, left, by_col)
+    ids = fill(place, blocks, around, 0, right, left, by_col, apart)
     gram = transposed_dot(left[...], right[...])
     resid = jnp.where(diagonal_of(place, multiplier.shape), shift_value, 0.0) - gram
     weight = (multiplier[...].astype(f32) + penalty * resid).astype(bf16)
@@ -416,6 +424,7 @@
         ((width, cols * lanes), bf16),
         ((block, cols * lanes), bf16),
         ((cols, block, lanes), bf16),
+        ((cols, width, lanes), bf16),
     ]
     parts_e, parts_f, scale = call(
         g_kernel,

time: 121 us -> 121 us (level)
    ppermute x21, starting transfers between devices: 32.3 us -> 33.9 us  [turn(): return lax.ppermute(x, name, pairs)]
    ppermute x1, waiting for transfers between devices: 2.62 us -> 4.17 us  [to_column(): return lax.ppermute(x, both, pairs)]
    all_to_all x1, starting transfers between devices: 6.56 us -> 5.26 us  [local(): returned = lax.all_to_all(back.reshape(rows, group, lanes), 'row', 0, 0)]
where the time goes in v6:
time: 121 us
  starting transfers between devices  49.6 us (41%)
  waiting for transfers between devices  38 us (31%)
  blocking collectives  18.9 us (16%)
  Pallas kernels  10.7 us (9%)
  local copies, waits for them, and re-layouts  2.44 us (2%)
    ppermute x21, starting transfers between devices, turn(): return lax.ppermute(x, name, pairs)  33.9 us
    ppermute x21, waiting for transfers between devices, turn(): return lax.ppermute(x, name, pairs)  26.8 us
    all_to_all x1, blocking collectives, local(): incoming = lax.all_to_all(leaving.reshape(rows, group, lanes), 'row', 0, 0)  18.9 us
    pallas_call x7, Pallas kernels, call(): pl.pallas_call(kernel, out_shape=[jax.ShapeDtypeStruct(s, d) for s, d in...  10.7 us
    all_to_all x1, waiting for transfers between devices, local(): sums_e = lax.all_to_all(parts_e, 'col', 0, 0)  7.05 us
    ppermute x1, starting transfers between devices, to_column(): return lax.ppermute(x, both, pairs)  6.87 us
    all_to_all x1, starting transfers between devices, local(): returned = lax.all_to_all(back.reshape(rows, group, lanes), 'row', 0, 0)  5.26 us
    ppermute x1, waiting for transfers between devices, to_column(): return lax.ppermute(x, both, pairs)  4.17 us
  transfers between devices with their start and end apart: 24, of which 11 were waited for; matrix products, arithmetic and copies ran while one was open for 0% of the time, Pallas kernels for 1%

profile of v6, /device:TPU:64, one launch (start us, length us, event | category | flops | bytes accessed | tf_op | source)
XLA Modules:
  0.0 120.7 jit_solution(5823624047255246929)
XLA Ops:
  1.4 3.0 %routes.1 = (bf16[256,128]{1,0:T(8,128)(2,1)}, bf16[2,192,128]{2,1,0:T(8,128)(2,1)}, bf16[192,256]{1,0:T(8,128)(2,1)}, bf16[192,256]{1,0:T(8,128)(2,1)}, bf16[25...) custom-call(s32[5]{0:T(128)} %stack.62.place.refs_0_, s32[48,128]{1,0:T(8,128)} %bitcast.61, ...), custom_call_target="tpu_custom_call" | custom-call | tf_op jit(solution)/shard_map/routes/pallas_call | solution.py:350
  4.3 18.9 %all_to_all.15 = bf16[32,8,128]{2,1,0:T(8,128)(2,1)S(1)} all-to-all(bf16[32,8,128]{2,1,0:T(8,128)(2,1)} %bitcast.57), channel_id=1, replica_groups=mesh['row'=32,'col'=8] {'row'}, dimensions={0} | all-to-all | bytes 131072 | tf_op jit(solution)/shard_map/all_to_all | solution.py:402
  24.3 6.9 %collective-permute-start = (bf16[384,128]{1,0:T(8,128)(2,1)S(1)}, bf16[384,128]{1,0:T(8,128)(2,1)S(1)}, u32[]{:S(2)}, u32[]{:S(2)}) collective-permute-start(bf16[384,128]{1,0:T(8,128)(2,1)S(1)} %get-tuple-element.37), channel_id=1, source_target_pairs={{0,0},{1,48},{2,64},{3,112},{4,128},{5,176},{6,192},{7,240},{8,8},... | collective-permute-start | bytes 294920 | tf_op jit(solution)/shard_map/ppermute | solution.py:60
  31.3 4.2 %collective-permute-done = bf16[384,128]{1,0:T(8,128)(2,1)S(1)} collective-permute-done((bf16[384,128]{1,0:T(8,128)(2,1)S(1)}, bf16[384,128]{1,0:T(8,128)(2,1)S(1)}, u32[]{:S(2)}, u32[]{:S(2)}) %collective-permute-start) | collective-permute-done | bytes 98336 | tf_op jit(solution)/shard_map/ppermute | solution.py:60
  35.5 4.9 %collective-permute-start.3 = (bf16[384,128]{1,0:T(8,128)(2,1)S(1)}, bf16[384,128]{1,0:T(8,128)(2,1)S(1)}, u32[]{:S(2)}, u32[]{:S(2)}) collective-permute-start(bf16[384,128]{1,0:T(8,128)(2,1)S(1)} %collective-permute-done), channel_id=1, source_target_pairs={{0,128},{8,136},{16,144},{24,152},{32,160},{40,168},{48,176},{56,1... | collective-permute-start | bytes 294920 | tf_op jit(solution)/shard_map/ppermute | solution.py:39
  40.4 4.1 %collective-permute-start.1 = (bf16[384,128]{1,0:T(8,128)(2,1)S(1)}, bf16[384,128]{1,0:T(8,128)(2,1)S(1)}, u32[]{:S(2)}, u32[]{:S(2)}) collective-permute-start(bf16[384,128]{1,0:T(8,128)(2,1)S(1)} %collective-permute-done), channel_id=1, source_target_pairs={{0,64},{8,72},{16,80},{24,88},{32,96},{40,104},{48,112},{56,120},{... | collective-permute-start | bytes 294920 | tf_op jit(solution)/shard_map/ppermute | solution.py:39
  45.5 3.3 %collective-permute-done.2 = bf16[384,128]{1,0:T(8,128)(2,1)S(1)} collective-permute-done((bf16[384,128]{1,0:T(8,128)(2,1)S(1)}, bf16[384,128]{1,0:T(8,128)(2,1)S(1)}, u32[]{:S(2)}, u32[]{:S(2)}) %collective-permute-start.2) | collective-permute-done | bytes 98336 | tf_op jit(solution)/shard_map/ppermute | solution.py:39
  48.8 4.1 %collective-permute-start.7 = (bf16[4,192,128]{2,1,0:T(8,128)(2,1)S(1)}, bf16[4,192,128]{2,1,0:T(8,128)(2,1)S(1)}, u32[]{:S(2)}, u32[]{:S(2)}) collective-permute-start(bf16[4,192,128]{2,1,0:T(8,128)(2,1)S(1)} %pad_maximum_fusion.2), channel_id=1, source_target_pairs={{0,48},{8,56},{16,0},{24,8},{32,16},{40,24},{48,32},{56,40},{64,11... | collective-permute-start | bytes 589832 | tf_op jit(solution)/shard_map/ppermute | solution.py:39
  52.9 3.3 %collective-permute-start.8 = (bf16[4,192,128]{2,1,0:T(8,128)(2,1)S(1)}, bf16[4,192,128]{2,1,0:T(8,128)(2,1)S(1)}, u32[]{:S(2)}, u32[]{:S(2)}) collective-permute-start(bf16[4,192,128]{2,1,0:T(8,128)(2,1)S(1)} %pad_maximum_fusion.3), channel_id=1, source_target_pairs={{0,48},{8,56},{16,0},{24,8},{32,16},{40,24},{48,32},{56,40},{64,11... | collective-permute-start | bytes 589832 | tf_op jit(solution)/shard_map/ppermute | solution.py:39
  56.4 5.2 %collective-permute-done.4 = bf16[4,192,128]{2,1,0:T(8,128)(2,1)S(1)} collective-permute-done((bf16[4,192,128]{2,1,0:T(8,128)(2,1)S(1)}, bf16[4,192,128]{2,1,0:T(8,128)(2,1)S(1)}, u32[]{:S(2)}, u32[]{:S(2)}) %collective-permute-start.4) | collective-permute-done | bytes 196640 | tf_op jit(solution)/shard_map/ppermute | solution.py:39
  61.6 4.1 %collective-permute-start.13 = (bf16[2,400,128]{2,1,0:T(8,128)(2,1)S(1)}, bf16[2,400,128]{2,1,0:T(8,128)(2,1)S(1)}, u32[]{:S(2)}, u32[]{:S(2)}) collective-permute-start(bf16[2,400,128]{2,1,0:T(8,128)(2,1)S(1)} %pad_maximum_fusion.1.refs_9_), channel_id=1, source_target_pairs={{0,2},{1,3},{2,0},{3,1},{4,6},{5,7},{6,4},{7,5},{8,10},{9,11},{10,... | collective-permute-start | bytes 614408 | tf_op jit(solution)/shard_map/ppermute | solution.py:39
  65.8 3.2 %collective-permute-start.10 = (bf16[4,192,128]{2,1,0:T(8,128)(2,1)S(1)}, bf16[4,192,128]{2,1,0:T(8,128)(2,1)S(1)}, u32[]{:S(2)}, u32[]{:S(2)}) collective-permute-start(bf16[4,192,128]{2,1,0:T(8,128)(2,1)S(1)} %collective-permute-done.8), channel_id=1, source_target_pairs={{0,48},{8,56},{16,0},{24,8},{32,16},{40,24},{48,32},{56,40},{64,11... | collective-permute-start | bytes 589832 | tf_op jit(solution)/shard_map/ppermute | solution.py:39
  69.0 2.1 %collective-permute-start.11 = (bf16[2,400,128]{2,1,0:T(8,128)(2,1)S(1)}, bf16[2,400,128]{2,1,0:T(8,128)(2,1)S(1)}, u32[]{:S(2)}, u32[]{:S(2)}) collective-permute-start(bf16[2,400,128]{2,1,0:T(8,128)(2,1)S(1)} %pad_maximum_fusion.1.refs_9_), channel_id=1, source_target_pairs={{0,1},{1,2},{2,3},{3,0},{4,5},{5,6},{6,7},{7,4},{8,9},{9,10},{10,1... | collective-permute-start | bytes 614408 | tf_op jit(solution)/shard_map/ppermute | solution.py:39
  73.3 2.8 %collective-permute-done.11.refs_10_ = bf16[2,400,128]{2,1,0:T(8,128)(2,1)S(1)} collective-permute-done((bf16[2,400,128]{2,1,0:T(8,128)(2,1)S(1)}, bf16[2,400,128]{2,1,0:T(8,128)(2,1)S(1)}, u32[]{:S(2)}, u32[]{:S(2)}) %collective-permute-start.11) | collective-permute-done | bytes 204832 | tf_op jit(solution)/shard_map/ppermute | solution.py:39
  78.5 2.9 %weights_g.1 = (f32[8,96,128]{2,1,0:T(8,128)}, f32[8,96,128]{2,1,0:T(8,128)S(1)}, f32[192,1]{1,0:T(8,128)S(1)}) custom-call(s32[5]{0:T(128)S(1)} %copy-done.9, bf16[8,192,128]{2,1,0:T(8,128)(2,1)S(1)} %constant_dynamic-update-slice_fusion.refs_1_, bf16[8,192,128]{2,1,0:T(8,128)(2,1)S(1)} %constant_dynamic-update-slice_fusion.8.refs_2_, ...), custom_call_target="tpu_custom_call" | custom-call | tf_op jit(solution)/shard_map/weights_g/pallas_call | solution.py:350
  81.4 2.4 %weights_q.1 = (f32[4,288,128]{2,1,0:T(8,128)S(1)}, f32[4,288,128]{2,1,0:T(8,128)S(1)}) custom-call(s32[5]{0:T(128)S(1)} %copy-done.9, bf16[8,192,128]{2,1,0:T(8,128)(2,1)S(1)} %constant_dynamic-update-slice_fusion.refs_1_, bf16[8,192,128]{2,1,0:T(8,128)(2,1)S(1)} %constant_dynamic-update-slice_fusion.8.refs_2_, ...), custom_call_target="tpu_custom_call" | custom-call | tf_op jit(solution)/shard_map/weights_q/pallas_call | solution.py:350
  83.8 3.6 %all-to-all-start.1 = ((f32[8,96,128]{2,1,0:T(8,128)}), f32[8,96,128]{2,1,0:T(8,128)S(1)}, u32[]{:S(2)}, u32[]{:S(2)}) async-start(f32[8,96,128]{2,1,0:T(8,128)} %get-tuple-element.58), calls=%async_computation.1 | async-start | bytes 786432 | tf_op jit(solution)/shard_map/all_to_all | solution.py:447
  87.4 1.9 %collective-permute-start.18 = (f32[4,288,128]{2,1,0:T(8,128)S(1)}, f32[4,288,128]{2,1,0:T(8,128)S(1)}, u32[]{:S(2)}, u32[]{:S(2)}) collective-permute-start(f32[4,288,128]{2,1,0:T(8,128)S(1)} %get-tuple-element.53), channel_id=1, source_target_pairs={{0,4},{1,5},{2,6},{3,7},{4,0},{5,1},{6,2},{7,3},{8,12},{9,13},{10,... | collective-permute-start | bytes 1769480 | tf_op jit(solution)/shard_map/ppermute | solution.py:39
  89.4 7.0 %all-to-all-done.1.parts = f32[8,96,128]{2,1,0:T(8,128)S(1)} async-done(((f32[8,96,128]{2,1,0:T(8,128)}), f32[8,96,128]{2,1,0:T(8,128)S(1)}, u32[]{:S(2)}, u32[]{:S(2)}) %all-to-all-start.1) | async-done | bytes 393248 | tf_op jit(solution)/shard_map/all_to_all | solution.py:447
  97.5 5.3 %all-to-all-start.2 = ((f32[32,8,128]{2,1,0:T(8,128)}), f32[32,8,128]{2,1,0:T(8,128)S(1)}, u32[]{:S(2)}, u32[]{:S(2)}) async-start(f32[32,8,128]{2,1,0:T(8,128)} %bitcast.22), calls=%async_computation.2 | async-start | bytes 262144 | tf_op jit(solution)/shard_map/all_to_all | solution.py:454
  102.8 5.8 %collective-permute-done.18.came = f32[4,288,128]{2,1,0:T(8,128)S(1)} collective-permute-done((f32[4,288,128]{2,1,0:T(8,128)S(1)}, f32[4,288,128]{2,1,0:T(8,128)S(1)}, u32[]{:S(2)}, u32[]{:S(2)}) %collective-permute-start.18) | collective-permute-done | bytes 589856 | tf_op jit(solution)/shard_map/ppermute | solution.py:39
  108.6 3.1 %collective-permute-start.19 = (f32[288,128]{1,0:T(8,128)S(1)}, f32[288,128]{1,0:T(8,128)S(1)}, u32[]{:S(2)}, u32[]{:S(2)}) collective-permute-start(f32[288,128]{1,0:T(8,128)S(1)} %get-tuple-element.55), channel_id=1, source_target_pairs={{0,3},{1,0},{2,1},{3,2},{4,7},{5,4},{6,5},{7,6},{8,11},{9,8},{10,9... | collective-permute-start | bytes 442376 | tf_op jit(solution)/shard_map/ppermute | solution.py:39
  111.7 2.3 %collective-permute-start.21 = (f32[288,128]{1,0:T(8,128)S(1)}, f32[288,128]{1,0:T(8,128)S(1)}, u32[]{:S(2)}, u32[]{:S(2)}) collective-permute-start(f32[288,128]{1,0:T(8,128)S(1)} %get-tuple-element.57), channel_id=1, source_target_pairs={{0,2},{1,3},{2,0},{3,1},{4,6},{5,7},{6,4},{7,5},{8,10},{9,11},{10,... | collective-permute-start | bytes 442376 | tf_op jit(solution)/shard_map/ppermute | solution.py:39
  115.8 3.9 %collective-permute-done.20.p2 = f32[288,128]{1,0:T(8,128)S(1)} collective-permute-done((f32[288,128]{1,0:T(8,128)S(1)}, f32[288,128]{1,0:T(8,128)S(1)}, u32[]{:S(2)}, u32[]{:S(2)}) %collective-permute-start.20) | collective-permute-done | bytes 147488 | tf_op jit(solution)/shard_map/ppermute | solution.py:39
  (75 shorter events, 11.6 us)
Async XLA Ops:
  24.3 11.2 %collective-permute-start = (bf16[384,128]{1,0:T(8,128)(2,1)S(1)}, bf16[384,128]{1,0:T(8,128)(2,1)S(1)}, u32[]{:S(2)}, u32[]{:S(2)}) collective-permute-start(bf16[384,128]{1,0:T(8,128)(2,1)S(1)} %get-tuple-element.37), channel_id=1, source_target_pairs={{0,0},{1,48},{2,64},{3,112},{4,128},{5,176},{6,192},{7,240},{8,8},... | collective-permute-start | bytes 294920 | tf_op jit(solution)/shard_map/ppermute | solution.py:60
  31.2 13.3 %collective-permute-start.5 = (bf16[400,128]{1,0:T(8,128)(2,1)S(1)}, bf16[400,128]{1,0:T(8,128)(2,1)S(1)}, u32[]{:S(2)}, u32[]{:S(2)}) collective-permute-start(bf16[400,128]{1,0:T(8,128)(2,1)S(1)} %get-tuple-element.38), channel_id=1, source_target_pairs={{0,4},{1,5},{2,6},{3,7},{4,0},{5,1},{6,2},{7,3},{8,12},{9,13},{10,... | collective-permute-start | bytes 307208 | tf_op jit(solution)/shard_map/ppermute | solution.py:39
  35.5 10.0 %collective-permute-start.3 = (bf16[384,128]{1,0:T(8,128)(2,1)S(1)}, bf16[384,128]{1,0:T(8,128)(2,1)S(1)}, u32[]{:S(2)}, u32[]{:S(2)}) collective-permute-start(bf16[384,128]{1,0:T(8,128)(2,1)S(1)} %collective-permute-done), channel_id=1, source_target_pairs={{0,128},{8,136},{16,144},{24,152},{32,160},{40,168},{48,176},{56,1... | collective-permute-start | bytes 294920 | tf_op jit(solution)/shard_map/ppermute | solution.py:39
  40.4 8.4 %collective-permute-start.2 = (bf16[384,128]{1,0:T(8,128)(2,1)S(1)}, bf16[384,128]{1,0:T(8,128)(2,1)S(1)}, u32[]{:S(2)}, u32[]{:S(2)}) collective-permute-start(bf16[384,128]{1,0:T(8,128)(2,1)S(1)} %collective-permute-done), channel_id=1, source_target_pairs={{0,192},{8,200},{16,208},{24,216},{32,224},{40,232},{48,240},{56,2... | collective-permute-start | bytes 294920 | tf_op jit(solution)/shard_map/ppermute | solution.py:39
  40.4 8.4 %collective-permute-start.1 = (bf16[384,128]{1,0:T(8,128)(2,1)S(1)}, bf16[384,128]{1,0:T(8,128)(2,1)S(1)}, u32[]{:S(2)}, u32[]{:S(2)}) collective-permute-start(bf16[384,128]{1,0:T(8,128)(2,1)S(1)} %collective-permute-done), channel_id=1, source_target_pairs={{0,64},{8,72},{16,80},{24,88},{32,96},{40,104},{48,112},{56,120},{... | collective-permute-start | bytes 294920 | tf_op jit(solution)/shard_map/ppermute | solution.py:39
  48.8 16.8 %collective-permute-start.7 = (bf16[4,192,128]{2,1,0:T(8,128)(2,1)S(1)}, bf16[4,192,128]{2,1,0:T(8,128)(2,1)S(1)}, u32[]{:S(2)}, u32[]{:S(2)}) collective-permute-start(bf16[4,192,128]{2,1,0:T(8,128)(2,1)S(1)} %pad_maximum_fusion.2), channel_id=1, source_target_pairs={{0,48},{8,56},{16,0},{24,8},{32,16},{40,24},{48,32},{56,40},{64,11... | collective-permute-start | bytes 589832 | tf_op jit(solution)/shard_map/ppermute | solution.py:39
  52.9 8.7 %collective-permute-start.4 = (bf16[4,192,128]{2,1,0:T(8,128)(2,1)S(1)}, bf16[4,192,128]{2,1,0:T(8,128)(2,1)S(1)}, u32[]{:S(2)}, u32[]{:S(2)}) collective-permute-start(bf16[4,192,128]{2,1,0:T(8,128)(2,1)S(1)} %pad_maximum_fusion.2), channel_id=1, source_target_pairs={{0,16},{8,24},{16,32},{24,40},{32,48},{40,56},{48,0},{56,8},{64,80... | collective-permute-start | bytes 589832 | tf_op jit(solution)/shard_map/ppermute | solution.py:39
  52.9 12.8 %collective-permute-start.8 = (bf16[4,192,128]{2,1,0:T(8,128)(2,1)S(1)}, bf16[4,192,128]{2,1,0:T(8,128)(2,1)S(1)}, u32[]{:S(2)}, u32[]{:S(2)}) collective-permute-start(bf16[4,192,128]{2,1,0:T(8,128)(2,1)S(1)} %pad_maximum_fusion.3), channel_id=1, source_target_pairs={{0,48},{8,56},{16,0},{24,8},{32,16},{40,24},{48,32},{56,40},{64,11... | collective-permute-start | bytes 589832 | tf_op jit(solution)/shard_map/ppermute | solution.py:39
  56.2 12.8 %collective-permute-start.6 = (bf16[4,192,128]{2,1,0:T(8,128)(2,1)S(1)}, bf16[4,192,128]{2,1,0:T(8,128)(2,1)S(1)}, u32[]{:S(2)}, u32[]{:S(2)}) collective-permute-start(bf16[4,192,128]{2,1,0:T(8,128)(2,1)S(1)} %pad_maximum_fusion.3), channel_id=1, source_target_pairs={{0,16},{8,24},{16,32},{24,40},{32,48},{40,56},{48,0},{56,8},{64,80... | collective-permute-start | bytes 589832 | tf_op jit(solution)/shard_map/ppermute | solution.py:39
  61.6 11.6 %collective-permute-start.13 = (bf16[2,400,128]{2,1,0:T(8,128)(2,1)S(1)}, bf16[2,400,128]{2,1,0:T(8,128)(2,1)S(1)}, u32[]{:S(2)}, u32[]{:S(2)}) collective-permute-start(bf16[2,400,128]{2,1,0:T(8,128)(2,1)S(1)} %pad_maximum_fusion.1.refs_9_), channel_id=1, source_target_pairs={{0,2},{1,3},{2,0},{3,1},{4,6},{5,7},{6,4},{7,5},{8,10},{9,11},{10,... | collective-permute-start | bytes 614408 | tf_op jit(solution)/shard_map/ppermute | solution.py:39
  65.6 7.7 %collective-permute-start.12 = (bf16[2,400,128]{2,1,0:T(8,128)(2,1)S(1)}, bf16[2,400,128]{2,1,0:T(8,128)(2,1)S(1)}, u32[]{:S(2)}, u32[]{:S(2)}) collective-permute-start(bf16[2,400,128]{2,1,0:T(8,128)(2,1)S(1)} %pad_maximum_fusion.1.refs_9_), channel_id=1, source_target_pairs={{0,3},{1,0},{2,1},{3,2},{4,7},{5,4},{6,5},{7,6},{8,11},{9,8},{10,9... | collective-permute-start | bytes 614408 | tf_op jit(solution)/shard_map/ppermute | solution.py:39
  65.7 7.0 %collective-permute-start.9 = (bf16[4,192,128]{2,1,0:T(8,128)(2,1)S(1)}, bf16[4,192,128]{2,1,0:T(8,128)(2,1)S(1)}, u32[]{:S(2)}, u32[]{:S(2)}) collective-permute-start(bf16[4,192,128]{2,1,0:T(8,128)(2,1)S(1)} %collective-permute-done.4), channel_id=1, source_target_pairs={{0,16},{8,24},{16,32},{24,40},{32,48},{40,56},{48,0},{56,8},{64,80... | collective-permute-start | bytes 589832 | tf_op jit(solution)/shard_map/ppermute | solution.py:39
  65.8 6.9 %collective-permute-start.10 = (bf16[4,192,128]{2,1,0:T(8,128)(2,1)S(1)}, bf16[4,192,128]{2,1,0:T(8,128)(2,1)S(1)}, u32[]{:S(2)}, u32[]{:S(2)}) collective-permute-start(bf16[4,192,128]{2,1,0:T(8,128)(2,1)S(1)} %collective-permute-done.8), channel_id=1, source_target_pairs={{0,48},{8,56},{16,0},{24,8},{32,16},{40,24},{48,32},{56,40},{64,11... | collective-permute-start | bytes 589832 | tf_op jit(solution)/shard_map/ppermute | solution.py:39
  69.0 7.0 %collective-permute-start.11 = (bf16[2,400,128]{2,1,0:T(8,128)(2,1)S(1)}, bf16[2,400,128]{2,1,0:T(8,128)(2,1)S(1)}, u32[]{:S(2)}, u32[]{:S(2)}) collective-permute-start(bf16[2,400,128]{2,1,0:T(8,128)(2,1)S(1)} %pad_maximum_fusion.1.refs_9_), channel_id=1, source_target_pairs={{0,1},{1,2},{2,3},{3,0},{4,5},{5,6},{6,7},{7,4},{8,9},{9,10},{10,1... | collective-permute-start | bytes 614408 | tf_op jit(solution)/shard_map/ppermute | solution.py:39
  72.6 3.5 %collective-permute-start.14 = (bf16[8,192,128]{2,1,0:T(8,128)(2,1)S(1)}, bf16[8,192,128]{2,1,0:T(8,128)(2,1)S(1)}, u32[]{:S(2)}, u32[]{:S(2)}) collective-permute-start(bf16[8,192,128]{2,1,0:T(8,128)(2,1)S(1)} %constant_dynamic-update-slice_fusion.refs_1_), channel_id=1, source_target_pairs={{0,8},{8,0},{16,24},{24,16},{32,40},{40,32},{48,56},{56,48},{64,72... | collective-permute-start | bytes 1179656 | tf_op jit(solution)/shard_map/ppermute | solution.py:39
  72.6 3.5 %collective-permute-start.15 = (bf16[8,192,128]{2,1,0:T(8,128)(2,1)S(1)}, bf16[8,192,128]{2,1,0:T(8,128)(2,1)S(1)}, u32[]{:S(2)}, u32[]{:S(2)}) collective-permute-start(bf16[8,192,128]{2,1,0:T(8,128)(2,1)S(1)} %constant_dynamic-update-slice_fusion.8.refs_2_), channel_id=1, source_target_pairs={{0,8},{8,0},{16,24},{24,16},{32,40},{40,32},{48,56},{56,48},{64,72... | collective-permute-start | bytes 1179656 | tf_op jit(solution)/shard_map/ppermute | solution.py:39
  73.2 2.9 %collective-permute-start.16 = (bf16[8,192,128]{2,1,0:T(8,128)(2,1)S(1)}, bf16[8,192,128]{2,1,0:T(8,128)(2,1)S(1)}, u32[]{:S(2)}, u32[]{:S(2)}) collective-permute-start(bf16[8,192,128]{2,1,0:T(8,128)(2,1)S(1)} %constant_dynamic-update-slice_fusion.10.refs_3_), channel_id=1, source_target_pairs={{0,8},{8,0},{16,24},{24,16},{32,40},{40,32},{48,56},{56,48},{64,72... | collective-permute-start | bytes 1179656 | tf_op jit(solution)/shard_map/ppermute | solution.py:39
  76.1 1.7 %collective-permute-start.17 = (bf16[8,192,128]{2,1,0:T(8,128)(2,1)S(1)}, bf16[8,192,128]{2,1,0:T(8,128)(2,1)S(1)}, u32[]{:S(2)}, u32[]{:S(2)}) collective-permute-start(bf16[8,192,128]{2,1,0:T(8,128)(2,1)S(1)} %pad_maximum_fusion.refs_4_), channel_id=1, source_target_pairs={{0,8},{8,0},{16,24},{24,16},{32,40},{40,32},{48,56},{56,48},{64,72... | collective-permute-start | bytes 1179656 | tf_op jit(solution)/shard_map/ppermute | solution.py:39
  83.8 12.6 %all-to-all-start.1 = ((f32[8,96,128]{2,1,0:T(8,128)}), f32[8,96,128]{2,1,0:T(8,128)S(1)}, u32[]{:S(2)}, u32[]{:S(2)}) async-start(f32[8,96,128]{2,1,0:T(8,128)} %get-tuple-element.58), calls=%async_computation.1 | async-start | bytes 786432 | tf_op jit(solution)/shard_map/all_to_all | solution.py:447
  87.4 21.1 %collective-permute-start.18 = (f32[4,288,128]{2,1,0:T(8,128)S(1)}, f32[4,288,128]{2,1,0:T(8,128)S(1)}, u32[]{:S(2)}, u32[]{:S(2)}) collective-permute-start(f32[4,288,128]{2,1,0:T(8,128)S(1)} %get-tuple-element.53), channel_id=1, source_target_pairs={{0,4},{1,5},{2,6},{3,7},{4,0},{5,1},{6,2},{7,3},{8,12},{9,13},{10,... | collective-permute-start | bytes 1769480 | tf_op jit(solution)/shard_map/ppermute | solution.py:39
  97.5 22.1 %all-to-all-start.2 = ((f32[32,8,128]{2,1,0:T(8,128)}), f32[32,8,128]{2,1,0:T(8,128)S(1)}, u32[]{:S(2)}, u32[]{:S(2)}) async-start(f32[32,8,128]{2,1,0:T(8,128)} %bitcast.22), calls=%async_computation.2 | async-start | bytes 262144 | tf_op jit(solution)/shard_map/all_to_all | solution.py:454
  108.6 7.1 %collective-permute-start.19 = (f32[288,128]{1,0:T(8,128)S(1)}, f32[288,128]{1,0:T(8,128)S(1)}, u32[]{:S(2)}, u32[]{:S(2)}) collective-permute-start(f32[288,128]{1,0:T(8,128)S(1)} %get-tuple-element.55), channel_id=1, source_target_pairs={{0,3},{1,0},{2,1},{3,2},{4,7},{5,4},{6,5},{7,6},{8,11},{9,8},{10,9... | collective-permute-start | bytes 442376 | tf_op jit(solution)/shard_map/ppermute | solution.py:39
  111.7 7.9 %collective-permute-start.20 = (f32[288,128]{1,0:T(8,128)S(1)}, f32[288,128]{1,0:T(8,128)S(1)}, u32[]{:S(2)}, u32[]{:S(2)}) collective-permute-start(f32[288,128]{1,0:T(8,128)S(1)} %get-tuple-element.56), channel_id=1, source_target_pairs={{0,1},{1,2},{2,3},{3,0},{4,5},{5,6},{6,7},{7,4},{8,9},{9,10},{10,1... | collective-permute-start | bytes 442376 | tf_op jit(solution)/shard_map/ppermute | solution.py:39
  111.7 7.9 %collective-permute-start.21 = (f32[288,128]{1,0:T(8,128)S(1)}, f32[288,128]{1,0:T(8,128)S(1)}, u32[]{:S(2)}, u32[]{:S(2)}) collective-permute-start(f32[288,128]{1,0:T(8,128)S(1)} %get-tuple-element.57), channel_id=1, source_target_pairs={{0,2},{1,3},{2,0},{3,1},{4,6},{5,7},{6,4},{7,5},{8,10},{9,11},{10,... | collective-permute-start | bytes 442376 | tf_op jit(solution)/shard_map/ppermute | solution.py:39
  (11 other events, 76.3 us)

commit v7 on v6

--- a/solution.py
+++ b/solution.py
@@ -23,11 +23,6 @@
 z_hi, x_axis, core = ("row", 8, 4), ("row", 2, 4), ("row", 1, 2)
 z_lo, y_axis = ("col", 4, 2), ("col", 1, 4)
 offsets = (0, -1, 1, 2)
-
-
-def digit(axis):
-    name, stride, length = axis
-    return lax.axis_index(name) // stride % length
 
 
 def turn(x, axis, step):
@@ -142,7 +137,7 @@
     width = multiplier.shape[1]
     padded = receive_across.shape[0]
     rows = padded // group
-    r, c = place[3], place[4]
+    r, c = place[0], place[1]
     square = (block, block)
     ids = r * block + iota((block, 1), 0)
     target = jnp.zeros((block, lanes), i32)
@@ -244,22 +239,22 @@
 
 def diagonal_of(place, shape):
     block, width = shape
-    return iota(shape, 0) + (place[3] * block - place[4] * width) == iota(shape, 1)
+    return iota(shape, 0) + (place[0] * block - place[1] * width) == iota(shape, 1)
 
 
 def column_at(place, y_place, z_place):
-    return ((place[4] + offsets[y_place]) & 3) + (((place[4] >> 2) + z_place) & 1) * 4
+    return ((place[1] + offsets[y_place]) & 3) + (((place[1] >> 2) + z_place) & 1) * 4
 
 
 def fill(place, blocks, around, second, right, left, by_col, apart):
     block = left.shape[0]
     base = second * block
-    zh, xx, cc = place[0], place[1], place[2]
+    zh, xx, cc = place[0] >> 3, (place[0] >> 1) & 3, place[0] & 1
     ids = [((zh + o) & 3) * 2 + b for o in offsets for b in range(2)]
     for k, source in enumerate(blocks):
         x = (xx + offsets[k % 4]) & 3
         other = cc if k < 4 else 1 - cc
-        mirrored = jnp.where((x >> 1) == (place[4] & 1), 0, 1)
+        mirrored = jnp.where((x >> 1) == (place[1] & 1), 0, 1)
         j = (jnp.where(mirrored == 0, x, 3 - x) & 1) * 2 + other
         rows = pl.ds(pl.multiple_of(j * block, block), block)
         for z_place in range(4):
@@ -375,10 +370,7 @@
     width = multiplier_q.shape[1]
     per = width // block
     padded = rows * group
-    place = jnp.stack(
-        [digit(axis) for axis in (z_hi, x_axis, core)]
-        + [lax.axis_index("row"), lax.axis_index("col")]
-    ).astype(i32)
+    place = jnp.stack([lax.axis_index("row"), lax.axis_index("col")]).astype(i32)
     lengths = block_lengths[None, :]
     perm = ph_perm.reshape(-1, lanes)
     leaving, mine, send, receive, receive_across, segments, ph_segments = call(

time: 121 us -> 121 us (level)
  no operation moved by 1% of the time
where the time goes in v7:
time: 121 us
  starting transfers between devices  49.6 us (41%)
  waiting for transfers between devices  38 us (31%)
  blocking collectives  18.9 us (16%)
  Pallas kernels  11 us (9%)
  local copies, waits for them, and re-layouts  1.78 us (1%)
    ppermute x21, starting transfers between devices, turn(): return lax.ppermute(x, name, pairs)  33.9 us
    ppermute x21, waiting for transfers between devices, turn(): return lax.ppermute(x, name, pairs)  26.8 us
    all_to_all x1, blocking collectives, local(): incoming = lax.all_to_all(leaving.reshape(rows, group, lanes), 'row', 0, 0)  18.9 us
    pallas_call x7, Pallas kernels, call(): pl.pallas_call(kernel, out_shape=[jax.ShapeDtypeStruct(s, d) for s, d in...  11 us
    all_to_all x1, waiting for transfers between devices, local(): sums_e = lax.all_to_all(parts_e, 'col', 0, 0)  7.05 us
    ppermute x1, starting transfers between devices, to_column(): return lax.ppermute(x, both, pairs)  6.87 us
    all_to_all x1, starting transfers between devices, local(): returned = lax.all_to_all(back.reshape(rows, group, lanes), 'row', 0, 0)  5.24 us
    ppermute x1, waiting for transfers between devices, to_column(): return lax.ppermute(x, both, pairs)  4.17 us
  transfers between devices with their start and end apart: 24, of which 11 were waited for; matrix products, arithmetic and copies ran while one was open for 0% of the time, Pallas kernels for 1%

profile of v7, /device:TPU:64, one launch (start us, length us, event | category | flops | bytes accessed | tf_op | source)
XLA Modules:
  0.0 120.9 jit_solution(17610172339726493039)
XLA Ops:
  1.2 3.0 %routes.1 = (bf16[256,128]{1,0:T(8,128)(2,1)}, bf16[2,192,128]{2,1,0:T(8,128)(2,1)}, bf16[192,256]{1,0:T(8,128)(2,1)}, bf16[192,256]{1,0:T(8,128)(2,1)}, bf16[25...) custom-call(s32[2]{0:T(128)} %pad_add_fusion.place.refs_0_, s32[48,128]{1,0:T(8,128)} %bitcast.58, ...), custom_call_target="tpu_custom_call" | custom-call | tf_op jit(solution)/shard_map/routes/pallas_call | solution.py:345
  4.2 18.9 %all_to_all.15 = bf16[32,8,128]{2,1,0:T(8,128)(2,1)S(1)} all-to-all(bf16[32,8,128]{2,1,0:T(8,128)(2,1)} %bitcast.54), channel_id=1, replica_groups=mesh['row'=32,'col'=8] {'row'}, dimensions={0} | all-to-all | bytes 131072 | tf_op jit(solution)/shard_map/all_to_all | solution.py:394
  24.2 6.9 %collective-permute-start = (bf16[384,128]{1,0:T(8,128)(2,1)S(1)}, bf16[384,128]{1,0:T(8,128)(2,1)S(1)}, u32[]{:S(2)}, u32[]{:S(2)}) collective-permute-start(bf16[384,128]{1,0:T(8,128)(2,1)S(1)} %get-tuple-element.37), channel_id=1, source_target_pairs={{0,0},{1,48},{2,64},{3,112},{4,128},{5,176},{6,192},{7,240},{8,8},... | collective-permute-start | bytes 294920 | tf_op jit(solution)/shard_map/ppermute | solution.py:55
  31.2 4.2 %collective-permute-done = bf16[384,128]{1,0:T(8,128)(2,1)S(1)} collective-permute-done((bf16[384,128]{1,0:T(8,128)(2,1)S(1)}, bf16[384,128]{1,0:T(8,128)(2,1)S(1)}, u32[]{:S(2)}, u32[]{:S(2)}) %collective-permute-start) | collective-permute-done | bytes 98336 | tf_op jit(solution)/shard_map/ppermute | solution.py:55
  35.3 4.9 %collective-permute-start.3 = (bf16[384,128]{1,0:T(8,128)(2,1)S(1)}, bf16[384,128]{1,0:T(8,128)(2,1)S(1)}, u32[]{:S(2)}, u32[]{:S(2)}) collective-permute-start(bf16[384,128]{1,0:T(8,128)(2,1)S(1)} %collective-permute-done), channel_id=1, source_target_pairs={{0,128},{8,136},{16,144},{24,152},{32,160},{40,168},{48,176},{56,1... | collective-permute-start | bytes 294920 | tf_op jit(solution)/shard_map/ppermute | solution.py:34
  40.3 4.1 %collective-permute-start.1 = (bf16[384,128]{1,0:T(8,128)(2,1)S(1)}, bf16[384,128]{1,0:T(8,128)(2,1)S(1)}, u32[]{:S(2)}, u32[]{:S(2)}) collective-permute-start(bf16[384,128]{1,0:T(8,128)(2,1)S(1)} %collective-permute-done), channel_id=1, source_target_pairs={{0,64},{8,72},{16,80},{24,88},{32,96},{40,104},{48,112},{56,120},{... | collective-permute-start | bytes 294920 | tf_op jit(solution)/shard_map/ppermute | solution.py:34
  45.3 3.3 %collective-permute-done.2 = bf16[384,128]{1,0:T(8,128)(2,1)S(1)} collective-permute-done((bf16[384,128]{1,0:T(8,128)(2,1)S(1)}, bf16[384,128]{1,0:T(8,128)(2,1)S(1)}, u32[]{:S(2)}, u32[]{:S(2)}) %collective-permute-start.2) | collective-permute-done | bytes 98336 | tf_op jit(solution)/shard_map/ppermute | solution.py:34
  48.7 4.1 %collective-permute-start.7 = (bf16[4,192,128]{2,1,0:T(8,128)(2,1)S(1)}, bf16[4,192,128]{2,1,0:T(8,128)(2,1)S(1)}, u32[]{:S(2)}, u32[]{:S(2)}) collective-permute-start(bf16[4,192,128]{2,1,0:T(8,128)(2,1)S(1)} %pad_maximum_fusion.2), channel_id=1, source_target_pairs={{0,48},{8,56},{16,0},{24,8},{32,16},{40,24},{48,32},{56,40},{64,11... | collective-permute-start | bytes 589832 | tf_op jit(solution)/shard_map/ppermute | solution.py:34
  52.8 3.3 %collective-permute-start.8 = (bf16[4,192,128]{2,1,0:T(8,128)(2,1)S(1)}, bf16[4,192,128]{2,1,0:T(8,128)(2,1)S(1)}, u32[]{:S(2)}, u32[]{:S(2)}) collective-permute-start(bf16[4,192,128]{2,1,0:T(8,128)(2,1)S(1)} %pad_maximum_fusion.3), channel_id=1, source_target_pairs={{0,48},{8,56},{16,0},{24,8},{32,16},{40,24},{48,32},{56,40},{64,11... | collective-permute-start | bytes 589832 | tf_op jit(solution)/shard_map/ppermute | solution.py:34
  56.2 5.2 %collective-permute-done.4 = bf16[4,192,128]{2,1,0:T(8,128)(2,1)S(1)} collective-permute-done((bf16[4,192,128]{2,1,0:T(8,128)(2,1)S(1)}, bf16[4,192,128]{2,1,0:T(8,128)(2,1)S(1)}, u32[]{:S(2)}, u32[]{:S(2)}) %collective-permute-start.4) | collective-permute-done | bytes 196640 | tf_op jit(solution)/shard_map/ppermute | solution.py:34
  61.4 4.1 %collective-permute-start.13 = (bf16[2,400,128]{2,1,0:T(8,128)(2,1)S(1)}, bf16[2,400,128]{2,1,0:T(8,128)(2,1)S(1)}, u32[]{:S(2)}, u32[]{:S(2)}) collective-permute-start(bf16[2,400,128]{2,1,0:T(8,128)(2,1)S(1)} %pad_maximum_fusion.1.refs_9_), channel_id=1, source_target_pairs={{0,2},{1,3},{2,0},{3,1},{4,6},{5,7},{6,4},{7,5},{8,10},{9,11},{10,... | collective-permute-start | bytes 614408 | tf_op jit(solution)/shard_map/ppermute | solution.py:34
  65.6 3.2 %collective-permute-start.10 = (bf16[4,192,128]{2,1,0:T(8,128)(2,1)S(1)}, bf16[4,192,128]{2,1,0:T(8,128)(2,1)S(1)}, u32[]{:S(2)}, u32[]{:S(2)}) collective-permute-start(bf16[4,192,128]{2,1,0:T(8,128)(2,1)S(1)} %collective-permute-done.8), channel_id=1, source_target_pairs={{0,48},{8,56},{16,0},{24,8},{32,16},{40,24},{48,32},{56,40},{64,11... | collective-permute-start | bytes 589832 | tf_op jit(solution)/shard_map/ppermute | solution.py:34
  68.9 2.1 %collective-permute-start.11 = (bf16[2,400,128]{2,1,0:T(8,128)(2,1)S(1)}, bf16[2,400,128]{2,1,0:T(8,128)(2,1)S(1)}, u32[]{:S(2)}, u32[]{:S(2)}) collective-permute-start(bf16[2,400,128]{2,1,0:T(8,128)(2,1)S(1)} %pad_maximum_fusion.1.refs_9_), channel_id=1, source_target_pairs={{0,1},{1,2},{2,3},{3,0},{4,5},{5,6},{6,7},{7,4},{8,9},{9,10},{10,1... | collective-permute-start | bytes 614408 | tf_op jit(solution)/shard_map/ppermute | solution.py:34
  73.2 2.8 %collective-permute-done.11.refs_10_ = bf16[2,400,128]{2,1,0:T(8,128)(2,1)S(1)} collective-permute-done((bf16[2,400,128]{2,1,0:T(8,128)(2,1)S(1)}, bf16[2,400,128]{2,1,0:T(8,128)(2,1)S(1)}, u32[]{:S(2)}, u32[]{:S(2)}) %collective-permute-start.11) | collective-permute-done | bytes 204832 | tf_op jit(solution)/shard_map/ppermute | solution.py:34
  78.3 3.0 %weights_g.1 = (f32[8,96,128]{2,1,0:T(8,128)}, f32[8,96,128]{2,1,0:T(8,128)S(1)}, f32[192,1]{1,0:T(8,128)S(1)}) custom-call(s32[2]{0:T(128)S(1)} %copy-done.9, bf16[8,192,128]{2,1,0:T(8,128)(2,1)S(1)} %constant_dynamic-update-slice_fusion.refs_1_, bf16[8,192,128]{2,1,0:T(8,128)(2,1)S(1)} %constant_dynamic-update-slice_fusion.8.refs_2_, ...), custom_call_target="tpu_custom_call" | custom-call | tf_op jit(solution)/shard_map/weights_g/pallas_call | solution.py:345
  81.4 2.6 %weights_q.1 = (f32[4,288,128]{2,1,0:T(8,128)S(1)}, f32[4,288,128]{2,1,0:T(8,128)S(1)}) custom-call(s32[2]{0:T(128)S(1)} %copy-done.9, bf16[8,192,128]{2,1,0:T(8,128)(2,1)S(1)} %constant_dynamic-update-slice_fusion.refs_1_, bf16[8,192,128]{2,1,0:T(8,128)(2,1)S(1)} %constant_dynamic-update-slice_fusion.8.refs_2_, ...), custom_call_target="tpu_custom_call" | custom-call | tf_op jit(solution)/shard_map/weights_q/pallas_call | solution.py:345
  84.0 3.6 %all-to-all-start.1 = ((f32[8,96,128]{2,1,0:T(8,128)}), f32[8,96,128]{2,1,0:T(8,128)S(1)}, u32[]{:S(2)}, u32[]{:S(2)}) async-start(f32[8,96,128]{2,1,0:T(8,128)} %get-tuple-element.58), calls=%async_computation.1 | async-start | bytes 786432 | tf_op jit(solution)/shard_map/all_to_all | solution.py:439
  87.6 1.9 %collective-permute-start.18 = (f32[4,288,128]{2,1,0:T(8,128)S(1)}, f32[4,288,128]{2,1,0:T(8,128)S(1)}, u32[]{:S(2)}, u32[]{:S(2)}) collective-permute-start(f32[4,288,128]{2,1,0:T(8,128)S(1)} %get-tuple-element.53), channel_id=1, source_target_pairs={{0,4},{1,5},{2,6},{3,7},{4,0},{5,1},{6,2},{7,3},{8,12},{9,13},{10,... | collective-permute-start | bytes 1769480 | tf_op jit(solution)/shard_map/ppermute | solution.py:34
  89.5 7.0 %all-to-all-done.1.parts = f32[8,96,128]{2,1,0:T(8,128)S(1)} async-done(((f32[8,96,128]{2,1,0:T(8,128)}), f32[8,96,128]{2,1,0:T(8,128)S(1)}, u32[]{:S(2)}, u32[]{:S(2)}) %all-to-all-start.1) | async-done | bytes 393248 | tf_op jit(solution)/shard_map/all_to_all | solution.py:439
  97.7 5.2 %all-to-all-start.2 = ((f32[32,8,128]{2,1,0:T(8,128)}), f32[32,8,128]{2,1,0:T(8,128)S(1)}, u32[]{:S(2)}, u32[]{:S(2)}) async-start(f32[32,8,128]{2,1,0:T(8,128)} %bitcast.19), calls=%async_computation.2 | async-start | bytes 262144 | tf_op jit(solution)/shard_map/all_to_all | solution.py:446
  102.9 5.8 %collective-permute-done.18.came = f32[4,288,128]{2,1,0:T(8,128)S(1)} collective-permute-done((f32[4,288,128]{2,1,0:T(8,128)S(1)}, f32[4,288,128]{2,1,0:T(8,128)S(1)}, u32[]{:S(2)}, u32[]{:S(2)}) %collective-permute-start.18) | collective-permute-done | bytes 589856 | tf_op jit(solution)/shard_map/ppermute | solution.py:34
  108.8 3.0 %collective-permute-start.19 = (f32[288,128]{1,0:T(8,128)S(1)}, f32[288,128]{1,0:T(8,128)S(1)}, u32[]{:S(2)}, u32[]{:S(2)}) collective-permute-start(f32[288,128]{1,0:T(8,128)S(1)} %get-tuple-element.55), channel_id=1, source_target_pairs={{0,3},{1,0},{2,1},{3,2},{4,7},{5,4},{6,5},{7,6},{8,11},{9,8},{10,9... | collective-permute-start | bytes 442376 | tf_op jit(solution)/shard_map/ppermute | solution.py:34
  111.8 2.3 %collective-permute-start.21 = (f32[288,128]{1,0:T(8,128)S(1)}, f32[288,128]{1,0:T(8,128)S(1)}, u32[]{:S(2)}, u32[]{:S(2)}) collective-permute-start(f32[288,128]{1,0:T(8,128)S(1)} %get-tuple-element.57), channel_id=1, source_target_pairs={{0,2},{1,3},{2,0},{3,1},{4,6},{5,7},{6,4},{7,5},{8,10},{9,11},{10,... | collective-permute-start | bytes 442376 | tf_op jit(solution)/shard_map/ppermute | solution.py:34
  115.9 3.9 %collective-permute-done.20.p2 = f32[288,128]{1,0:T(8,128)S(1)} collective-permute-done((f32[288,128]{1,0:T(8,128)S(1)}, f32[288,128]{1,0:T(8,128)S(1)}, u32[]{:S(2)}, u32[]{:S(2)}) %collective-permute-start.20) | collective-permute-done | bytes 147488 | tf_op jit(solution)/shard_map/ppermute | solution.py:34
  (75 shorter events, 11.5 us)
Async XLA Ops:
  24.2 11.2 %collective-permute-start = (bf16[384,128]{1,0:T(8,128)(2,1)S(1)}, bf16[384,128]{1,0:T(8,128)(2,1)S(1)}, u32[]{:S(2)}, u32[]{:S(2)}) collective-permute-start(bf16[384,128]{1,0:T(8,128)(2,1)S(1)} %get-tuple-element.37), channel_id=1, source_target_pairs={{0,0},{1,48},{2,64},{3,112},{4,128},{5,176},{6,192},{7,240},{8,8},... | collective-permute-start | bytes 294920 | tf_op jit(solution)/shard_map/ppermute | solution.py:55
  31.1 13.3 %collective-permute-start.5 = (bf16[400,128]{1,0:T(8,128)(2,1)S(1)}, bf16[400,128]{1,0:T(8,128)(2,1)S(1)}, u32[]{:S(2)}, u32[]{:S(2)}) collective-permute-start(bf16[400,128]{1,0:T(8,128)(2,1)S(1)} %get-tuple-element.38), channel_id=1, source_target_pairs={{0,4},{1,5},{2,6},{3,7},{4,0},{5,1},{6,2},{7,3},{8,12},{9,13},{10,... | collective-permute-start | bytes 307208 | tf_op jit(solution)/shard_map/ppermute | solution.py:34
  35.3 10.0 %collective-permute-start.3 = (bf16[384,128]{1,0:T(8,128)(2,1)S(1)}, bf16[384,128]{1,0:T(8,128)(2,1)S(1)}, u32[]{:S(2)}, u32[]{:S(2)}) collective-permute-start(bf16[384,128]{1,0:T(8,128)(2,1)S(1)} %collective-permute-done), channel_id=1, source_target_pairs={{0,128},{8,136},{16,144},{24,152},{32,160},{40,168},{48,176},{56,1... | collective-permute-start | bytes 294920 | tf_op jit(solution)/shard_map/ppermute | solution.py:34
  40.3 8.4 %collective-permute-start.2 = (bf16[384,128]{1,0:T(8,128)(2,1)S(1)}, bf16[384,128]{1,0:T(8,128)(2,1)S(1)}, u32[]{:S(2)}, u32[]{:S(2)}) collective-permute-start(bf16[384,128]{1,0:T(8,128)(2,1)S(1)} %collective-permute-done), channel_id=1, source_target_pairs={{0,192},{8,200},{16,208},{24,216},{32,224},{40,232},{48,240},{56,2... | collective-permute-start | bytes 294920 | tf_op jit(solution)/shard_map/ppermute | solution.py:34
  40.3 8.4 %collective-permute-start.1 = (bf16[384,128]{1,0:T(8,128)(2,1)S(1)}, bf16[384,128]{1,0:T(8,128)(2,1)S(1)}, u32[]{:S(2)}, u32[]{:S(2)}) collective-permute-start(bf16[384,128]{1,0:T(8,128)(2,1)S(1)} %collective-permute-done), channel_id=1, source_target_pairs={{0,64},{8,72},{16,80},{24,88},{32,96},{40,104},{48,112},{56,120},{... | collective-permute-start | bytes 294920 | tf_op jit(solution)/shard_map/ppermute | solution.py:34
  48.7 16.8 %collective-permute-start.7 = (bf16[4,192,128]{2,1,0:T(8,128)(2,1)S(1)}, bf16[4,192,128]{2,1,0:T(8,128)(2,1)S(1)}, u32[]{:S(2)}, u32[]{:S(2)}) collective-permute-start(bf16[4,192,128]{2,1,0:T(8,128)(2,1)S(1)} %pad_maximum_fusion.2), channel_id=1, source_target_pairs={{0,48},{8,56},{16,0},{24,8},{32,16},{40,24},{48,32},{56,40},{64,11... | collective-permute-start | bytes 589832 | tf_op jit(solution)/shard_map/ppermute | solution.py:34
  52.8 8.7 %collective-permute-start.4 = (bf16[4,192,128]{2,1,0:T(8,128)(2,1)S(1)}, bf16[4,192,128]{2,1,0:T(8,128)(2,1)S(1)}, u32[]{:S(2)}, u32[]{:S(2)}) collective-permute-start(bf16[4,192,128]{2,1,0:T(8,128)(2,1)S(1)} %pad_maximum_fusion.2), channel_id=1, source_target_pairs={{0,16},{8,24},{16,32},{24,40},{32,48},{40,56},{48,0},{56,8},{64,80... | collective-permute-start | bytes 589832 | tf_op jit(solution)/shard_map/ppermute | solution.py:34
  52.8 12.8 %collective-permute-start.8 = (bf16[4,192,128]{2,1,0:T(8,128)(2,1)S(1)}, bf16[4,192,128]{2,1,0:T(8,128)(2,1)S(1)}, u32[]{:S(2)}, u32[]{:S(2)}) collective-permute-start(bf16[4,192,128]{2,1,0:T(8,128)(2,1)S(1)} %pad_maximum_fusion.3), channel_id=1, source_target_pairs={{0,48},{8,56},{16,0},{24,8},{32,16},{40,24},{48,32},{56,40},{64,11... | collective-permute-start | bytes 589832 | tf_op jit(solution)/shard_map/ppermute | solution.py:34
  56.1 12.8 %collective-permute-start.6 = (bf16[4,192,128]{2,1,0:T(8,128)(2,1)S(1)}, bf16[4,192,128]{2,1,0:T(8,128)(2,1)S(1)}, u32[]{:S(2)}, u32[]{:S(2)}) collective-permute-start(bf16[4,192,128]{2,1,0:T(8,128)(2,1)S(1)} %pad_maximum_fusion.3), channel_id=1, source_target_pairs={{0,16},{8,24},{16,32},{24,40},{32,48},{40,56},{48,0},{56,8},{64,80... | collective-permute-start | bytes 589832 | tf_op jit(solution)/shard_map/ppermute | solution.py:34
  61.4 11.6 %collective-permute-start.13 = (bf16[2,400,128]{2,1,0:T(8,128)(2,1)S(1)}, bf16[2,400,128]{2,1,0:T(8,128)(2,1)S(1)}, u32[]{:S(2)}, u32[]{:S(2)}) collective-permute-start(bf16[2,400,128]{2,1,0:T(8,128)(2,1)S(1)} %pad_maximum_fusion.1.refs_9_), channel_id=1, source_target_pairs={{0,2},{1,3},{2,0},{3,1},{4,6},{5,7},{6,4},{7,5},{8,10},{9,11},{10,... | collective-permute-start | bytes 614408 | tf_op jit(solution)/shard_map/ppermute | solution.py:34
  65.5 7.7 %collective-permute-start.12 = (bf16[2,400,128]{2,1,0:T(8,128)(2,1)S(1)}, bf16[2,400,128]{2,1,0:T(8,128)(2,1)S(1)}, u32[]{:S(2)}, u32[]{:S(2)}) collective-permute-start(bf16[2,400,128]{2,1,0:T(8,128)(2,1)S(1)} %pad_maximum_fusion.1.refs_9_), channel_id=1, source_target_pairs={{0,3},{1,0},{2,1},{3,2},{4,7},{5,4},{6,5},{7,6},{8,11},{9,8},{10,9... | collective-permute-start | bytes 614408 | tf_op jit(solution)/shard_map/ppermute | solution.py:34
  65.5 7.0 %collective-permute-start.9 = (bf16[4,192,128]{2,1,0:T(8,128)(2,1)S(1)}, bf16[4,192,128]{2,1,0:T(8,128)(2,1)S(1)}, u32[]{:S(2)}, u32[]{:S(2)}) collective-permute-start(bf16[4,192,128]{2,1,0:T(8,128)(2,1)S(1)} %collective-permute-done.4), channel_id=1, source_target_pairs={{0,16},{8,24},{16,32},{24,40},{32,48},{40,56},{48,0},{56,8},{64,80... | collective-permute-start | bytes 589832 | tf_op jit(solution)/shard_map/ppermute | solution.py:34
  65.6 6.9 %collective-permute-start.10 = (bf16[4,192,128]{2,1,0:T(8,128)(2,1)S(1)}, bf16[4,192,128]{2,1,0:T(8,128)(2,1)S(1)}, u32[]{:S(2)}, u32[]{:S(2)}) collective-permute-start(bf16[4,192,128]{2,1,0:T(8,128)(2,1)S(1)} %collective-permute-done.8), channel_id=1, source_target_pairs={{0,48},{8,56},{16,0},{24,8},{32,16},{40,24},{48,32},{56,40},{64,11... | collective-permute-start | bytes 589832 | tf_op jit(solution)/shard_map/ppermute | solution.py:34
  68.9 7.0 %collective-permute-start.11 = (bf16[2,400,128]{2,1,0:T(8,128)(2,1)S(1)}, bf16[2,400,128]{2,1,0:T(8,128)(2,1)S(1)}, u32[]{:S(2)}, u32[]{:S(2)}) collective-permute-start(bf16[2,400,128]{2,1,0:T(8,128)(2,1)S(1)} %pad_maximum_fusion.1.refs_9_), channel_id=1, source_target_pairs={{0,1},{1,2},{2,3},{3,0},{4,5},{5,6},{6,7},{7,4},{8,9},{9,10},{10,1... | collective-permute-start | bytes 614408 | tf_op jit(solution)/shard_map/ppermute | solution.py:34
  72.5 3.5 %collective-permute-start.14 = (bf16[8,192,128]{2,1,0:T(8,128)(2,1)S(1)}, bf16[8,192,128]{2,1,0:T(8,128)(2,1)S(1)}, u32[]{:S(2)}, u32[]{:S(2)}) collective-permute-start(bf16[8,192,128]{2,1,0:T(8,128)(2,1)S(1)} %constant_dynamic-update-slice_fusion.refs_1_), channel_id=1, source_target_pairs={{0,8},{8,0},{16,24},{24,16},{32,40},{40,32},{48,56},{56,48},{64,72... | collective-permute-start | bytes 1179656 | tf_op jit(solution)/shard_map/ppermute | solution.py:34
  72.5 3.5 %collective-permute-start.15 = (bf16[8,192,128]{2,1,0:T(8,128)(2,1)S(1)}, bf16[8,192,128]{2,1,0:T(8,128)(2,1)S(1)}, u32[]{:S(2)}, u32[]{:S(2)}) collective-permute-start(bf16[8,192,128]{2,1,0:T(8,128)(2,1)S(1)} %constant_dynamic-update-slice_fusion.8.refs_2_), channel_id=1, source_target_pairs={{0,8},{8,0},{16,24},{24,16},{32,40},{40,32},{48,56},{56,48},{64,72... | collective-permute-start | bytes 1179656 | tf_op jit(solution)/shard_map/ppermute | solution.py:34
  73.0 2.9 %collective-permute-start.16 = (bf16[8,192,128]{2,1,0:T(8,128)(2,1)S(1)}, bf16[8,192,128]{2,1,0:T(8,128)(2,1)S(1)}, u32[]{:S(2)}, u32[]{:S(2)}) collective-permute-start(bf16[8,192,128]{2,1,0:T(8,128)(2,1)S(1)} %constant_dynamic-update-slice_fusion.10.refs_3_), channel_id=1, source_target_pairs={{0,8},{8,0},{16,24},{24,16},{32,40},{40,32},{48,56},{56,48},{64,72... | collective-permute-start | bytes 1179656 | tf_op jit(solution)/shard_map/ppermute | solution.py:34
  76.0 1.7 %collective-permute-start.17 = (bf16[8,192,128]{2,1,0:T(8,128)(2,1)S(1)}, bf16[8,192,128]{2,1,0:T(8,128)(2,1)S(1)}, u32[]{:S(2)}, u32[]{:S(2)}) collective-permute-start(bf16[8,192,128]{2,1,0:T(8,128)(2,1)S(1)} %pad_maximum_fusion.refs_4_), channel_id=1, source_target_pairs={{0,8},{8,0},{16,24},{24,16},{32,40},{40,32},{48,56},{56,48},{64,72... | collective-permute-start | bytes 1179656 | tf_op jit(solution)/shard_map/ppermute | solution.py:34
  84.0 12.6 %all-to-all-start.1 = ((f32[8,96,128]{2,1,0:T(8,128)}), f32[8,96,128]{2,1,0:T(8,128)S(1)}, u32[]{:S(2)}, u32[]{:S(2)}) async-start(f32[8,96,128]{2,1,0:T(8,128)} %get-tuple-element.58), calls=%async_computation.1 | async-start | bytes 786432 | tf_op jit(solution)/shard_map/all_to_all | solution.py:439
  87.6 21.1 %collective-permute-start.18 = (f32[4,288,128]{2,1,0:T(8,128)S(1)}, f32[4,288,128]{2,1,0:T(8,128)S(1)}, u32[]{:S(2)}, u32[]{:S(2)}) collective-permute-start(f32[4,288,128]{2,1,0:T(8,128)S(1)} %get-tuple-element.53), channel_id=1, source_target_pairs={{0,4},{1,5},{2,6},{3,7},{4,0},{5,1},{6,2},{7,3},{8,12},{9,13},{10,... | collective-permute-start | bytes 1769480 | tf_op jit(solution)/shard_map/ppermute | solution.py:34
  97.7 22.1 %all-to-all-start.2 = ((f32[32,8,128]{2,1,0:T(8,128)}), f32[32,8,128]{2,1,0:T(8,128)S(1)}, u32[]{:S(2)}, u32[]{:S(2)}) async-start(f32[32,8,128]{2,1,0:T(8,128)} %bitcast.19), calls=%async_computation.2 | async-start | bytes 262144 | tf_op jit(solution)/shard_map/all_to_all | solution.py:446
  108.8 7.1 %collective-permute-start.19 = (f32[288,128]{1,0:T(8,128)S(1)}, f32[288,128]{1,0:T(8,128)S(1)}, u32[]{:S(2)}, u32[]{:S(2)}) collective-permute-start(f32[288,128]{1,0:T(8,128)S(1)} %get-tuple-element.55), channel_id=1, source_target_pairs={{0,3},{1,0},{2,1},{3,2},{4,7},{5,4},{6,5},{7,6},{8,11},{9,8},{10,9... | collective-permute-start | bytes 442376 | tf_op jit(solution)/shard_map/ppermute | solution.py:34
  111.8 7.9 %collective-permute-start.20 = (f32[288,128]{1,0:T(8,128)S(1)}, f32[288,128]{1,0:T(8,128)S(1)}, u32[]{:S(2)}, u32[]{:S(2)}) collective-permute-start(f32[288,128]{1,0:T(8,128)S(1)} %get-tuple-element.56), channel_id=1, source_target_pairs={{0,1},{1,2},{2,3},{3,0},{4,5},{5,6},{6,7},{7,4},{8,9},{9,10},{10,1... | collective-permute-start | bytes 442376 | tf_op jit(solution)/shard_map/ppermute | solution.py:34
  111.8 7.9 %collective-permute-start.21 = (f32[288,128]{1,0:T(8,128)S(1)}, f32[288,128]{1,0:T(8,128)S(1)}, u32[]{:S(2)}, u32[]{:S(2)}) collective-permute-start(f32[288,128]{1,0:T(8,128)S(1)} %get-tuple-element.57), channel_id=1, source_target_pairs={{0,2},{1,3},{2,0},{3,1},{4,6},{5,7},{6,4},{7,5},{8,10},{9,11},{10,... | collective-permute-start | bytes 442376 | tf_op jit(solution)/shard_map/ppermute | solution.py:34
  (11 other events, 76.6 us)
